TPU v7x, 512 devices: a whole 4x4x16 slice. The times are simulated.
512 devices in a mesh: dom: 128 (over z, y, core), pipe: 4 (over x).
Axes of the slice: x: 4, y: 4, z: 16, core: 2. Of those that a mesh axis runs over, the one named last changes fastest.
Arguments:
- inputs: bfloat16 [2, 32768, 512], P(None, 'dom'), may hold values from -6 to 6
- cotangent: bfloat16 [2, 32768, 512], P(None, 'dom'), may hold values from -6 to 6
- w_send: bfloat16 [4, 512, 512], P('pipe'), may hold values from -0.25 to 0.25
- w_recv: bfloat16 [4, 512, 512], P('pipe'), may hold values from -0.25 to 0.25
- w_message: bfloat16 [4, 512, 512], P('pipe'), may hold values from -0.25 to 0.25
- w_node: bfloat16 [4, 512, 512], P('pipe'), may hold values from -0.25 to 0.25
- w_aggregate: bfloat16 [4, 512, 512], P('pipe'), may hold values from -0.25 to 0.25
- gains: float32 [4, 512], P('pipe'), may hold values from 0.1 to 1.9
- edge_send: int32 [256, 128], P('dom'), may hold values from 0 to 511, as said below
- edge_recv: int32 [256, 128], P('dom'), may hold values from 0 to 255, as said below
- edge_count: int32 [256], P('dom'), may hold values from 1 to 128, as said below
- halo_send: int32 [128, 2, 1], P('dom'), may hold values from 0 to 1, as said below
Outputs:
- section_out: bfloat16 [4, 2, 32768, 512], P('pipe', None, 'dom')
- input_grad: bfloat16 [4, 2, 32768, 512], P('pipe', None, 'dom')
Inputs may be any that keep to these rules, and one draw needn't show every extreme that they name: `edge_send`: rows 0 to 255 are the partition's own rows, the next 128 the blocks received from the previous partition in list order, the last 128 those from the next partition. The largest and smallest values are reached. `edge_recv`: both ends are reached. `edge_count`: the live slots of a block are its first ones; one block is full and one has a single live slot. `halo_send`: each list names 1 distinct own blocks. Lists wrap around the partitions.
All inputs are finite; a program needn't handle non-finite values.
Results may differ from a plain program's by a relative error of at most 0.015.
Values may be sent and summed in bfloat16 or wider, within the bound.
A program may use at most 64 MiB of HBM per device.

v0:
```python
import functools

import jax
import jax.numpy as jnp
from jax import lax
from jax.experimental import pallas as pl
from jax.experimental.pallas import tpu as pltpu
from jax.sharding import PartitionSpec as P

EPSILON = 1e-05
F32 = jnp.float32
BF16 = jnp.bfloat16


def mm(x, w):
    return jnp.dot(x, w, preferred_element_type=F32)


def mm_t(x, w):
    return lax.dot_general(x, w, (((1,), (1,)), ((), ())), preferred_element_type=F32)


def sigmoid(v):
    return 1.0 / (1.0 + jnp.exp(-v))


def split_sum(onehot, values):
    hi = values.astype(BF16)
    lo = (values - hi.astype(F32)).astype(BF16)
    return mm(onehot, hi) + mm(onehot, lo)


def fwd_kernel(hs_ref, h_ref, fp_ref, fn_ref, osnd_ref, orcv_ref, orcvt_ref,
               ws_ref, wr_ref, wm_ref, wn_ref, wa_ref, g_ref,
               out_ref, a_ref, u_ref, hn_ref, hp_ref):
    own = h_ref.shape[1]
    span = fp_ref.shape[1]
    block = span
    gain = g_ref[...]
    osnd = osnd_ref[...]
    for m in range(h_ref.shape[0]):
        h = h_ref[m]
        gathered = (mm(osnd[:, :own], h) + mm(osnd[:, own:own + span], fp_ref[m])
                    + mm(osnd[:, own + span:], fn_ref[m])).astype(BF16)
        send_part = mm(gathered, ws_ref[...]).astype(BF16).astype(F32)
        recv_rows = mm(orcv_ref[...], h).astype(BF16)
        pre = send_part + mm(recv_rows, wr_ref[...])
        a_ref[m] = pre
        edge_hidden = (pre * sigmoid(pre)).astype(BF16)
        messages = mm(edge_hidden, wm_ref[...])
        agg = split_sum(orcvt_ref[...], messages).astype(BF16)
        node_pre = mm(h, wn_ref[...]) + mm(agg, wa_ref[...])
        u_ref[m] = node_pre
        act = node_pre * sigmoid(node_pre)
        mean = jnp.mean(act, axis=-1, keepdims=True)
        cen = act - mean
        var = jnp.mean(cen * cen, axis=-1, keepdims=True)
        unit = cen * lax.rsqrt(var + EPSILON)
        out = (h.astype(F32) + unit * gain).astype(BF16)
        out_ref[m] = out
        hs0 = hs_ref[0]
        hs1 = hs_ref[1]
        nblocks = own // block
        sel_n = out[0:block]
        sel_p = out[0:block]
        for b in range(1, nblocks):
            piece = out[b * block:(b + 1) * block]
            sel_n = jnp.where(hs0 == b, piece, sel_n)
            sel_p = jnp.where(hs1 == b, piece, sel_p)
        hn_ref[m] = sel_n
        hp_ref[m] = sel_p


def bwd_kernel(hs_ref, pin_ref, gn_ref, gp_ref, a_ref, u_ref, osndt_ref, orcvl_ref, orcvt_ref,
               ws_ref, wr_ref, wm_ref, wn_ref, wa_ref, g_ref,
               p32_ref, p16_ref, hg_ref):
    own = pin_ref.shape[1]
    span = gn_ref.shape[1]
    block = span
    nblocks = own // block
    gain = g_ref[...]
    hs0 = hs_ref[0]
    hs1 = hs_ref[1]
    osndt = osndt_ref[...]
    for m in range(pin_ref.shape[0]):
        pieces = []
        gn = gn_ref[m].astype(F32)
        gp = gp_ref[m].astype(F32)
        for b in range(nblocks):
            piece = pin_ref[m, b * block:(b + 1) * block].astype(F32)
            piece = piece + jnp.where(hs0 == b, gn, 0.0) + jnp.where(hs1 == b, gp, 0.0)
            pieces.append(piece)
        c = jnp.concatenate(pieces, axis=0).astype(BF16).astype(F32)
        node_pre = u_ref[m]
        sig_u = sigmoid(node_pre)
        act = node_pre * sig_u
        mean = jnp.mean(act, axis=-1, keepdims=True)
        cen = act - mean
        var = jnp.mean(cen * cen, axis=-1, keepdims=True)
        rs = lax.rsqrt(var + EPSILON)
        unit = cen * rs
        gu = c * gain
        gact = rs * (gu - jnp.mean(gu, axis=-1, keepdims=True)
                     - unit * jnp.mean(gu * unit, axis=-1, keepdims=True))
        du = (gact * (sig_u * (1.0 + node_pre * (1.0 - sig_u)))).astype(BF16)
        dagg = mm_t(du, wa_ref[...]).astype(BF16)
        rows = c + mm_t(du, wn_ref[...])
        gmsg = mm(orcvl_ref[...], dagg).astype(BF16)
        pre = a_ref[m]
        sig_a = sigmoid(pre)
        dedge = (mm_t(gmsg, wm_ref[...]) * (sig_a * (1.0 + pre * (1.0 - sig_a)))).astype(BF16)
        rows = rows + split_sum(orcvt_ref[...], mm_t(dedge, wr_ref[...]))
        send_rows = split_sum(osndt, mm_t(dedge, ws_ref[...]))
        total = rows + send_rows[:own]
        p32_ref[m] = total
        p16_ref[m] = total.astype(BF16)
        hg_ref[m] = send_rows[own:].astype(BF16)


def vmem_call(kernel, out_shapes, n_in, smem_first=True):
    in_specs = [pl.BlockSpec(memory_space=pltpu.SMEM)] + [pl.BlockSpec(memory_space=pltpu.VMEM)] * (n_in - 1)
    return pl.pallas_call(
        kernel,
        out_shape=out_shapes,
        in_specs=in_specs,
        out_specs=tuple(pl.BlockSpec(memory_space=pltpu.VMEM) for _ in out_shapes),
        compiler_params=pltpu.CompilerParams(vmem_limit_bytes=48 * 1024 * 1024),
    )


def shards(inputs, cotangent, w_send, w_recv, w_message, w_node, w_aggregate, gains,
           edge_send, edge_recv, edge_count, halo_send):
    sections = lax.axis_size("pipe")
    parts = lax.axis_size("dom")
    p_idx = lax.axis_index("pipe")
    micro, own, latent = inputs.shape
    block = edge_send.shape[1]
    span = halo_send.shape[2] * block
    ext_rows = own + 2 * span
    weights = (w_send[0], w_recv[0], w_message[0], w_node[0], w_aggregate[0])
    gain = gains[0].reshape(1, latent)
    hs = halo_send[0].reshape(-1).astype(jnp.int32)

    snd = edge_send.reshape(-1)
    rcv = edge_recv.reshape(-1)
    live = (jnp.arange(block)[None, :] < edge_count[:, None]).reshape(-1)
    osnd = (snd[:, None] == jnp.arange(ext_rows)[None, :]).astype(BF16)
    orcv_b = rcv[:, None] == jnp.arange(own)[None, :]
    orcv = orcv_b.astype(BF16)
    orcvl_b = orcv_b & live[:, None]
    orcvl = orcvl_b.astype(BF16)
    orcvt = orcvl_b.T.astype(BF16)
    osndt = osnd.T

    def blocks_of(x):
        shaped = x.reshape(micro, own // block, block, latent)
        nxt = jnp.take(shaped, hs[0], axis=1)
        prv = jnp.take(shaped, hs[1], axis=1)
        return nxt, prv

    S, D = sections, parts

    def perm_pipe(shift):
        return [(i, (i + shift) % S) for i in range(S)]

    def perm_both(dshift, pshift):
        return [(d * S + p, ((d + dshift) % D) * S + (p + pshift) % S)
                for d in range(D) for p in range(S)]

    both = ("dom", "pipe")

    fwd = vmem_call(
        fwd_kernel,
        (jax.ShapeDtypeStruct((micro, own, latent), BF16),
         jax.ShapeDtypeStruct((micro, own, latent), F32),
         jax.ShapeDtypeStruct((micro, own, latent), F32),
         jax.ShapeDtypeStruct((micro, span, latent), BF16),
         jax.ShapeDtypeStruct((micro, span, latent), BF16)),
        13)
    bwd = vmem_call(
        bwd_kernel,
        (jax.ShapeDtypeStruct((micro, own, latent), F32),
         jax.ShapeDtypeStruct((micro, own, latent), BF16),
         jax.ShapeDtypeStruct((micro, 2 * span, latent), BF16)),
        15)

    nxt0, prv0 = blocks_of(inputs)
    from_prev = lax.ppermute(nxt0, "dom", [(i, (i + 1) % D) for i in range(D)])
    from_next = lax.ppermute(prv0, "dom", [(i, (i - 1) % D) for i in range(D)])
    h = inputs
    out_rec = a_rec = u_rec = None
    for t in range(S):
        out, a, u, hn, hp = fwd(hs, h, from_prev, from_next, osnd, orcv, orcvt, *weights, gain)
        here = p_idx == t
        if t == 0:
            out_rec, a_rec, u_rec = out, a, u
        else:
            out_rec = jnp.where(here, out, out_rec)
            a_rec = jnp.where(here, a, a_rec)
            u_rec = jnp.where(here, u, u_rec)
        if t < S - 1:
            h = lax.ppermute(out, "pipe", perm_pipe(1))
            from_prev = lax.ppermute(hn, both, perm_both(1, 1))
            from_next = lax.ppermute(hp, both, perm_both(-1, 1))

    pin = cotangent
    zeros = jnp.zeros((micro, span, latent), BF16)
    g_next = g_prev = zeros
    grad_rec = None
    for t in range(S - 1, -1, -1):
        p32, p16, hg = bwd(hs, pin, g_next, g_prev, a_rec, u_rec, osndt, orcvl, orcvt, *weights, gain)
        to_prev = hg[:, :span]
        to_next = hg[:, span:]
        sn = lax.ppermute(to_prev, "dom", [(i, (i - 1) % D) for i in range(D)])
        sp = lax.ppermute(to_next, "dom", [(i, (i + 1) % D) for i in range(D)])
        shaped = p32.reshape(micro, own // block, block, latent)
        sel = jnp.arange(own // block)[None, :, None, None]
        summed = (shaped + jnp.where(sel == hs[0], sn.astype(F32)[:, None], 0.0)
                  + jnp.where(sel == hs[1], sp.astype(F32)[:, None], 0.0))
        grad = summed.reshape(micro, own, latent).astype(BF16)
        here = p_idx == t
        grad_rec = grad if t == S - 1 else jnp.where(here, grad, grad_rec)
        if t > 0:
            pin = lax.ppermute(p16, "pipe", perm_pipe(-1))
            g_next = lax.ppermute(to_prev, both, perm_both(-1, -1))
            g_prev = lax.ppermute(to_next, both, perm_both(1, -1))
    return (out_rec[None], grad_rec[None])


def solution(mesh):
    in_specs = (
        P(None, "dom", None),
        P(None, "dom", None),
        P("pipe", None, None),
        P("pipe", None, None),
        P("pipe", None, None),
        P("pipe", None, None),
        P("pipe", None, None),
        P("pipe", None),
        P("dom", None),
        P("dom", None),
        P("dom"),
        P("dom", None, None),
    )
    out_specs = (P("pipe", None, "dom", None), P("pipe", None, "dom", None))
    return jax.shard_map(shards, mesh=mesh, in_specs=in_specs, out_specs=out_specs, check_vma=False)
```

profile of v0, /device:TPU:6, one launch (start us, length us, event | category | flops | bytes accessed | tf_op | source)
XLA Modules:
  0.0 272.4 jit_solution(14150100609245584111)
XLA Ops:
  9.1 13.3 %collective-permute-start.1 = (bf16[2,128,512]{2,1,0:T(8,128)(2,1)S(1)}, bf16[2,128,512]{2,1,0:T(8,128)(2,1)S(1)}, u32[]{:S(2)}, u32[]{:S(2)}) collective-permute-start(bf16[2,128,512]{2,1,0:T(8,128)(2,1)S(1)} %get-tuple-element.80), channel_id=1, source_target_pairs={{0,508},{4,0},{8,4},{12,8},{16,12},{20,16},{24,20},{28,24},{32,28}... | collective-permute-start | bytes 786440 | tf_op jit(solution)/shard_map/ppermute | solution.py:189
  30.0 4.9 %shard_map.131 = (bf16[2,256,512]{2,1,0:T(8,128)(2,1)S(1)}, f32[2,256,512]{2,1,0:T(8,128)}, f32[2,256,512]{2,1,0:T(8,128)}, bf16[2,128,512]{2,1,0:T(8,128)(2,1)S(1)}, bf16[2,128,512]{2,1,0:T(8,128)(2,1)S(1)}) custom-call(s32[2]{0:T(128)S(1)} %bitcast.145, bf16[2,256,512]{2,1,0:T(8,128)(2,1)S(1)} %copy-done.7, ...), custom_call_target="tpu_custom_call" | custom-call | tf_op jit(solution)/shard_map/pallas_call | solution.py:193
  39.3 8.8 %collective-permute-start.4 = (bf16[2,128,512]{2,1,0:T(8,128)(2,1)S(1)}, bf16[2,128,512]{2,1,0:T(8,128)(2,1)S(1)}, u32[]{:S(2)}, u32[]{:S(2)}) collective-permute-start(bf16[2,128,512]{2,1,0:T(8,128)(2,1)S(1)} %get-tuple-element.34), channel_id=1, source_target_pairs={{0,509},{1,510},{2,511},{3,508},{4,1},{5,2},{6,3},{7,0},{8,5},{9,6... | collective-permute-start | bytes 786440 | tf_op jit(solution)/shard_map/ppermute | solution.py:204
  52.5 4.9 %shard_map.132 = (bf16[2,256,512]{2,1,0:T(8,128)(2,1)S(1)}, f32[2,256,512]{2,1,0:T(8,128)}, f32[2,256,512]{2,1,0:T(8,128)}, bf16[2,128,512]{2,1,0:T(8,128)(2,1)S(1)}, bf16[2,128,512]{2,1,0:T(8,128)(2,1)S(1)}) custom-call(s32[2]{0:T(128)S(1)} %bitcast.146, bf16[2,256,512]{2,1,0:T(8,128)(2,1)S(1)} %collective-permute-done.2.h_ref, ...), custom_call_target="tpu_custom_call" | custom-call | tf_op jit(solution)/shard_map/pallas_call | solution.py:193
  64.4 11.0 %collective-permute-start.7 = (bf16[2,128,512]{2,1,0:T(8,128)(2,1)S(1)}, bf16[2,128,512]{2,1,0:T(8,128)(2,1)S(1)}, u32[]{:S(2)}, u32[]{:S(2)}) collective-permute-start(bf16[2,128,512]{2,1,0:T(8,128)(2,1)S(1)} %get-tuple-element.37), channel_id=1, source_target_pairs={{0,509},{1,510},{2,511},{3,508},{4,1},{5,2},{6,3},{7,0},{8,5},{9,6... | collective-permute-start | bytes 786440 | tf_op jit(solution)/shard_map/ppermute | solution.py:204
  75.3 5.3 %collective-permute-done.6.fp_ref = bf16[2,128,512]{2,1,0:T(8,128)(2,1)S(1)} collective-permute-done((bf16[2,128,512]{2,1,0:T(8,128)(2,1)S(1)}, bf16[2,128,512]{2,1,0:T(8,128)(2,1)S(1)}, u32[]{:S(2)}, u32[]{:S(2)}) %collective-permute-start.6) | collective-permute-done | bytes 262176 | tf_op jit(solution)/shard_map/ppermute | solution.py:203
  80.7 4.7 %collective-permute-done.7.fn_ref = bf16[2,128,512]{2,1,0:T(8,128)(2,1)S(1)} collective-permute-done((bf16[2,128,512]{2,1,0:T(8,128)(2,1)S(1)}, bf16[2,128,512]{2,1,0:T(8,128)(2,1)S(1)}, u32[]{:S(2)}, u32[]{:S(2)}) %collective-permute-start.7) | collective-permute-done | bytes 262176 | tf_op jit(solution)/shard_map/ppermute | solution.py:204
  85.3 5.3 %shard_map.133 = (bf16[2,256,512]{2,1,0:T(8,128)(2,1)}, f32[2,256,512]{2,1,0:T(8,128)}, f32[2,256,512]{2,1,0:T(8,128)}, bf16[2,128,512]{2,1,0:T(8,128)(2,1)}, bf16[2,128,512]{2,1,0:T(8,128)(2,1)}) custom-call(s32[2]{0:T(128)S(1)} %bitcast.147, bf16[2,256,512]{2,1,0:T(8,128)(2,1)S(1)} %collective-permute-done.5.h_ref, ...), custom_call_target="tpu_custom_call" | custom-call | tf_op jit(solution)/shard_map/pallas_call | solution.py:193
  90.6 4.7 %collective-permute-start.8 = (bf16[2,256,512]{2,1,0:T(8,128)(2,1)}, bf16[2,256,512]{2,1,0:T(8,128)(2,1)}, u32[]{:S(2)}, u32[]{:S(2)}) collective-permute-start(bf16[2,256,512]{2,1,0:T(8,128)(2,1)} %get-tuple-element.38), channel_id=1, source_target_pairs={{0,1},{1,2},{2,3},{3,0},{4,5},{5,6},{6,7},{7,4},{8,9},{9,10},{10,1... | collective-permute-start | bytes 1572872 | tf_op jit(solution)/shard_map/ppermute | solution.py:202
  97.9 7.2 %collective-permute-start.10 = (bf16[2,128,512]{2,1,0:T(8,128)(2,1)}, bf16[2,128,512]{2,1,0:T(8,128)(2,1)}, u32[]{:S(2)}, u32[]{:S(2)}) collective-permute-start(bf16[2,128,512]{2,1,0:T(8,128)(2,1)} %get-tuple-element.40), channel_id=1, source_target_pairs={{0,509},{1,510},{2,511},{3,508},{4,1},{5,2},{6,3},{7,0},{8,5},{9,6... | collective-permute-start | bytes 786440 | tf_op jit(solution)/shard_map/ppermute | solution.py:204
  105.3 11.1 %collective-permute-done.9.fp_ref = bf16[2,128,512]{2,1,0:T(8,128)(2,1)} collective-permute-done((bf16[2,128,512]{2,1,0:T(8,128)(2,1)}, bf16[2,128,512]{2,1,0:T(8,128)(2,1)}, u32[]{:S(2)}, u32[]{:S(2)}) %collective-permute-start.9) | collective-permute-done | bytes 262176 | tf_op jit(solution)/shard_map/ppermute | solution.py:203
  118.9 5.8 %shard_map.134 = (bf16[2,256,512]{2,1,0:T(8,128)(2,1)S(1)}, f32[2,256,512]{2,1,0:T(8,128)}, f32[2,256,512]{2,1,0:T(8,128)}, bf16[2,128,512]{2,1,0:T(8,128)(2,1)}, bf16[2,128,512]{2,1,0:T(8,128)(2,1)}) custom-call(s32[2]{0:T(128)S(1)} %bitcast.148, bf16[2,256,512]{2,1,0:T(8,128)(2,1)} %collective-permute-done.8.h_ref, ...), custom_call_target="tpu_custom_call" | custom-call | tf_op jit(solution)/shard_map/pallas_call | solution.py:193
  128.8 5.8 %shard_map.135 = (f32[2,256,512]{2,1,0:T(8,128)S(1)}, bf16[2,256,512]{2,1,0:T(8,128)(2,1)S(1)}, bf16[2,256,512]{2,1,0:T(8,128)(2,1)S(1)}) custom-call(s32[2]{0:T(128)S(1)} %bitcast.149, bf16[2,256,512]{2,1,0:T(8,128)(2,1)S(1)} %copy-done.10, bf16[2,128,512]{2,1,0:T(8,128)(2,1)S(1)} %broadcast_in_dim.144.gn_ref.gp_ref, ...), custom_call_target="tpu_custom_call" | custom-call | tf_op jit(solution)/shard_map/pallas_call | solution.py:211
  145.8 15.3 %collective-permute-done.12.gn_ref = bf16[2,128,512]{2,1,0:T(8,128)(2,1)S(1)} collective-permute-done((bf16[2,128,512]{2,1,0:T(8,128)(2,1)}, bf16[2,128,512]{2,1,0:T(8,128)(2,1)S(1)}, u32[]{:S(2)}, u32[]{:S(2)}) %collective-permute-start.12) | collective-permute-done | bytes 262176 | tf_op jit(solution)/shard_map/ppermute | solution.py:225
  161.0 6.7 %shard_map.136 = (f32[2,256,512]{2,1,0:T(8,128)}, bf16[2,256,512]{2,1,0:T(8,128)(2,1)S(1)}, bf16[2,256,512]{2,1,0:T(8,128)(2,1)S(1)}) custom-call(s32[2]{0:T(128)S(1)} %bitcast.150, bf16[2,256,512]{2,1,0:T(8,128)(2,1)S(1)} %collective-permute-done.11.pin_ref, bf16[2,128,512]{2,1,0:T(8,128)(2,1)S(1)} %collective-permute-done.12.gn_ref, ...), custom_call_target="tpu_custom_call" | custom-call | tf_op jit(solution)/shard_map/pallas_call | solution.py:211
  170.4 6.8 %collective-permute-start.15 = (bf16[2,128,512]{2,1,0:T(8,128)(2,1)S(1)}, bf16[2,128,512]{2,1,0:T(8,128)(2,1)S(1)}, u32[]{:S(2)}, u32[]{:S(2)}) collective-permute-start(bf16[2,128,512]{2,1,0:T(8,128)(2,1)S(1)} %get-tuple-element.77), channel_id=1, source_target_pairs={{0,511},{1,508},{2,509},{3,510},{4,3},{5,0},{6,1},{7,2},{8,7},{9,4... | collective-permute-start | bytes 786440 | tf_op jit(solution)/shard_map/ppermute | solution.py:225
  179.3 14.2 %collective-permute-done.15.gn_ref = bf16[2,128,512]{2,1,0:T(8,128)(2,1)S(1)} collective-permute-done((bf16[2,128,512]{2,1,0:T(8,128)(2,1)S(1)}, bf16[2,128,512]{2,1,0:T(8,128)(2,1)S(1)}, u32[]{:S(2)}, u32[]{:S(2)}) %collective-permute-start.15) | collective-permute-done | bytes 262176 | tf_op jit(solution)/shard_map/ppermute | solution.py:225
  193.5 6.9 %shard_map.137 = (f32[2,256,512]{2,1,0:T(8,128)}, bf16[2,256,512]{2,1,0:T(8,128)(2,1)}, bf16[2,256,512]{2,1,0:T(8,128)(2,1)S(1)}) custom-call(s32[2]{0:T(128)S(1)} %bitcast.151, bf16[2,256,512]{2,1,0:T(8,128)(2,1)S(1)} %collective-permute-done.14.pin_ref, bf16[2,128,512]{2,1,0:T(8,128)(2,1)S(1)} %collective-permute-done.15.gn_ref, ...), custom_call_target="tpu_custom_call" | custom-call | tf_op jit(solution)/shard_map/pallas_call | solution.py:211
  203.1 8.1 %collective-permute-start.18 = (bf16[2,128,512]{2,1,0:T(8,128)(2,1)S(1)}, bf16[2,128,512]{2,1,0:T(8,128)(2,1)S(1)}, u32[]{:S(2)}, u32[]{:S(2)}) collective-permute-start(bf16[2,128,512]{2,1,0:T(8,128)(2,1)S(1)} %get-tuple-element.75), channel_id=1, source_target_pairs={{0,511},{1,508},{2,509},{3,510},{4,3},{5,0},{6,1},{7,2},{8,7},{9,4... | collective-permute-start | bytes 786440 | tf_op jit(solution)/shard_map/ppermute | solution.py:225
  216.3 8.5 %collective-permute-start.26 = (bf16[2,128,512]{2,1,0:T(8,128)(2,1)}, bf16[2,128,512]{2,1,0:T(8,128)(2,1)}, u32[]{:S(2)}, u32[]{:S(2)}) collective-permute-start(bf16[2,128,512]{2,1,0:T(8,128)(2,1)} %get-tuple-element.79), channel_id=1, source_target_pairs={{0,508},{4,0},{8,4},{12,8},{16,12},{20,16},{24,20},{28,24},{32,28}... | collective-permute-start | bytes 786440 | tf_op jit(solution)/shard_map/ppermute | solution.py:214
  229.1 9.5 %collective-permute-start.24 = (bf16[2,128,512]{2,1,0:T(8,128)(2,1)}, bf16[2,128,512]{2,1,0:T(8,128)(2,1)S(1)}, u32[]{:S(2)}, u32[]{:S(2)}) collective-permute-start(bf16[2,128,512]{2,1,0:T(8,128)(2,1)} %copy-done.26), channel_id=1, source_target_pairs={{0,508},{4,0},{8,4},{12,8},{16,12},{20,16},{24,20},{28,24},{32,28}... | collective-permute-start | bytes 786440 | tf_op jit(solution)/shard_map/ppermute | solution.py:214
  240.6 7.2 %shard_map.138 = (f32[2,256,512]{2,1,0:T(8,128)}, bf16[2,256,512]{2,1,0:T(8,128)(2,1)}, bf16[2,256,512]{2,1,0:T(8,128)(2,1)S(1)}) custom-call(s32[2]{0:T(128)S(1)} %bitcast.152, bf16[2,256,512]{2,1,0:T(8,128)(2,1)} %collective-permute-done.17.pin_ref, bf16[2,128,512]{2,1,0:T(8,128)(2,1)S(1)} %collective-permute-done.18.gn_ref, ...), custom_call_target="tpu_custom_call" | custom-call | tf_op jit(solution)/shard_map/pallas_call | solution.py:211
  247.8 7.1 %collective-permute-start.22 = (bf16[2,128,512]{2,1,0:T(8,128)(2,1)S(1)}, bf16[2,128,512]{2,1,0:T(8,128)(2,1)S(1)}, u32[]{:S(2)}, u32[]{:S(2)}) collective-permute-start(bf16[2,128,512]{2,1,0:T(8,128)(2,1)S(1)} %copy-done.28), channel_id=1, source_target_pairs={{0,508},{4,0},{8,4},{12,8},{16,12},{20,16},{24,20},{28,24},{32,28}... | collective-permute-start | bytes 786440 | tf_op jit(solution)/shard_map/ppermute | solution.py:214
  256.9 7.0 %collective-permute-start.20 = (bf16[2,128,512]{2,1,0:T(8,128)(2,1)S(1)}, bf16[2,128,512]{2,1,0:T(8,128)(2,1)S(1)}, u32[]{:S(2)}, u32[]{:S(2)}) collective-permute-start(bf16[2,128,512]{2,1,0:T(8,128)(2,1)S(1)} %get-tuple-element.72), channel_id=1, source_target_pairs={{0,508},{4,0},{8,4},{12,8},{16,12},{20,16},{24,20},{28,24},{32,28}... | collective-permute-start | bytes 786440 | tf_op jit(solution)/shard_map/ppermute | solution.py:214
  (129 shorter events, 77.3 us)
Async XLA Ops:
  7.0 17.5 %collective-permute-start = (bf16[2,128,512]{2,1,0:T(8,128)(2,1)S(1)}, bf16[2,128,512]{2,1,0:T(8,128)(2,1)S(1)}, u32[]{:S(2)}, u32[]{:S(2)}) collective-permute-start(bf16[2,128,512]{2,1,0:T(8,128)(2,1)S(1)} %get-tuple-element.81), channel_id=1, source_target_pairs={{0,4},{4,8},{8,12},{12,16},{16,20},{20,24},{24,28},{28,32},{32,36}... | collective-permute-start | bytes 786440 | tf_op jit(solution)/shard_map/ppermute | solution.py:188
  9.1 17.2 %collective-permute-start.1 = (bf16[2,128,512]{2,1,0:T(8,128)(2,1)S(1)}, bf16[2,128,512]{2,1,0:T(8,128)(2,1)S(1)}, u32[]{:S(2)}, u32[]{:S(2)}) collective-permute-start(bf16[2,128,512]{2,1,0:T(8,128)(2,1)S(1)} %get-tuple-element.80), channel_id=1, source_target_pairs={{0,508},{4,0},{8,4},{12,8},{16,12},{20,16},{24,20},{28,24},{32,28}... | collective-permute-start | bytes 786440 | tf_op jit(solution)/shard_map/ppermute | solution.py:189
  35.0 17.5 %collective-permute-start.2 = (bf16[2,256,512]{2,1,0:T(8,128)(2,1)S(1)}, bf16[2,256,512]{2,1,0:T(8,128)(2,1)S(1)}, u32[]{:S(2)}, u32[]{:S(2)}) collective-permute-start(bf16[2,256,512]{2,1,0:T(8,128)(2,1)S(1)} %get-tuple-element.32), channel_id=1, source_target_pairs={{0,1},{1,2},{2,3},{3,0},{4,5},{5,6},{6,7},{7,4},{8,9},{9,10},{10,1... | collective-permute-start | bytes 1572872 | tf_op jit(solution)/shard_map/ppermute | solution.py:202
  57.4 27.9 %collective-permute-start.5 = (bf16[2,256,512]{2,1,0:T(8,128)(2,1)S(1)}, bf16[2,256,512]{2,1,0:T(8,128)(2,1)S(1)}, u32[]{:S(2)}, u32[]{:S(2)}) collective-permute-start(bf16[2,256,512]{2,1,0:T(8,128)(2,1)S(1)} %get-tuple-element.35), channel_id=1, source_target_pairs={{0,1},{1,2},{2,3},{3,0},{4,5},{5,6},{6,7},{7,4},{8,9},{9,10},{10,1... | collective-permute-start | bytes 1572872 | tf_op jit(solution)/shard_map/ppermute | solution.py:202
  60.9 19.8 %collective-permute-start.6 = (bf16[2,128,512]{2,1,0:T(8,128)(2,1)S(1)}, bf16[2,128,512]{2,1,0:T(8,128)(2,1)S(1)}, u32[]{:S(2)}, u32[]{:S(2)}) collective-permute-start(bf16[2,128,512]{2,1,0:T(8,128)(2,1)S(1)} %get-tuple-element.36), channel_id=1, source_target_pairs={{0,5},{1,6},{2,7},{3,4},{4,9},{5,10},{6,11},{7,8},{8,13},{9,14},{1... | collective-permute-start | bytes 786440 | tf_op jit(solution)/shard_map/ppermute | solution.py:203
  64.4 21.0 %collective-permute-start.7 = (bf16[2,128,512]{2,1,0:T(8,128)(2,1)S(1)}, bf16[2,128,512]{2,1,0:T(8,128)(2,1)S(1)}, u32[]{:S(2)}, u32[]{:S(2)}) collective-permute-start(bf16[2,128,512]{2,1,0:T(8,128)(2,1)S(1)} %get-tuple-element.37), channel_id=1, source_target_pairs={{0,509},{1,510},{2,511},{3,508},{4,1},{5,2},{6,3},{7,0},{8,5},{9,6... | collective-permute-start | bytes 786440 | tf_op jit(solution)/shard_map/ppermute | solution.py:204
  90.6 28.2 %collective-permute-start.8 = (bf16[2,256,512]{2,1,0:T(8,128)(2,1)}, bf16[2,256,512]{2,1,0:T(8,128)(2,1)}, u32[]{:S(2)}, u32[]{:S(2)}) collective-permute-start(bf16[2,256,512]{2,1,0:T(8,128)(2,1)} %get-tuple-element.38), channel_id=1, source_target_pairs={{0,1},{1,2},{2,3},{3,0},{4,5},{5,6},{6,7},{7,4},{8,9},{9,10},{10,1... | collective-permute-start | bytes 1572872 | tf_op jit(solution)/shard_map/ppermute | solution.py:202
  95.3 21.0 %collective-permute-start.9 = (bf16[2,128,512]{2,1,0:T(8,128)(2,1)}, bf16[2,128,512]{2,1,0:T(8,128)(2,1)}, u32[]{:S(2)}, u32[]{:S(2)}) collective-permute-start(bf16[2,128,512]{2,1,0:T(8,128)(2,1)} %get-tuple-element.39), channel_id=1, source_target_pairs={{0,5},{1,6},{2,7},{3,4},{4,9},{5,10},{6,11},{7,8},{8,13},{9,14},{1... | collective-permute-start | bytes 786440 | tf_op jit(solution)/shard_map/ppermute | solution.py:203
  97.9 20.9 %collective-permute-start.10 = (bf16[2,128,512]{2,1,0:T(8,128)(2,1)}, bf16[2,128,512]{2,1,0:T(8,128)(2,1)}, u32[]{:S(2)}, u32[]{:S(2)}) collective-permute-start(bf16[2,128,512]{2,1,0:T(8,128)(2,1)} %get-tuple-element.40), channel_id=1, source_target_pairs={{0,509},{1,510},{2,511},{3,508},{4,1},{5,2},{6,3},{7,0},{8,5},{9,6... | collective-permute-start | bytes 786440 | tf_op jit(solution)/shard_map/ppermute | solution.py:204
  135.6 25.4 %collective-permute-start.11 = (bf16[2,256,512]{2,1,0:T(8,128)(2,1)S(1)}, bf16[2,256,512]{2,1,0:T(8,128)(2,1)S(1)}, u32[]{:S(2)}, u32[]{:S(2)}) collective-permute-start(bf16[2,256,512]{2,1,0:T(8,128)(2,1)S(1)} %get-tuple-element.50), channel_id=1, source_target_pairs={{0,3},{1,0},{2,1},{3,2},{4,7},{5,4},{6,5},{7,6},{8,11},{9,8},{10,9... | collective-permute-start | bytes 1572872 | tf_op jit(solution)/shard_map/ppermute | solution.py:224
  139.3 21.7 %collective-permute-start.12 = (bf16[2,128,512]{2,1,0:T(8,128)(2,1)}, bf16[2,128,512]{2,1,0:T(8,128)(2,1)S(1)}, u32[]{:S(2)}, u32[]{:S(2)}) collective-permute-start(bf16[2,128,512]{2,1,0:T(8,128)(2,1)} %get-tuple-element.79), channel_id=1, source_target_pairs={{0,511},{1,508},{2,509},{3,510},{4,3},{5,0},{6,1},{7,2},{8,7},{9,4... | collective-permute-start | bytes 786440 | tf_op jit(solution)/shard_map/ppermute | solution.py:225
  143.5 17.5 %collective-permute-start.13 = (bf16[2,128,512]{2,1,0:T(8,128)(2,1)}, bf16[2,128,512]{2,1,0:T(8,128)(2,1)S(1)}, u32[]{:S(2)}, u32[]{:S(2)}) collective-permute-start(bf16[2,128,512]{2,1,0:T(8,128)(2,1)} %get-tuple-element.78), channel_id=1, source_target_pairs={{0,7},{1,4},{2,5},{3,6},{4,11},{5,8},{6,9},{7,10},{8,15},{9,12},{1... | collective-permute-start | bytes 786440 | tf_op jit(solution)/shard_map/ppermute | solution.py:226
  167.7 25.8 %collective-permute-start.14 = (bf16[2,256,512]{2,1,0:T(8,128)(2,1)S(1)}, bf16[2,256,512]{2,1,0:T(8,128)(2,1)S(1)}, u32[]{:S(2)}, u32[]{:S(2)}) collective-permute-start(bf16[2,256,512]{2,1,0:T(8,128)(2,1)S(1)} %get-tuple-element.52), channel_id=1, source_target_pairs={{0,3},{1,0},{2,1},{3,2},{4,7},{5,4},{6,5},{7,6},{8,11},{9,8},{10,9... | collective-permute-start | bytes 1572872 | tf_op jit(solution)/shard_map/ppermute | solution.py:224
  170.4 23.1 %collective-permute-start.15 = (bf16[2,128,512]{2,1,0:T(8,128)(2,1)S(1)}, bf16[2,128,512]{2,1,0:T(8,128)(2,1)S(1)}, u32[]{:S(2)}, u32[]{:S(2)}) collective-permute-start(bf16[2,128,512]{2,1,0:T(8,128)(2,1)S(1)} %get-tuple-element.77), channel_id=1, source_target_pairs={{0,511},{1,508},{2,509},{3,510},{4,3},{5,0},{6,1},{7,2},{8,7},{9,4... | collective-permute-start | bytes 786440 | tf_op jit(solution)/shard_map/ppermute | solution.py:225
  177.2 16.3 %collective-permute-start.16 = (bf16[2,128,512]{2,1,0:T(8,128)(2,1)}, bf16[2,128,512]{2,1,0:T(8,128)(2,1)S(1)}, u32[]{:S(2)}, u32[]{:S(2)}) collective-permute-start(bf16[2,128,512]{2,1,0:T(8,128)(2,1)} %get-tuple-element.76), channel_id=1, source_target_pairs={{0,7},{1,4},{2,5},{3,6},{4,11},{5,8},{6,9},{7,10},{8,15},{9,12},{1... | collective-permute-start | bytes 786440 | tf_op jit(solution)/shard_map/ppermute | solution.py:226
  200.4 38.2 %collective-permute-start.17 = (bf16[2,256,512]{2,1,0:T(8,128)(2,1)}, bf16[2,256,512]{2,1,0:T(8,128)(2,1)}, u32[]{:S(2)}, u32[]{:S(2)}) collective-permute-start(bf16[2,256,512]{2,1,0:T(8,128)(2,1)} %get-tuple-element.54), channel_id=1, source_target_pairs={{0,3},{1,0},{2,1},{3,2},{4,7},{5,4},{6,5},{7,6},{8,11},{9,8},{10,9... | collective-permute-start | bytes 1572872 | tf_op jit(solution)/shard_map/ppermute | solution.py:224
  203.1 23.8 %collective-permute-start.18 = (bf16[2,128,512]{2,1,0:T(8,128)(2,1)S(1)}, bf16[2,128,512]{2,1,0:T(8,128)(2,1)S(1)}, u32[]{:S(2)}, u32[]{:S(2)}) collective-permute-start(bf16[2,128,512]{2,1,0:T(8,128)(2,1)S(1)} %get-tuple-element.75), channel_id=1, source_target_pairs={{0,511},{1,508},{2,509},{3,510},{4,3},{5,0},{6,1},{7,2},{8,7},{9,4... | collective-permute-start | bytes 786440 | tf_op jit(solution)/shard_map/ppermute | solution.py:225
  211.8 17.3 %collective-permute-start.19 = (bf16[2,128,512]{2,1,0:T(8,128)(2,1)}, bf16[2,128,512]{2,1,0:T(8,128)(2,1)}, u32[]{:S(2)}, u32[]{:S(2)}) collective-permute-start(bf16[2,128,512]{2,1,0:T(8,128)(2,1)} %get-tuple-element.74), channel_id=1, source_target_pairs={{0,7},{1,4},{2,5},{3,6},{4,11},{5,8},{6,9},{7,10},{8,15},{9,12},{1... | collective-permute-start | bytes 786440 | tf_op jit(solution)/shard_map/ppermute | solution.py:226
  214.4 33.5 %collective-permute-start.27 = (bf16[2,128,512]{2,1,0:T(8,128)(2,1)}, bf16[2,128,512]{2,1,0:T(8,128)(2,1)}, u32[]{:S(2)}, u32[]{:S(2)}) collective-permute-start(bf16[2,128,512]{2,1,0:T(8,128)(2,1)} %get-tuple-element.78), channel_id=1, source_target_pairs={{0,4},{4,8},{8,12},{12,16},{16,20},{20,24},{24,28},{28,32},{32,36}... | collective-permute-start | bytes 786440 | tf_op jit(solution)/shard_map/ppermute | solution.py:215
  216.3 38.6 %collective-permute-start.26 = (bf16[2,128,512]{2,1,0:T(8,128)(2,1)}, bf16[2,128,512]{2,1,0:T(8,128)(2,1)}, u32[]{:S(2)}, u32[]{:S(2)}) collective-permute-start(bf16[2,128,512]{2,1,0:T(8,128)(2,1)} %get-tuple-element.79), channel_id=1, source_target_pairs={{0,508},{4,0},{8,4},{12,8},{16,12},{20,16},{24,20},{28,24},{32,28}... | collective-permute-start | bytes 786440 | tf_op jit(solution)/shard_map/ppermute | solution.py:214
  226.9 29.9 %collective-permute-start.25 = (bf16[2,128,512]{2,1,0:T(8,128)(2,1)}, bf16[2,128,512]{2,1,0:T(8,128)(2,1)}, u32[]{:S(2)}, u32[]{:S(2)}) collective-permute-start(bf16[2,128,512]{2,1,0:T(8,128)(2,1)} %get-tuple-element.76), channel_id=1, source_target_pairs={{0,4},{4,8},{8,12},{12,16},{16,20},{20,24},{24,28},{28,32},{32,36}... | collective-permute-start | bytes 786440 | tf_op jit(solution)/shard_map/ppermute | solution.py:215
  229.1 38.8 %collective-permute-start.24 = (bf16[2,128,512]{2,1,0:T(8,128)(2,1)}, bf16[2,128,512]{2,1,0:T(8,128)(2,1)S(1)}, u32[]{:S(2)}, u32[]{:S(2)}) collective-permute-start(bf16[2,128,512]{2,1,0:T(8,128)(2,1)} %copy-done.26), channel_id=1, source_target_pairs={{0,508},{4,0},{8,4},{12,8},{16,12},{20,16},{24,20},{28,24},{32,28}... | collective-permute-start | bytes 786440 | tf_op jit(solution)/shard_map/ppermute | solution.py:214
  238.6 29.4 %collective-permute-start.23 = (bf16[2,128,512]{2,1,0:T(8,128)(2,1)}, bf16[2,128,512]{2,1,0:T(8,128)(2,1)S(1)}, u32[]{:S(2)}, u32[]{:S(2)}) collective-permute-start(bf16[2,128,512]{2,1,0:T(8,128)(2,1)} %get-tuple-element.74), channel_id=1, source_target_pairs={{0,4},{4,8},{8,12},{12,16},{16,20},{20,24},{24,28},{28,32},{32,36}... | collective-permute-start | bytes 786440 | tf_op jit(solution)/shard_map/ppermute | solution.py:215
  247.8 20.3 %collective-permute-start.22 = (bf16[2,128,512]{2,1,0:T(8,128)(2,1)S(1)}, bf16[2,128,512]{2,1,0:T(8,128)(2,1)S(1)}, u32[]{:S(2)}, u32[]{:S(2)}) collective-permute-start(bf16[2,128,512]{2,1,0:T(8,128)(2,1)S(1)} %copy-done.28), channel_id=1, source_target_pairs={{0,508},{4,0},{8,4},{12,8},{16,12},{20,16},{24,20},{28,24},{32,28}... | collective-permute-start | bytes 786440 | tf_op jit(solution)/shard_map/ppermute | solution.py:214
  (36 other events, 493.1 us)
where the time goes:
time: 274 us; the launch traced here: 272 us
  starting transfers between devices  133 us (49%)
  waiting for transfers between devices  62.9 us (23%)
  Pallas kernels  47.6 us (17%)
  other arithmetic  13.7 us (5%)
  local copies, waits for them, and re-layouts  10.3 us (4%)
  between operations  5.1 us (2%)
    ppermute x4, starting transfers between devices, shards(): sn = lax.ppermute(to_prev, 'dom', [(i, (i - 1) % D) for i in range(D)])  32.1 us
    ppermute x3, waiting for transfers between devices, shards(): g_next = lax.ppermute(to_prev, both, perm_both(-1, -1))  31.5 us
    ppermute x3, starting transfers between devices, shards(): from_next = lax.ppermute(hp, both, perm_both(-1, 1))  27 us
    pallas_call x4, Pallas kernels, shards(): bwd(hs, pin, g_next, g_prev, a_rec, u_rec, osndt, orcvl, orcvt, *weights,...  26.7 us
    pallas_call x4, Pallas kernels, shards(): fwd(hs, h, from_prev, from_next, osnd, orcv, orcvt, *weights, gain)  21 us
    ppermute x3, waiting for transfers between devices, shards(): from_prev = lax.ppermute(hn, both, perm_both(1, 1))  20.7 us
    ppermute x3, starting transfers between devices, shards(): g_next = lax.ppermute(to_prev, both, perm_both(-1, -1))  19.1 us
    ppermute x1, starting transfers between devices, shards(): from_next = lax.ppermute(prv0, 'dom', [(i, (i - 1) % D) for i in range(D)])  13.3 us
  transfers between devices with their start and end apart: 28, of which 10 were waited for; matrix products, arithmetic and copies ran while one was open for 3% of the time, Pallas kernels for 3%

commit v1 on v0

--- a/solution.py
+++ b/solution.py
@@ -117,6 +117,51 @@
         hg_ref[m] = send_rows[own:].astype(BF16)
 
 
+MESH_ID = pl.DeviceIdType.MESH
+
+
+def comm_kernel(sends, n_in, parts, sections, *refs):
+    ins = refs[:n_in]
+    outs = refs[n_in:n_in + len(sends)]
+    send_sem, recv_sem = refs[n_in + len(sends):]
+    d = lax.axis_index("dom")
+    p = lax.axis_index("pipe")
+    barrier = pltpu.get_barrier_semaphore()
+    for _, _, _, dd, dp in sends:
+        src = (lax.rem(d - dd + parts, parts), lax.rem(p - dp + sections, sections))
+        pl.semaphore_signal(barrier, 1, device_id=src, device_id_type=MESH_ID)
+    pl.semaphore_wait(barrier, len(sends))
+    copies = []
+    for i, (k, start, rows, dd, dp) in enumerate(sends):
+        dst = (lax.rem(d + dd + parts, parts), lax.rem(p + dp + sections, sections))
+        source = ins[k] if start is None else ins[k].at[:, pl.ds(start, rows)]
+        copy = pltpu.make_async_remote_copy(
+            src_ref=source, dst_ref=outs[i], send_sem=send_sem.at[i], recv_sem=recv_sem.at[i],
+            device_id=dst, device_id_type=MESH_ID)
+        copy.start()
+        copies.append(copy)
+    for copy in copies:
+        copy.wait()
+
+
+def exchange(sends, payloads, parts, sections, cid):
+    out_shapes = []
+    for k, start, rows, _, _ in sends:
+        shape = payloads[k].shape
+        if start is not None:
+            shape = (shape[0], rows) + shape[2:]
+        out_shapes.append(jax.ShapeDtypeStruct(shape, payloads[k].dtype))
+    n = len(sends)
+    return pl.pallas_call(
+        functools.partial(comm_kernel, tuple(sends), len(payloads), parts, sections),
+        out_shape=tuple(out_shapes),
+        in_specs=[pl.BlockSpec(memory_space=pl.ANY)] * len(payloads),
+        out_specs=tuple(pl.BlockSpec(memory_space=pl.ANY) for _ in sends),
+        scratch_shapes=[pltpu.SemaphoreType.DMA((n,)), pltpu.SemaphoreType.DMA((n,))],
+        compiler_params=pltpu.CompilerParams(collective_id=cid, has_side_effects=True),
+    )(*payloads)
+
+
 def vmem_call(kernel, out_shapes, n_in, smem_first=True):
     in_specs = [pl.BlockSpec(memory_space=pltpu.SMEM)] + [pl.BlockSpec(memory_space=pltpu.VMEM)] * (n_in - 1)
     return pl.pallas_call(
@@ -185,8 +230,8 @@
         15)
 
     nxt0, prv0 = blocks_of(inputs)
-    from_prev = lax.ppermute(nxt0, "dom", [(i, (i + 1) % D) for i in range(D)])
-    from_next = lax.ppermute(prv0, "dom", [(i, (i - 1) % D) for i in range(D)])
+    from_prev, from_next = exchange(
+        [(0, None, span, 1, 0), (1, None, span, -1, 0)], (nxt0, prv0), D, S, 0)
     h = inputs
     out_rec = a_rec = u_rec = None
     for t in range(S):
@@ -199,9 +244,9 @@
             a_rec = jnp.where(here, a, a_rec)
             u_rec = jnp.where(here, u, u_rec)
         if t < S - 1:
-            h = lax.ppermute(out, "pipe", perm_pipe(1))
-            from_prev = lax.ppermute(hn, both, perm_both(1, 1))
-            from_next = lax.ppermute(hp, both, perm_both(-1, 1))
+            h, from_prev, from_next = exchange(
+                [(0, None, own, 0, 1), (1, None, span, 1, 1), (2, None, span, -1, 1)],
+                (out, hn, hp), D, S, 1)
 
     pin = cotangent
     zeros = jnp.zeros((micro, span, latent), BF16)
@@ -209,10 +254,13 @@
     grad_rec = None
     for t in range(S - 1, -1, -1):
         p32, p16, hg = bwd(hs, pin, g_next, g_prev, a_rec, u_rec, osndt, orcvl, orcvt, *weights, gain)
-        to_prev = hg[:, :span]
-        to_next = hg[:, span:]
-        sn = lax.ppermute(to_prev, "dom", [(i, (i - 1) % D) for i in range(D)])
-        sp = lax.ppermute(to_next, "dom", [(i, (i + 1) % D) for i in range(D)])
+        if t > 0:
+            sn, sp, pin, g_next, g_prev = exchange(
+                [(1, 0, span, -1, 0), (1, span, span, 1, 0), (0, None, own, 0, -1),
+                 (1, 0, span, -1, -1), (1, span, span, 1, -1)],
+                (p16, hg), D, S, 2)
+        else:
+            sn, sp = exchange([(0, 0, span, -1, 0), (0, span, span, 1, 0)], (hg,), D, S, 3)
         shaped = p32.reshape(micro, own // block, block, latent)
         sel = jnp.arange(own // block)[None, :, None, None]
         summed = (shaped + jnp.where(sel == hs[0], sn.astype(F32)[:, None], 0.0)
@@ -220,10 +268,6 @@
         grad = summed.reshape(micro, own, latent).astype(BF16)
         here = p_idx == t
         grad_rec = grad if t == S - 1 else jnp.where(here, grad, grad_rec)
-        if t > 0:
-            pin = lax.ppermute(p16, "pipe", perm_pipe(-1))
-            g_next = lax.ppermute(to_prev, both, perm_both(-1, -1))
-            g_prev = lax.ppermute(to_next, both, perm_both(1, -1))
     return (out_rec[None], grad_rec[None])
 
 

time: 274 us -> 304 us (1.11)
  Pallas kernels: 47.6 us -> 237 us
  starting transfers between devices: 133 us -> 0 us
  waiting for transfers between devices: 62.9 us -> 0 us
  local copies, waits for them, and re-layouts: 10.3 us -> 41.6 us
  other arithmetic: 13.7 us -> 19.5 us
    pallas_call x0 -> x8, Pallas kernels: none -> 191 us  [exchange(): pl.pallas_call(functools.partial(comm_kernel, tuple(sends), len(payloads)...]
    ppermute x28 -> x0, starting transfers between devices: 133 us -> none  [the longest x4 32.1 us: shards(): sn = lax.ppermute(to_prev, 'dom', [(i, (i - 1) % D) for i in range(D)])]
    ppermute x28 -> x0, waiting for transfers between devices: 62.9 us -> none  [the longest x3 31.5 us: shards(): g_next = lax.ppermute(to_prev, both, perm_both(-1, -1))]
    unnamed x64 -> x122, local copies, waits for them, and re-layouts: 6.47 us -> 40.9 us
  transfers between devices with their start and end apart: 28 -> 0, of which waited for: 10 -> 0; matrix products, arithmetic and copies ran while one was open for 3% -> 0% of each run, Pallas kernels for 3% -> 0%
where the time goes in v1:
time: 304 us; the launch traced here: 303 us
  Pallas kernels  237 us (78%)
  local copies, waits for them, and re-layouts  41.6 us (14%)
  other arithmetic  19.5 us (6%)
  between operations  4.79 us (2%)
    pallas_call x8, Pallas kernels, exchange(): pl.pallas_call(functools.partial(comm_kernel, tuple(sends), len(payloads)...  191 us
    unnamed x122, local copies, waits for them, and re-layouts  40.9 us
    pallas_call x4, Pallas kernels, shards(): bwd(hs, pin, g_next, g_prev, a_rec, u_rec, osndt, orcvl, orcvt, *weights,...  26.2 us
    pallas_call x4, Pallas kernels, shards(): fwd(hs, h, from_prev, from_next, osnd, orcv, orcvt, *weights, gain)  20 us

profile of v1, /device:TPU:6, one launch (start us, length us, event | category | flops | bytes accessed | tf_op | source)
XLA Modules:
  0.0 302.7 jit_solution(553734436156474956)
XLA Ops:
  5.7 2.0 fusion.17
  7.7 17.3 %shard_map.131 = (bf16[2,128,512]{2,1,0:T(8,128)(2,1)}, bf16[2,128,512]{2,1,0:T(8,128)(2,1)}) custom-call(bf16[2,128,512]{2,1,0:T(8,128)(2,1)} %get-tuple-element.129.refs_0_, bf16[2,128,512]{2,1,0:T(8,128)(2,1)} %get-tuple-element.128.refs_1_), custom_call_target="tpu_custom_call" | custom-call | tf_op jit(solution)/shard_map/pallas_call | solution.py:155
  26.1 1.0 copy-done.4
  27.1 1.0 copy-done.9
  30.1 4.9 %shard_map.132 = (bf16[2,256,512]{2,1,0:T(8,128)(2,1)S(1)}, f32[2,256,512]{2,1,0:T(8,128)}, f32[2,256,512]{2,1,0:T(8,128)}, bf16[2,128,512]{2,1,0:T(8,128)(2,1)S(1)}, bf16[2,128,512]{2,1,0:T(8,128)(2,1)S(1)}) custom-call(s32[2]{0:T(128)S(1)} %bitcast.145, bf16[2,256,512]{2,1,0:T(8,128)(2,1)S(1)} %copy-done.9, bf16[2,128,512]{2,1,0:T(8,128)(2,1)S(1)} %copy-done.27, ...), custom_call_target="tpu_custom_call" | custom-call | tf_op jit(solution)/shard_map/pallas_call | solution.py:238
  37.2 22.2 %shard_map.133 = (bf16[2,256,512]{2,1,0:T(8,128)(2,1)}, bf16[2,128,512]{2,1,0:T(8,128)(2,1)}, bf16[2,128,512]{2,1,0:T(8,128)(2,1)}) custom-call(bf16[2,256,512]{2,1,0:T(8,128)(2,1)} %copy-done.6, bf16[2,128,512]{2,1,0:T(8,128)(2,1)} %copy-done.45, bf16[2,128,512]{2,1,0:T(8,128)(2,1)} %copy-done.46), custom_call_target="tpu_custom_call" | custom-call | tf_op jit(solution)/shard_map/pallas_call | solution.py:155
  62.4 5.0 %shard_map.134 = (bf16[2,256,512]{2,1,0:T(8,128)(2,1)S(1)}, f32[2,256,512]{2,1,0:T(8,128)}, f32[2,256,512]{2,1,0:T(8,128)}, bf16[2,128,512]{2,1,0:T(8,128)(2,1)S(1)}, bf16[2,128,512]{2,1,0:T(8,128)(2,1)S(1)}) custom-call(s32[2]{0:T(128)S(1)} %bitcast.146, bf16[2,256,512]{2,1,0:T(8,128)(2,1)S(1)} %copy-done.25, bf16[2,128,512]{2,1,0:T(8,128)(2,1)S(1)} %copy-done.33, ...), custom_call_target="tpu_custom_call" | custom-call | tf_op jit(solution)/shard_map/pallas_call | solution.py:238
  69.5 24.0 %shard_map.135 = (bf16[2,256,512]{2,1,0:T(8,128)(2,1)}, bf16[2,128,512]{2,1,0:T(8,128)(2,1)}, bf16[2,128,512]{2,1,0:T(8,128)(2,1)}) custom-call(bf16[2,256,512]{2,1,0:T(8,128)(2,1)} %copy-done.7, bf16[2,128,512]{2,1,0:T(8,128)(2,1)} %copy-done.41, bf16[2,128,512]{2,1,0:T(8,128)(2,1)} %copy-done.42), custom_call_target="tpu_custom_call" | custom-call | tf_op jit(solution)/shard_map/pallas_call | solution.py:155
  96.5 5.0 %shard_map.136 = (bf16[2,256,512]{2,1,0:T(8,128)(2,1)S(1)}, f32[2,256,512]{2,1,0:T(8,128)}, f32[2,256,512]{2,1,0:T(8,128)}, bf16[2,128,512]{2,1,0:T(8,128)(2,1)S(1)}, bf16[2,128,512]{2,1,0:T(8,128)(2,1)S(1)}) custom-call(s32[2]{0:T(128)S(1)} %bitcast.147, bf16[2,256,512]{2,1,0:T(8,128)(2,1)S(1)} %copy-done.26, bf16[2,128,512]{2,1,0:T(8,128)(2,1)S(1)} %copy-done.35, ...), custom_call_target="tpu_custom_call" | custom-call | tf_op jit(solution)/shard_map/pallas_call | solution.py:238
  103.7 27.1 %shard_map.137 = (bf16[2,256,512]{2,1,0:T(8,128)(2,1)}, bf16[2,128,512]{2,1,0:T(8,128)(2,1)}, bf16[2,128,512]{2,1,0:T(8,128)(2,1)}) custom-call(bf16[2,256,512]{2,1,0:T(8,128)(2,1)} %copy-done.8, bf16[2,128,512]{2,1,0:T(8,128)(2,1)} %copy-done.43, bf16[2,128,512]{2,1,0:T(8,128)(2,1)} %copy-done.44), custom_call_target="tpu_custom_call" | custom-call | tf_op jit(solution)/shard_map/pallas_call | solution.py:155
  133.8 5.1 %shard_map.138 = (bf16[2,256,512]{2,1,0:T(8,128)(2,1)S(1)}, f32[2,256,512]{2,1,0:T(8,128)}, f32[2,256,512]{2,1,0:T(8,128)}, bf16[2,128,512]{2,1,0:T(8,128)(2,1)}, bf16[2,128,512]{2,1,0:T(8,128)(2,1)}) custom-call(s32[2]{0:T(128)S(1)} %bitcast.148, bf16[2,256,512]{2,1,0:T(8,128)(2,1)S(1)} %copy-done.24, bf16[2,128,512]{2,1,0:T(8,128)(2,1)S(1)} %copy-done.31, ...), custom_call_target="tpu_custom_call" | custom-call | tf_op jit(solution)/shard_map/pallas_call | solution.py:238
  139.7 2.2 select_bitcast_fusion
  141.9 4.1 %select_select_fusion = (f32[2,256,512]{2,1,0:T(8,128)}, f32[2,256,512]{2,1,0:T(8,128)}) fusion(f32[2,256,512]{2,1,0:T(8,128)} %get-tuple-element.85, f32[2,256,512]{2,1,0:T(8,128)} %get-tuple-element.86, f32[2,256,512]{2,1,0:T(8,128)} %get-tuple-element.87, f32[2,256,512]{2,1,0:T(8,128)S(1)} %copy-done.50, pred[]{:T(512)S(6)} %eq.105, pred[]{:T(512)S(6)} %eq.104, ...), kind=kLoop, calls=%fused_computation.20 | loop fusion | flops 1572864 | bytes 10485763 | tf_op jit(solution)/shard_map/jit(_where)/select_n | solution.py:245
  147.1 5.8 %shard_map.139 = (f32[2,256,512]{2,1,0:T(8,128)S(1)}, bf16[2,256,512]{2,1,0:T(8,128)(2,1)S(1)}, bf16[2,256,512]{2,1,0:T(8,128)(2,1)S(1)}) custom-call(s32[2]{0:T(128)S(1)} %bitcast.149, bf16[2,256,512]{2,1,0:T(8,128)(2,1)S(1)} %copy-done.12, bf16[2,128,512]{2,1,0:T(8,128)(2,1)S(1)} %broadcast_in_dim.144.gn_ref.gp_ref, ...), custom_call_target="tpu_custom_call" | custom-call | tf_op jit(solution)/shard_map/pallas_call | solution.py:256
  155.4 24.9 %shard_map.140 = (bf16[2,128,512]{2,1,0:T(8,128)(2,1)}, bf16[2,128,512]{2,1,0:T(8,128)(2,1)}, bf16[2,256,512]{2,1,0:T(8,128)(2,1)}, bf16[2,128,512]{2,1,0:T(8,128)(2,1)}, bf16[2,128,512]{2,1,0:T(8,128)(2,1)}) custom-call(bf16[2,256,512]{2,1,0:T(8,128)(2,1)} %copy-done.21, bf16[2,256,512]{2,1,0:T(8,128)(2,1)} %copy-done.22), custom_call_target="tpu_custom_call" | custom-call | tf_op jit(solution)/shard_map/pallas_call | solution.py:155
  183.3 6.7 %shard_map.141 = (f32[2,256,512]{2,1,0:T(8,128)}, bf16[2,256,512]{2,1,0:T(8,128)(2,1)S(1)}, bf16[2,256,512]{2,1,0:T(8,128)(2,1)S(1)}) custom-call(s32[2]{0:T(128)S(1)} %bitcast.150, bf16[2,256,512]{2,1,0:T(8,128)(2,1)S(1)} %copy-done.14, bf16[2,128,512]{2,1,0:T(8,128)(2,1)S(1)} %copy-done.37, bf16[2,128,512]{2,1,0:T(8,128)(2,1)S(1)} %copy-done.38, ...), custom_call_target="tpu_custom_call" | custom-call | tf_op jit(solution)/shard_map/pallas_call | solution.py:256
  191.6 27.9 %shard_map.142 = (bf16[2,128,512]{2,1,0:T(8,128)(2,1)}, bf16[2,128,512]{2,1,0:T(8,128)(2,1)}, bf16[2,256,512]{2,1,0:T(8,128)(2,1)}, bf16[2,128,512]{2,1,0:T(8,128)(2,1)}, bf16[2,128,512]{2,1,0:T(8,128)(2,1)}) custom-call(bf16[2,256,512]{2,1,0:T(8,128)(2,1)} %copy-done.17, bf16[2,256,512]{2,1,0:T(8,128)(2,1)} %copy-done.18), custom_call_target="tpu_custom_call" | custom-call | tf_op jit(solution)/shard_map/pallas_call | solution.py:155
  222.4 6.7 %shard_map.143 = (f32[2,256,512]{2,1,0:T(8,128)}, bf16[2,256,512]{2,1,0:T(8,128)(2,1)S(1)}, bf16[2,256,512]{2,1,0:T(8,128)(2,1)S(1)}) custom-call(s32[2]{0:T(128)S(1)} %bitcast.151, bf16[2,256,512]{2,1,0:T(8,128)(2,1)S(1)} %copy-done.15, bf16[2,128,512]{2,1,0:T(8,128)(2,1)S(1)} %copy-done.39, bf16[2,128,512]{2,1,0:T(8,128)(2,1)S(1)} %copy-done.40, ...), custom_call_target="tpu_custom_call" | custom-call | tf_op jit(solution)/shard_map/pallas_call | solution.py:256
  230.7 27.2 %shard_map.144 = (bf16[2,128,512]{2,1,0:T(8,128)(2,1)}, bf16[2,128,512]{2,1,0:T(8,128)(2,1)}, bf16[2,256,512]{2,1,0:T(8,128)(2,1)}, bf16[2,128,512]{2,1,0:T(8,128)(2,1)}, bf16[2,128,512]{2,1,0:T(8,128)(2,1)}) custom-call(bf16[2,256,512]{2,1,0:T(8,128)(2,1)} %copy-done.19, bf16[2,256,512]{2,1,0:T(8,128)(2,1)} %copy-done.20), custom_call_target="tpu_custom_call" | custom-call | tf_op jit(solution)/shard_map/pallas_call | solution.py:155
  260.9 7.1 %shard_map.145 = (f32[2,256,512]{2,1,0:T(8,128)}, bf16[2,256,512]{2,1,0:T(8,128)(2,1)}, bf16[2,256,512]{2,1,0:T(8,128)(2,1)S(1)}) custom-call(s32[2]{0:T(128)S(1)} %bitcast.152, bf16[2,256,512]{2,1,0:T(8,128)(2,1)S(1)} %copy-done.13, bf16[2,128,512]{2,1,0:T(8,128)(2,1)S(1)} %copy-done.29, bf16[2,128,512]{2,1,0:T(8,128)(2,1)S(1)} %copy-done.30, ...), custom_call_target="tpu_custom_call" | custom-call | tf_op jit(solution)/shard_map/pallas_call | solution.py:256
  268.1 1.1 copy-done.51
  273.8 19.8 %shard_map.146 = (bf16[2,128,512]{2,1,0:T(8,128)(2,1)}, bf16[2,128,512]{2,1,0:T(8,128)(2,1)}) custom-call(bf16[2,256,512]{2,1,0:T(8,128)(2,1)} %copy-done.16), custom_call_target="tpu_custom_call" | custom-call | tf_op jit(solution)/shard_map/pallas_call | solution.py:155
  293.7 1.8 convert_element_type.56
  297.7 4.9 %fusion.12 = bf16[2,256,512]{2,1,0:T(8,128)(2,1)} fusion(f32[2,256,512]{2,1,0:T(8,128)} %get-tuple-element.104, f32[2,256,512]{2,1,0:T(8,128)} %get-tuple-element.108, f32[2,256,512]{2,1,0:T(8,128)} %get-tuple-element.111, f32[2,256,512]{2,1,0:T(8,128)S(1)} %copy-done.11, f32[2,128,512]{2,1,0:T(8,128)S(1)} %convert_element_type.65, ...), kind=kLoop, calls=%fused_computation.22 | loop fusion | flops 6029312 | bytes 8913411 | tf_op jit(solution)/shard_map/jit(_where)/select_n | solution.py:270
  (135 shorter events, 42.9 us)
Async XLA Ops:
  5.7 19.3 %copy-start.59 = (s32[2,128]{1,0:T(2,128)S(1)}, s32[2,128]{1,0:T(2,128)}, u32[]{:S(2)}) copy-start(s32[2,128]{1,0:T(2,128)} %param.22) | copy-start | bytes 3076
  5.7 19.5 %copy-start.60 = (s32[2]{0:T(128)S(1)}, s32[2]{0:T(128)}, u32[]{:S(2)}) copy-start(s32[2]{0:T(128)} %param.24) | copy-start | bytes 28
  5.7 19.5 %copy-start.58 = (s32[2,128]{1,0:T(2,128)S(1)}, s32[2,128]{1,0:T(2,128)}, u32[]{:S(2)}) copy-start(s32[2,128]{1,0:T(2,128)} %param.23) | copy-start | bytes 3076
  5.7 19.7 %copy-start.2 = (bf16[1,512,512]{2,1,0:T(8,128)(2,1)S(1)}, bf16[1,512,512]{2,1,0:T(8,128)(2,1)}, u32[]{:S(2)}) copy-start(bf16[1,512,512]{2,1,0:T(8,128)(2,1)} %param.18) | copy-start | bytes 1572868
  5.7 19.7 %copy-start.3 = (bf16[1,512,512]{2,1,0:T(8,128)(2,1)S(1)}, bf16[1,512,512]{2,1,0:T(8,128)(2,1)}, u32[]{:S(2)}) copy-start(bf16[1,512,512]{2,1,0:T(8,128)(2,1)} %param.19) | copy-start | bytes 1572868
  7.7 17.7 %copy-start = (bf16[1,512,512]{2,1,0:T(8,128)(2,1)S(1)}, bf16[1,512,512]{2,1,0:T(8,128)(2,1)}, u32[]{:S(2)}) copy-start(bf16[1,512,512]{2,1,0:T(8,128)(2,1)} %param.16) | copy-start | bytes 1572868
  7.7 17.7 %copy-start.1 = (bf16[1,512,512]{2,1,0:T(8,128)(2,1)S(1)}, bf16[1,512,512]{2,1,0:T(8,128)(2,1)}, u32[]{:S(2)}) copy-start(bf16[1,512,512]{2,1,0:T(8,128)(2,1)} %param.17) | copy-start | bytes 1572868
  26.1 1.0 copy-start.4
  27.1 1.0 copy-start.9
  37.2 22.3 %copy-start.5 = (bf16[1,512,512]{2,1,0:T(8,128)(2,1)S(1)}, bf16[1,512,512]{2,1,0:T(8,128)(2,1)}, u32[]{:S(2)}) copy-start(bf16[1,512,512]{2,1,0:T(8,128)(2,1)} %param.20) | copy-start | bytes 1572868
  59.4 1.0 copy-start.25
  93.6 1.0 copy-start.26
  130.8 1.0 copy-start.24
  139.7 2.2 copy-start.49
  139.7 2.2 copy-start.50
  146.0 1.0 copy-start.12
  180.3 1.0 copy-start.14
  219.5 1.0 copy-start.15
  258.0 1.0 copy-start.13
  260.9 7.1 %copy-start.52 = (bf16[2,128,512]{2,1,0:T(8,128)(2,1)S(1)}, bf16[2,128,512]{2,1,0:T(8,128)(2,1)}, u32[]{:S(2)}) copy-start(bf16[2,128,512]{2,1,0:T(8,128)(2,1)} %get-tuple-element.116) | copy-start | bytes 786436
  268.0 1.2 copy-start.16
  268.0 1.1 copy-start.51
  273.8 23.9 %copy-start.11 = (f32[2,256,512]{2,1,0:T(8,128)S(1)}, f32[2,256,512]{2,1,0:T(8,128)}, u32[]{:S(2)}) copy-start(f32[2,256,512]{2,1,0:T(8,128)} %copy-done.10) | copy-start | bytes 3145732
  293.7 1.9 copy-start.57
  (37 other events, 31.6 us)

commit v2 on v1

--- a/solution.py
+++ b/solution.py
@@ -71,26 +71,14 @@
         hp_ref[m] = sel_p
 
 
-def bwd_kernel(hs_ref, pin_ref, gn_ref, gp_ref, a_ref, u_ref, osndt_ref, orcvl_ref, orcvt_ref,
+def bwd_kernel(hs_ref, pin_ref, a_ref, u_ref, osndt_ref, orcvl_ref, orcvt_ref,
                ws_ref, wr_ref, wm_ref, wn_ref, wa_ref, g_ref,
-               p32_ref, p16_ref, hg_ref):
+               p32_ref, hg_ref):
     own = pin_ref.shape[1]
-    span = gn_ref.shape[1]
-    block = span
-    nblocks = own // block
     gain = g_ref[...]
-    hs0 = hs_ref[0]
-    hs1 = hs_ref[1]
     osndt = osndt_ref[...]
     for m in range(pin_ref.shape[0]):
-        pieces = []
-        gn = gn_ref[m].astype(F32)
-        gp = gp_ref[m].astype(F32)
-        for b in range(nblocks):
-            piece = pin_ref[m, b * block:(b + 1) * block].astype(F32)
-            piece = piece + jnp.where(hs0 == b, gn, 0.0) + jnp.where(hs1 == b, gp, 0.0)
-            pieces.append(piece)
-        c = jnp.concatenate(pieces, axis=0).astype(BF16).astype(F32)
+        c = pin_ref[m].astype(F32)
         node_pre = u_ref[m]
         sig_u = sigmoid(node_pre)
         act = node_pre * sig_u
@@ -113,7 +101,6 @@
         send_rows = split_sum(osndt, mm_t(dedge, ws_ref[...]))
         total = rows + send_rows[:own]
         p32_ref[m] = total
-        p16_ref[m] = total.astype(BF16)
         hg_ref[m] = send_rows[own:].astype(BF16)
 
 
@@ -225,13 +212,12 @@
     bwd = vmem_call(
         bwd_kernel,
         (jax.ShapeDtypeStruct((micro, own, latent), F32),
-         jax.ShapeDtypeStruct((micro, own, latent), BF16),
          jax.ShapeDtypeStruct((micro, 2 * span, latent), BF16)),
-        15)
+        13)
 
     nxt0, prv0 = blocks_of(inputs)
-    from_prev, from_next = exchange(
-        [(0, None, span, 1, 0), (1, None, span, -1, 0)], (nxt0, prv0), D, S, 0)
+    halo_fwd = [(0, None, span, 1, 0), (1, None, span, -1, 0)]
+    from_prev, from_next = exchange(halo_fwd, (nxt0, prv0), D, S, 0)
     h = inputs
     out_rec = a_rec = u_rec = None
     for t in range(S):
@@ -244,23 +230,15 @@
             a_rec = jnp.where(here, a, a_rec)
             u_rec = jnp.where(here, u, u_rec)
         if t < S - 1:
-            h, from_prev, from_next = exchange(
-                [(0, None, own, 0, 1), (1, None, span, 1, 1), (2, None, span, -1, 1)],
-                (out, hn, hp), D, S, 1)
+            (h,) = exchange([(0, None, own, 0, 1)], (out,), D, S, 1)
+            nxt, prv = blocks_of(h)
+            from_prev, from_next = exchange(halo_fwd, (nxt, prv), D, S, 0)
 
     pin = cotangent
-    zeros = jnp.zeros((micro, span, latent), BF16)
-    g_next = g_prev = zeros
     grad_rec = None
     for t in range(S - 1, -1, -1):
-        p32, p16, hg = bwd(hs, pin, g_next, g_prev, a_rec, u_rec, osndt, orcvl, orcvt, *weights, gain)
-        if t > 0:
-            sn, sp, pin, g_next, g_prev = exchange(
-                [(1, 0, span, -1, 0), (1, span, span, 1, 0), (0, None, own, 0, -1),
-                 (1, 0, span, -1, -1), (1, span, span, 1, -1)],
-                (p16, hg), D, S, 2)
-        else:
-            sn, sp = exchange([(0, 0, span, -1, 0), (0, span, span, 1, 0)], (hg,), D, S, 3)
+        p32, hg = bwd(hs, pin, a_rec, u_rec, osndt, orcvl, orcvt, *weights, gain)
+        sn, sp = exchange([(0, 0, span, -1, 0), (0, span, span, 1, 0)], (hg,), D, S, 2)
         shaped = p32.reshape(micro, own // block, block, latent)
         sel = jnp.arange(own // block)[None, :, None, None]
         summed = (shaped + jnp.where(sel == hs[0], sn.astype(F32)[:, None], 0.0)
@@ -268,6 +246,8 @@
         grad = summed.reshape(micro, own, latent).astype(BF16)
         here = p_idx == t
         grad_rec = grad if t == S - 1 else jnp.where(here, grad, grad_rec)
+        if t > 0:
+            (pin,) = exchange([(0, None, own, 0, -1)], (grad,), D, S, 3)
     return (out_rec[None], grad_rec[None])
 
 

time: 304 us -> 268 us (0.88)
  Pallas kernels: 237 us -> 204 us
  local copies, waits for them, and re-layouts: 41.6 us -> 28.7 us
  other arithmetic: 19.5 us -> 29 us
    pallas_call x8 -> x14, Pallas kernels: 191 us -> 161 us  [exchange(): pl.pallas_call(functools.partial(comm_kernel, tuple(sends), len(payloads)...]
    unnamed x122 -> x104, local copies, waits for them, and re-layouts: 40.9 us -> 28.1 us
    select_n x1 -> x4, other arithmetic: 1.96 us -> 7.72 us  [blocks_of(): prv = jnp.take(shaped, hs[1], axis=1)]
    select_n x1, other arithmetic: 4.94 us -> 1.23 us  [shards(): grad_rec = grad if t == S - 1 else jnp.where(here, grad, grad_rec)]
    pallas_call x4, Pallas kernels: 26.2 us -> 22.6 us  [shards(): p32, hg = bwd(hs, pin, a_rec, u_rec, osndt, orcvl, orcvt, *weights, gain)]
    convert_element_type x0 -> x3, other arithmetic: none -> 3.23 us  [shards(): grad = summed.reshape(micro, own, latent).astype(BF16)]
where the time goes in v2:
time: 268 us; the launch traced here: 267 us
  Pallas kernels  204 us (76%)
  other arithmetic  29 us (11%)
  local copies, waits for them, and re-layouts  28.7 us (11%)
  between operations  4.79 us (2%)
    pallas_call x14, Pallas kernels, exchange(): pl.pallas_call(functools.partial(comm_kernel, tuple(sends), len(payloads)...  161 us
    unnamed x104, local copies, waits for them, and re-layouts  28.1 us
    pallas_call x4, Pallas kernels, shards(): p32, hg = bwd(hs, pin, a_rec, u_rec, osndt, orcvl, orcvt, *weights, gain)  22.6 us
    pallas_call x4, Pallas kernels, shards(): fwd(hs, h, from_prev, from_next, osnd, orcv, orcvt, *weights, gain)  20.6 us
    select_n x4, other arithmetic, blocks_of(): prv = jnp.take(shaped, hs[1], axis=1)  7.72 us

profile of v2, /device:TPU:6, one launch (start us, length us, event | category | flops | bytes accessed | tf_op | source)
XLA Modules:
  0.0 266.9 jit_solution(2252841720657347643)
XLA Ops:
  7.5 17.3 %shard_map.131 = (bf16[2,128,512]{2,1,0:T(8,128)(2,1)}, bf16[2,128,512]{2,1,0:T(8,128)(2,1)}) custom-call(bf16[2,128,512]{2,1,0:T(8,128)(2,1)} %get-tuple-element.93.refs_0_, bf16[2,128,512]{2,1,0:T(8,128)(2,1)} %get-tuple-element.92.refs_1_), custom_call_target="tpu_custom_call" | custom-call | tf_op jit(solution)/shard_map/pallas_call | solution.py:142
  30.5 5.1 %shard_map.132 = (bf16[2,256,512]{2,1,0:T(8,128)(2,1)S(1)}, f32[2,256,512]{2,1,0:T(8,128)}, f32[2,256,512]{2,1,0:T(8,128)}, bf16[2,128,512]{2,1,0:T(8,128)(2,1)}, bf16[2,128,512]{2,1,0:T(8,128)(2,1)}) custom-call(s32[2]{0:T(128)S(1)} %bitcast.167, bf16[2,256,512]{2,1,0:T(8,128)(2,1)S(1)} %copy-done.17, bf16[2,128,512]{2,1,0:T(8,128)(2,1)S(1)} %copy-done.35, ...), custom_call_target="tpu_custom_call" | custom-call | tf_op jit(solution)/shard_map/pallas_call | solution.py:224
  36.4 11.7 %shard_map.133.h_ref = bf16[2,256,512]{2,1,0:T(8,128)(2,1)} custom-call(bf16[2,256,512]{2,1,0:T(8,128)(2,1)} %copy-done.14), custom_call_target="tpu_custom_call" | custom-call | tf_op jit(solution)/shard_map/pallas_call | solution.py:142
  50.1 10.4 %shard_map.134 = (bf16[2,128,512]{2,1,0:T(8,128)(2,1)}, bf16[2,128,512]{2,1,0:T(8,128)(2,1)}) custom-call(bf16[2,128,512]{2,1,0:T(8,128)(2,1)} %get-tuple-element.91.refs_0_, bf16[2,128,512]{2,1,0:T(8,128)(2,1)} %get-tuple-element.90.refs_1_), custom_call_target="tpu_custom_call" | custom-call | tf_op jit(solution)/shard_map/pallas_call | solution.py:142
  63.3 5.1 %shard_map.135 = (bf16[2,256,512]{2,1,0:T(8,128)(2,1)S(1)}, f32[2,256,512]{2,1,0:T(8,128)}, f32[2,256,512]{2,1,0:T(8,128)}, bf16[2,128,512]{2,1,0:T(8,128)(2,1)}, bf16[2,128,512]{2,1,0:T(8,128)(2,1)}) custom-call(s32[2]{0:T(128)S(1)} %bitcast.168, bf16[2,256,512]{2,1,0:T(8,128)(2,1)S(1)} %copy-done.7, bf16[2,128,512]{2,1,0:T(8,128)(2,1)S(1)} %copy-done.39, ...), custom_call_target="tpu_custom_call" | custom-call | tf_op jit(solution)/shard_map/pallas_call | solution.py:224
  69.3 12.3 %shard_map.136.h_ref = bf16[2,256,512]{2,1,0:T(8,128)(2,1)} custom-call(bf16[2,256,512]{2,1,0:T(8,128)(2,1)} %copy-done.15), custom_call_target="tpu_custom_call" | custom-call | tf_op jit(solution)/shard_map/pallas_call | solution.py:142
  83.5 10.3 %shard_map.137 = (bf16[2,128,512]{2,1,0:T(8,128)(2,1)}, bf16[2,128,512]{2,1,0:T(8,128)(2,1)}) custom-call(bf16[2,128,512]{2,1,0:T(8,128)(2,1)} %get-tuple-element.89.refs_0_, bf16[2,128,512]{2,1,0:T(8,128)(2,1)} %get-tuple-element.88.refs_1_), custom_call_target="tpu_custom_call" | custom-call | tf_op jit(solution)/shard_map/pallas_call | solution.py:142
  96.7 5.2 %shard_map.138 = (bf16[2,256,512]{2,1,0:T(8,128)(2,1)S(1)}, f32[2,256,512]{2,1,0:T(8,128)}, f32[2,256,512]{2,1,0:T(8,128)}, bf16[2,128,512]{2,1,0:T(8,128)(2,1)}, bf16[2,128,512]{2,1,0:T(8,128)(2,1)}) custom-call(s32[2]{0:T(128)S(1)} %bitcast.169, bf16[2,256,512]{2,1,0:T(8,128)(2,1)S(1)} %copy-done.8, bf16[2,128,512]{2,1,0:T(8,128)(2,1)S(1)} %copy-done.41, ...), custom_call_target="tpu_custom_call" | custom-call | tf_op jit(solution)/shard_map/pallas_call | solution.py:224
  102.6 11.2 %shard_map.139.h_ref = bf16[2,256,512]{2,1,0:T(8,128)(2,1)} custom-call(bf16[2,256,512]{2,1,0:T(8,128)(2,1)} %copy-done.16), custom_call_target="tpu_custom_call" | custom-call | tf_op jit(solution)/shard_map/pallas_call | solution.py:142
  115.8 10.3 %shard_map.140 = (bf16[2,128,512]{2,1,0:T(8,128)(2,1)}, bf16[2,128,512]{2,1,0:T(8,128)(2,1)}) custom-call(bf16[2,128,512]{2,1,0:T(8,128)(2,1)} %get-tuple-element.87.refs_0_, bf16[2,128,512]{2,1,0:T(8,128)(2,1)} %get-tuple-element.86.refs_1_), custom_call_target="tpu_custom_call" | custom-call | tf_op jit(solution)/shard_map/pallas_call | solution.py:142
  128.9 5.2 %shard_map.141 = (bf16[2,256,512]{2,1,0:T(8,128)(2,1)S(1)}, f32[2,256,512]{2,1,0:T(8,128)}, f32[2,256,512]{2,1,0:T(8,128)}, bf16[2,128,512]{2,1,0:T(8,128)(2,1)}, bf16[2,128,512]{2,1,0:T(8,128)(2,1)}) custom-call(s32[2]{0:T(128)S(1)} %bitcast.170, bf16[2,256,512]{2,1,0:T(8,128)(2,1)S(1)} %copy-done.6, bf16[2,128,512]{2,1,0:T(8,128)(2,1)S(1)} %copy-done.37, ...), custom_call_target="tpu_custom_call" | custom-call | tf_op jit(solution)/shard_map/pallas_call | solution.py:224
  134.9 2.2 select_bitcast_fusion
  137.2 3.9 %select_select_fusion = (f32[2,256,512]{2,1,0:T(8,128)}, f32[2,256,512]{2,1,0:T(8,128)}) fusion(f32[2,256,512]{2,1,0:T(8,128)} %get-tuple-element.55, f32[2,256,512]{2,1,0:T(8,128)} %get-tuple-element.56, f32[2,256,512]{2,1,0:T(8,128)} %get-tuple-element.57, f32[2,256,512]{2,1,0:T(8,128)S(1)} %copy-done.48, pred[]{:T(512)S(6)} %eq.105, pred[]{:T(512)S(6)} %eq.104, ...), kind=kLoop, calls=%fused_computation.20 | loop fusion | flops 1572864 | bytes 10485763 | tf_op jit(solution)/shard_map/jit(_where)/select_n | solution.py:231
  142.0 5.6 %shard_map.142 = (f32[2,256,512]{2,1,0:T(8,128)S(1)}, bf16[2,256,512]{2,1,0:T(8,128)(2,1)S(1)}) custom-call(s32[2]{0:T(128)S(1)} %bitcast.171, bf16[2,256,512]{2,1,0:T(8,128)(2,1)S(1)} %copy-done.34, f32[2,256,512]{2,1,0:T(8,128)} %get-tuple-element.100.a_ref, f32[2,256,512]{2,1,0:T(8,128)} %get-tuple-element.99.u_ref, ...), custom_call_target="tpu_custom_call" | custom-call | tf_op jit(solution)/shard_map/pallas_call | solution.py:240
  149.4 10.2 %shard_map.143 = (bf16[2,128,512]{2,1,0:T(8,128)(2,1)}, bf16[2,128,512]{2,1,0:T(8,128)(2,1)}) custom-call(bf16[2,256,512]{2,1,0:T(8,128)(2,1)} %copy-done.32), custom_call_target="tpu_custom_call" | custom-call | tf_op jit(solution)/shard_map/pallas_call | solution.py:142
  164.1 13.4 %shard_map.144.pin_ref = bf16[2,256,512]{2,1,0:T(8,128)(2,1)} custom-call(bf16[2,256,512]{2,1,0:T(8,128)(2,1)} %fusion.10.refs_0_), custom_call_target="tpu_custom_call" | custom-call | tf_op jit(solution)/shard_map/pallas_call | solution.py:142
  178.5 5.6 %shard_map.145 = (f32[2,256,512]{2,1,0:T(8,128)S(1)}, bf16[2,256,512]{2,1,0:T(8,128)(2,1)S(1)}) custom-call(s32[2]{0:T(128)S(1)} %bitcast.172, bf16[2,256,512]{2,1,0:T(8,128)(2,1)S(1)} %copy-done.19, f32[2,256,512]{2,1,0:T(8,128)} %get-tuple-element.100.a_ref, f32[2,256,512]{2,1,0:T(8,128)} %get-tuple-element.99.u_ref, ...), custom_call_target="tpu_custom_call" | custom-call | tf_op jit(solution)/shard_map/pallas_call | solution.py:240
  185.9 10.2 %shard_map.146 = (bf16[2,128,512]{2,1,0:T(8,128)(2,1)}, bf16[2,128,512]{2,1,0:T(8,128)(2,1)}) custom-call(bf16[2,256,512]{2,1,0:T(8,128)(2,1)} %copy-done.30), custom_call_target="tpu_custom_call" | custom-call | tf_op jit(solution)/shard_map/pallas_call | solution.py:142
  199.3 11.6 %shard_map.147.pin_ref = bf16[2,256,512]{2,1,0:T(8,128)(2,1)} custom-call(bf16[2,256,512]{2,1,0:T(8,128)(2,1)} %fusion.7.refs_0_), custom_call_target="tpu_custom_call" | custom-call | tf_op jit(solution)/shard_map/pallas_call | solution.py:142
  212.0 5.6 %shard_map.148 = (f32[2,256,512]{2,1,0:T(8,128)S(1)}, bf16[2,256,512]{2,1,0:T(8,128)(2,1)S(1)}) custom-call(s32[2]{0:T(128)S(1)} %bitcast.173, bf16[2,256,512]{2,1,0:T(8,128)(2,1)S(1)} %copy-done.20, f32[2,256,512]{2,1,0:T(8,128)} %get-tuple-element.100.a_ref, f32[2,256,512]{2,1,0:T(8,128)} %get-tuple-element.99.u_ref, ...), custom_call_target="tpu_custom_call" | custom-call | tf_op jit(solution)/shard_map/pallas_call | solution.py:240
  219.4 10.2 %shard_map.149 = (bf16[2,128,512]{2,1,0:T(8,128)(2,1)}, bf16[2,128,512]{2,1,0:T(8,128)(2,1)}) custom-call(bf16[2,256,512]{2,1,0:T(8,128)(2,1)} %copy-done.31), custom_call_target="tpu_custom_call" | custom-call | tf_op jit(solution)/shard_map/pallas_call | solution.py:142
  232.8 11.6 %shard_map.150.pin_ref = bf16[2,256,512]{2,1,0:T(8,128)(2,1)} custom-call(bf16[2,256,512]{2,1,0:T(8,128)(2,1)} %fusion.4.refs_0_), custom_call_target="tpu_custom_call" | custom-call | tf_op jit(solution)/shard_map/pallas_call | solution.py:142
  245.5 5.8 %shard_map.151 = (f32[2,256,512]{2,1,0:T(8,128)S(1)}, bf16[2,256,512]{2,1,0:T(8,128)(2,1)S(1)}) custom-call(s32[2]{0:T(128)S(1)} %bitcast.174, bf16[2,256,512]{2,1,0:T(8,128)(2,1)S(1)} %copy-done.18, f32[2,256,512]{2,1,0:T(8,128)} %get-tuple-element.100.a_ref, f32[2,256,512]{2,1,0:T(8,128)} %get-tuple-element.99.u_ref, ...), custom_call_target="tpu_custom_call" | custom-call | tf_op jit(solution)/shard_map/pallas_call | solution.py:240
  253.1 10.3 %shard_map.152 = (bf16[2,128,512]{2,1,0:T(8,128)(2,1)}, bf16[2,128,512]{2,1,0:T(8,128)(2,1)}) custom-call(bf16[2,256,512]{2,1,0:T(8,128)(2,1)} %copy-done.29), custom_call_target="tpu_custom_call" | custom-call | tf_op jit(solution)/shard_map/pallas_call | solution.py:142
  (128 shorter events, 51.5 us)
Async XLA Ops:
  5.5 19.3 %copy-start.50 = (s32[2,128]{1,0:T(2,128)S(1)}, s32[2,128]{1,0:T(2,128)}, u32[]{:S(2)}) copy-start(s32[2,128]{1,0:T(2,128)} %param.22) | copy-start | bytes 3076
  5.5 19.5 %copy-start.51 = (s32[2]{0:T(128)S(1)}, s32[2]{0:T(128)}, u32[]{:S(2)}) copy-start(s32[2]{0:T(128)} %param.24) | copy-start | bytes 28
  5.5 19.5 %copy-start.49 = (s32[2,128]{1,0:T(2,128)S(1)}, s32[2,128]{1,0:T(2,128)}, u32[]{:S(2)}) copy-start(s32[2,128]{1,0:T(2,128)} %param.23) | copy-start | bytes 3076
  5.5 20.3 %copy-start.2 = (bf16[1,512,512]{2,1,0:T(8,128)(2,1)S(1)}, bf16[1,512,512]{2,1,0:T(8,128)(2,1)}, u32[]{:S(2)}) copy-start(bf16[1,512,512]{2,1,0:T(8,128)(2,1)} %param.18) | copy-start | bytes 1572868
  5.5 20.3 %copy-start.3 = (bf16[1,512,512]{2,1,0:T(8,128)(2,1)S(1)}, bf16[1,512,512]{2,1,0:T(8,128)(2,1)}, u32[]{:S(2)}) copy-start(bf16[1,512,512]{2,1,0:T(8,128)(2,1)} %param.19) | copy-start | bytes 1572868
  7.5 18.3 %copy-start = (bf16[1,512,512]{2,1,0:T(8,128)(2,1)S(1)}, bf16[1,512,512]{2,1,0:T(8,128)(2,1)}, u32[]{:S(2)}) copy-start(bf16[1,512,512]{2,1,0:T(8,128)(2,1)} %param.16) | copy-start | bytes 1572868
  7.5 18.3 %copy-start.1 = (bf16[1,512,512]{2,1,0:T(8,128)(2,1)S(1)}, bf16[1,512,512]{2,1,0:T(8,128)(2,1)}, u32[]{:S(2)}) copy-start(bf16[1,512,512]{2,1,0:T(8,128)(2,1)} %param.17) | copy-start | bytes 1572868
  25.8 9.8 %copy-start.10 = (bf16[256,256]{1,0:T(8,128)(2,1)}, bf16[256,256]{1,0:T(8,128)(2,1)S(1)}, u32[]{:S(2)}) copy-start(bf16[256,256]{1,0:T(8,128)(2,1)S(1)} %get-tuple-element.96.orcv_ref) | copy-start | bytes 393220
  48.1 12.4 %copy-start.7 = (bf16[2,256,512]{2,1,0:T(8,128)(2,1)S(1)}, bf16[2,256,512]{2,1,0:T(8,128)(2,1)}, u32[]{:S(2)}) copy-start(bf16[2,256,512]{2,1,0:T(8,128)(2,1)} %shard_map.133.h_ref) | copy-start | bytes 1572868
  50.1 10.5 %copy-start.5 = (bf16[1,512,512]{2,1,0:T(8,128)(2,1)S(1)}, bf16[1,512,512]{2,1,0:T(8,128)(2,1)}, u32[]{:S(2)}) copy-start(bf16[1,512,512]{2,1,0:T(8,128)(2,1)} %param.20) | copy-start | bytes 1572868
  83.5 10.3 %copy-start.8 = (bf16[2,256,512]{2,1,0:T(8,128)(2,1)S(1)}, bf16[2,256,512]{2,1,0:T(8,128)(2,1)}, u32[]{:S(2)}) copy-start(bf16[2,256,512]{2,1,0:T(8,128)(2,1)} %shard_map.136.h_ref) | copy-start | bytes 1572868
  115.8 10.3 %copy-start.6 = (bf16[2,256,512]{2,1,0:T(8,128)(2,1)S(1)}, bf16[2,256,512]{2,1,0:T(8,128)(2,1)}, u32[]{:S(2)}) copy-start(bf16[2,256,512]{2,1,0:T(8,128)(2,1)} %shard_map.139.h_ref) | copy-start | bytes 1572868
  134.9 2.2 copy-start.47
  134.9 2.2 copy-start.48
  137.2 4.0 %copy-start.34 = (bf16[2,256,512]{2,1,0:T(8,128)(2,1)S(1)}, bf16[2,256,512]{2,1,0:T(8,128)(2,1)}, u32[]{:S(2)}) copy-start(bf16[2,256,512]{2,1,0:T(8,128)(2,1)} %pin_ref.1) | copy-start | bytes 1572868
  159.6 3.4 %copy-start.22 = (f32[2,256,512]{2,1,0:T(8,128)S(1)}, f32[2,256,512]{2,1,0:T(8,128)}, u32[]{:S(2)}) copy-start(f32[2,256,512]{2,1,0:T(8,128)} %copy-done.21) | copy-start | bytes 3145732
  177.4 1.0 copy-start.19
  196.1 2.1 copy-start.24
  210.9 1.0 copy-start.20
  229.6 2.1 copy-start.26
  244.4 1.0 copy-start.18
  253.1 12.5 %copy-start.28 = (f32[2,256,512]{2,1,0:T(8,128)S(1)}, f32[2,256,512]{2,1,0:T(8,128)}, u32[]{:S(2)}) copy-start(f32[2,256,512]{2,1,0:T(8,128)} %copy-done.27) | copy-start | bytes 3145732
  263.4 2.2 copy-start.46
  264.5 1.1 copy-start.45
  (28 other events, 25.0 us)

commit v3 on v2

--- a/solution.py
+++ b/solution.py
@@ -149,6 +149,156 @@
     )(*payloads)
 
 
+def fwd_comm_kernel(parts, sections, hs_ref, out_ref, h_ref, fp_ref, fn_ref,
+                    hbuf, fpbuf, fnbuf, stage_n, stage_p, send_sem, recv_sem):
+    micro, own, _ = out_ref.shape
+    block = fp_ref.shape[1]
+    d = lax.axis_index("dom")
+    p = lax.axis_index("pipe")
+    pipe_next = (d, lax.rem(p + 1, sections))
+    pipe_prev = (d, lax.rem(p - 1 + sections, sections))
+    dom_next = (lax.rem(d + 1, parts), p)
+    dom_prev = (lax.rem(d - 1 + parts, parts), p)
+    barrier = pltpu.get_barrier_semaphore()
+    for src in (pipe_prev, dom_prev, dom_next):
+        pl.semaphore_signal(barrier, 1, device_id=src, device_id_type=MESH_ID)
+    pl.semaphore_wait(barrier, 3)
+    pipe_copies = []
+    for m in range(micro):
+        copy = pltpu.make_async_remote_copy(
+            src_ref=out_ref.at[m], dst_ref=hbuf.at[m], send_sem=send_sem.at[0, m],
+            recv_sem=recv_sem.at[0, m], device_id=pipe_next, device_id_type=MESH_ID)
+        copy.start()
+        pipe_copies.append(copy)
+    hs0 = hs_ref[0]
+    hs1 = hs_ref[1]
+    halo_copies = []
+    for m in range(micro):
+        pipe_copies[m].wait_recv()
+        h = hbuf[m]
+        sel_n = h[0:block]
+        sel_p = h[0:block]
+        for b in range(1, own // block):
+            piece = h[b * block:(b + 1) * block]
+            sel_n = jnp.where(hs0 == b, piece, sel_n)
+            sel_p = jnp.where(hs1 == b, piece, sel_p)
+        stage_n[m] = sel_n
+        stage_p[m] = sel_p
+        for j, (stage, buf, dst) in enumerate(((stage_n, fpbuf, dom_next), (stage_p, fnbuf, dom_prev))):
+            copy = pltpu.make_async_remote_copy(
+                src_ref=stage.at[m], dst_ref=buf.at[m], send_sem=send_sem.at[1 + j, m],
+                recv_sem=recv_sem.at[1 + j, m], device_id=dst, device_id_type=MESH_ID)
+            copy.start()
+            halo_copies.append(copy)
+    for copy in pipe_copies:
+        copy.wait_send()
+    for copy in halo_copies:
+        copy.wait()
+    h_ref[...] = hbuf[...]
+    fp_ref[...] = fpbuf[...]
+    fn_ref[...] = fnbuf[...]
+
+
+def fwd_comm(hs, out, span, parts, sections):
+    micro, own, latent = out.shape
+    vm = pl.BlockSpec(memory_space=pltpu.VMEM)
+    return pl.pallas_call(
+        functools.partial(fwd_comm_kernel, parts, sections),
+        out_shape=(jax.ShapeDtypeStruct((micro, own, latent), out.dtype),
+                   jax.ShapeDtypeStruct((micro, span, latent), out.dtype),
+                   jax.ShapeDtypeStruct((micro, span, latent), out.dtype)),
+        in_specs=[pl.BlockSpec(memory_space=pltpu.SMEM), vm],
+        out_specs=(vm, vm, vm),
+        scratch_shapes=[pltpu.VMEM((micro, own, latent), out.dtype),
+                        pltpu.VMEM((micro, span, latent), out.dtype),
+                        pltpu.VMEM((micro, span, latent), out.dtype),
+                        pltpu.VMEM((micro, span, latent), out.dtype),
+                        pltpu.VMEM((micro, span, latent), out.dtype),
+                        pltpu.SemaphoreType.DMA((3, micro)),
+                        pltpu.SemaphoreType.DMA((3, micro))],
+        compiler_params=pltpu.CompilerParams(collective_id=4, has_side_effects=True,
+                                             vmem_limit_bytes=48 * 1024 * 1024),
+    )(hs, out)
+
+
+def bwd_comm_kernel(parts, sections, send_pipe, hs_ref, p32_ref, hg_ref, *refs):
+    if send_pipe:
+        grad_ref, pin_ref, snbuf, spbuf, gbuf, pinbuf, send_sem, recv_sem = refs
+    else:
+        grad_ref, snbuf, spbuf, gbuf, send_sem, recv_sem = refs
+    micro, own, _ = p32_ref.shape
+    block = snbuf.shape[1]
+    d = lax.axis_index("dom")
+    p = lax.axis_index("pipe")
+    pipe_prev = (d, lax.rem(p - 1 + sections, sections))
+    pipe_next = (d, lax.rem(p + 1, sections))
+    dom_next = (lax.rem(d + 1, parts), p)
+    dom_prev = (lax.rem(d - 1 + parts, parts), p)
+    barrier = pltpu.get_barrier_semaphore()
+    sources = [dom_next, dom_prev] + ([pipe_next] if send_pipe else [])
+    for src in sources:
+        pl.semaphore_signal(barrier, 1, device_id=src, device_id_type=MESH_ID)
+    pl.semaphore_wait(barrier, len(sources))
+    halo_copies = []
+    for m in range(micro):
+        pair = []
+        for j, (lo, buf, dst) in enumerate(((0, snbuf, dom_prev), (block, spbuf, dom_next))):
+            copy = pltpu.make_async_remote_copy(
+                src_ref=hg_ref.at[m, pl.ds(lo, block)], dst_ref=buf.at[m],
+                send_sem=send_sem.at[j, m], recv_sem=recv_sem.at[j, m],
+                device_id=dst, device_id_type=MESH_ID)
+            copy.start()
+            pair.append(copy)
+        halo_copies.append(pair)
+    hs0 = hs_ref[0]
+    hs1 = hs_ref[1]
+    pipe_copies = []
+    for m in range(micro):
+        for copy in halo_copies[m]:
+            copy.wait_recv()
+        sn = snbuf[m].astype(F32)
+        sp = spbuf[m].astype(F32)
+        for b in range(own // block):
+            piece = p32_ref[m, b * block:(b + 1) * block]
+            piece = piece + jnp.where(hs0 == b, sn, 0.0) + jnp.where(hs1 == b, sp, 0.0)
+            gbuf[m, b * block:(b + 1) * block] = piece.astype(gbuf.dtype)
+        if send_pipe:
+            copy = pltpu.make_async_remote_copy(
+                src_ref=gbuf.at[m], dst_ref=pinbuf.at[m], send_sem=send_sem.at[2, m],
+                recv_sem=recv_sem.at[2, m], device_id=pipe_prev, device_id_type=MESH_ID)
+            copy.start()
+            pipe_copies.append(copy)
+    for pair in halo_copies:
+        for copy in pair:
+            copy.wait_send()
+    for copy in pipe_copies:
+        copy.wait()
+    grad_ref[...] = gbuf[...]
+    if send_pipe:
+        pin_ref[...] = pinbuf[...]
+
+
+def bwd_comm(hs, p32, hg, span, parts, sections, send_pipe):
+    micro, own, latent = p32.shape
+    vm = pl.BlockSpec(memory_space=pltpu.VMEM)
+    grad = jax.ShapeDtypeStruct((micro, own, latent), BF16)
+    scratch = [pltpu.VMEM((micro, span, latent), BF16), pltpu.VMEM((micro, span, latent), BF16),
+               pltpu.VMEM((micro, own, latent), BF16)]
+    if send_pipe:
+        scratch.append(pltpu.VMEM((micro, own, latent), BF16))
+    scratch += [pltpu.SemaphoreType.DMA((3, micro)), pltpu.SemaphoreType.DMA((3, micro))]
+    outs = (grad, grad) if send_pipe else (grad,)
+    return pl.pallas_call(
+        functools.partial(bwd_comm_kernel, parts, sections, send_pipe),
+        out_shape=outs,
+        in_specs=[pl.BlockSpec(memory_space=pltpu.SMEM), vm, vm],
+        out_specs=tuple(vm for _ in outs),
+        scratch_shapes=scratch,
+        compiler_params=pltpu.CompilerParams(collective_id=5 if send_pipe else 6, has_side_effects=True,
+                                             vmem_limit_bytes=48 * 1024 * 1024),
+    )(hs, p32, hg)
+
+
 def vmem_call(kernel, out_shapes, n_in, smem_first=True):
     in_specs = [pl.BlockSpec(memory_space=pltpu.SMEM)] + [pl.BlockSpec(memory_space=pltpu.VMEM)] * (n_in - 1)
     return pl.pallas_call(
@@ -230,24 +380,18 @@
             a_rec = jnp.where(here, a, a_rec)
             u_rec = jnp.where(here, u, u_rec)
         if t < S - 1:
-            (h,) = exchange([(0, None, own, 0, 1)], (out,), D, S, 1)
-            nxt, prv = blocks_of(h)
-            from_prev, from_next = exchange(halo_fwd, (nxt, prv), D, S, 0)
+            h, from_prev, from_next = fwd_comm(hs, out, span, D, S)
 
     pin = cotangent
     grad_rec = None
     for t in range(S - 1, -1, -1):
         p32, hg = bwd(hs, pin, a_rec, u_rec, osndt, orcvl, orcvt, *weights, gain)
-        sn, sp = exchange([(0, 0, span, -1, 0), (0, span, span, 1, 0)], (hg,), D, S, 2)
-        shaped = p32.reshape(micro, own // block, block, latent)
-        sel = jnp.arange(own // block)[None, :, None, None]
-        summed = (shaped + jnp.where(sel == hs[0], sn.astype(F32)[:, None], 0.0)
-                  + jnp.where(sel == hs[1], sp.astype(F32)[:, None], 0.0))
-        grad = summed.reshape(micro, own, latent).astype(BF16)
+        if t > 0:
+            grad, pin = bwd_comm(hs, p32, hg, span, D, S, True)
+        else:
+            (grad,) = bwd_comm(hs, p32, hg, span, D, S, False)
         here = p_idx == t
         grad_rec = grad if t == S - 1 else jnp.where(here, grad, grad_rec)
-        if t > 0:
-            (pin,) = exchange([(0, None, own, 0, -1)], (grad,), D, S, 3)
     return (out_rec[None], grad_rec[None])
 
 

time: 268 us -> 212 us (0.79)
  the two profiles are of different devices: /device:TPU:6 before, /device:TPU:4 now
where the time goes in v3:
time: 212 us; the launch traced here: 211 us
  Pallas kernels  190 us (90%)
  other arithmetic  9.6 us (5%)
  local copies, waits for them, and re-layouts  6.71 us (3%)
  between operations  4.82 us (2%)
    pallas_call x4, Pallas kernels, bwd_comm(): pl.pallas_call(functools.partial(bwd_comm_kernel, parts, sections, send_p...  66 us
    pallas_call x3, Pallas kernels, fwd_comm(): pl.pallas_call(functools.partial(fwd_comm_kernel, parts, sections), out_s...  63.6 us
    pallas_call x4, Pallas kernels, shards(): p32, hg = bwd(hs, pin, a_rec, u_rec, osndt, orcvl, orcvt, *weights, gain)  22.7 us
    pallas_call x4, Pallas kernels, shards(): fwd(hs, h, from_prev, from_next, osnd, orcv, orcvt, *weights, gain)  20.5 us
    pallas_call x1, Pallas kernels, exchange(): pl.pallas_call(functools.partial(comm_kernel, tuple(sends), len(payloads)...  17.3 us
    unnamed x42, local copies, waits for them, and re-layouts  6.13 us
    select_n x1, other arithmetic, shards(): u_rec = jnp.where(here, u, u_rec)  4.26 us

profile of v3, /device:TPU:4, one launch (start us, length us, event | category | flops | bytes accessed | tf_op | source)
XLA Modules:
  0.0 211.3 jit_solution(1161354132604008319)
XLA Ops:
  5.8 2.0 fusion.2
  7.8 17.3 %shard_map.131 = (bf16[2,128,512]{2,1,0:T(8,128)(2,1)}, bf16[2,128,512]{2,1,0:T(8,128)(2,1)}) custom-call(bf16[2,128,512]{2,1,0:T(8,128)(2,1)} %get-tuple-element.89.refs_0_, bf16[2,128,512]{2,1,0:T(8,128)(2,1)} %get-tuple-element.88.refs_1_), custom_call_target="tpu_custom_call" | custom-call | tf_op jit(solution)/shard_map/pallas_call | solution.py:142
  26.2 1.0 copy-done.4
  27.2 1.0 copy-done.7
  28.3 0.9 copy-done.12
  29.2 0.9 copy-done.13
  30.2 5.1 %shard_map.132 = (bf16[2,256,512]{2,1,0:T(8,128)(2,1)S(1)}, f32[2,256,512]{2,1,0:T(8,128)}, f32[2,256,512]{2,1,0:T(8,128)}, bf16[2,128,512]{2,1,0:T(8,128)(2,1)}, bf16[2,128,512]{2,1,0:T(8,128)(2,1)}) custom-call(s32[2]{0:T(128)S(1)} %bitcast.70, bf16[2,256,512]{2,1,0:T(8,128)(2,1)S(1)} %copy-done.7, bf16[2,128,512]{2,1,0:T(8,128)(2,1)S(1)} %copy-done.12, ...), custom_call_target="tpu_custom_call" | custom-call | tf_op jit(solution)/shard_map/pallas_call | solution.py:374
  35.3 21.8 %shard_map.133 = (bf16[2,256,512]{2,1,0:T(8,128)(2,1)S(1)}, bf16[2,128,512]{2,1,0:T(8,128)(2,1)S(1)}, bf16[2,128,512]{2,1,0:T(8,128)(2,1)S(1)}) custom-call(s32[2]{0:T(128)S(1)} %bitcast.71, bf16[2,256,512]{2,1,0:T(8,128)(2,1)S(1)} %get-tuple-element.42.out_ref), custom_call_target="tpu_custom_call" | custom-call | tf_op jit(solution)/shard_map/pallas_call | solution.py:205
  57.1 5.1 %shard_map.134 = (bf16[2,256,512]{2,1,0:T(8,128)(2,1)S(1)}, f32[2,256,512]{2,1,0:T(8,128)}, f32[2,256,512]{2,1,0:T(8,128)}, bf16[2,128,512]{2,1,0:T(8,128)(2,1)}, bf16[2,128,512]{2,1,0:T(8,128)(2,1)}) custom-call(s32[2]{0:T(128)S(1)} %bitcast.72, bf16[2,256,512]{2,1,0:T(8,128)(2,1)S(1)} %get-tuple-element.43.h_ref, ...), custom_call_target="tpu_custom_call" | custom-call | tf_op jit(solution)/shard_map/pallas_call | solution.py:374
  62.2 18.5 %shard_map.135 = (bf16[2,256,512]{2,1,0:T(8,128)(2,1)S(1)}, bf16[2,128,512]{2,1,0:T(8,128)(2,1)S(1)}, bf16[2,128,512]{2,1,0:T(8,128)(2,1)S(1)}) custom-call(s32[2]{0:T(128)S(1)} %bitcast.73, bf16[2,256,512]{2,1,0:T(8,128)(2,1)S(1)} %get-tuple-element.46.out_ref), custom_call_target="tpu_custom_call" | custom-call | tf_op jit(solution)/shard_map/pallas_call | solution.py:205
  80.7 5.1 %shard_map.136 = (bf16[2,256,512]{2,1,0:T(8,128)(2,1)S(1)}, f32[2,256,512]{2,1,0:T(8,128)}, f32[2,256,512]{2,1,0:T(8,128)}, bf16[2,128,512]{2,1,0:T(8,128)(2,1)}, bf16[2,128,512]{2,1,0:T(8,128)(2,1)}) custom-call(s32[2]{0:T(128)S(1)} %bitcast.74, bf16[2,256,512]{2,1,0:T(8,128)(2,1)S(1)} %get-tuple-element.47.h_ref, ...), custom_call_target="tpu_custom_call" | custom-call | tf_op jit(solution)/shard_map/pallas_call | solution.py:374
  85.8 23.3 %shard_map.137 = (bf16[2,256,512]{2,1,0:T(8,128)(2,1)S(1)}, bf16[2,128,512]{2,1,0:T(8,128)(2,1)S(1)}, bf16[2,128,512]{2,1,0:T(8,128)(2,1)S(1)}) custom-call(s32[2]{0:T(128)S(1)} %bitcast.75, bf16[2,256,512]{2,1,0:T(8,128)(2,1)S(1)} %get-tuple-element.50.out_ref), custom_call_target="tpu_custom_call" | custom-call | tf_op jit(solution)/shard_map/pallas_call | solution.py:205
  109.1 5.1 %shard_map.138 = (bf16[2,256,512]{2,1,0:T(8,128)(2,1)S(1)}, f32[2,256,512]{2,1,0:T(8,128)}, f32[2,256,512]{2,1,0:T(8,128)}, bf16[2,128,512]{2,1,0:T(8,128)(2,1)}, bf16[2,128,512]{2,1,0:T(8,128)(2,1)}) custom-call(s32[2]{0:T(128)S(1)} %bitcast.76, bf16[2,256,512]{2,1,0:T(8,128)(2,1)S(1)} %get-tuple-element.51.h_ref, ...), custom_call_target="tpu_custom_call" | custom-call | tf_op jit(solution)/shard_map/pallas_call | solution.py:374
  115.1 2.1 select_bitcast_fusion.1
  117.2 4.3 %select_select_fusion = (f32[2,256,512]{2,1,0:T(8,128)}, f32[2,256,512]{2,1,0:T(8,128)}) fusion(f32[2,256,512]{2,1,0:T(8,128)} %get-tuple-element.59, f32[2,256,512]{2,1,0:T(8,128)} %get-tuple-element.60, f32[2,256,512]{2,1,0:T(8,128)} %get-tuple-element.61, f32[2,256,512]{2,1,0:T(8,128)S(1)} %copy-done.17, pred[]{:T(512)S(6)} %eq.71, pred[]{:T(512)S(6)} %eq.70, ...), kind=kLoop, calls=%fused_computation | loop fusion | flops 1572864 | bytes 10485763 | tf_op jit(solution)/shard_map/jit(_where)/select_n | solution.py:381
  121.5 5.6 %shard_map.139 = (f32[2,256,512]{2,1,0:T(8,128)S(1)}, bf16[2,256,512]{2,1,0:T(8,128)(2,1)S(1)}) custom-call(s32[2]{0:T(128)S(1)} %bitcast.77, bf16[2,256,512]{2,1,0:T(8,128)(2,1)S(1)} %copy-done.11, f32[2,256,512]{2,1,0:T(8,128)} %get-tuple-element.96.a_ref, f32[2,256,512]{2,1,0:T(8,128)} %get-tuple-element.95.u_ref, bf16[512,256]{1,0:T(8,128)(2,1)S(1)} %fusion.1.osndt_ref, ...), custom_call_target="tpu_custom_call" | custom-call | tf_op jit(solution)/shard_map/pallas_call | solution.py:388
  127.1 17.0 %shard_map.140 = (bf16[2,256,512]{2,1,0:T(8,128)(2,1)S(1)}, bf16[2,256,512]{2,1,0:T(8,128)(2,1)S(1)}) custom-call(s32[2]{0:T(128)S(1)} %bitcast.78, f32[2,256,512]{2,1,0:T(8,128)S(1)} %get-tuple-element.63.p32_ref, bf16[2,256,512]{2,1,0:T(8,128)(2,1)S(1)} %get-tuple-element.64.hg_ref), custom_call_target="tpu_custom_call" | custom-call | tf_op jit(solution)/shard_map/pallas_call | solution.py:291
  144.1 5.6 %shard_map.141 = (f32[2,256,512]{2,1,0:T(8,128)S(1)}, bf16[2,256,512]{2,1,0:T(8,128)(2,1)S(1)}) custom-call(s32[2]{0:T(128)S(1)} %bitcast.79, bf16[2,256,512]{2,1,0:T(8,128)(2,1)S(1)} %get-tuple-element.65.pin_ref, f32[2,256,512]{2,1,0:T(8,128)} %get-tuple-element.96.a_ref, f32[2,256,512]{2,1,0:T(8,128)} %get-tuple-element.95.u_ref, ...), custom_call_target="tpu_custom_call" | custom-call | tf_op jit(solution)/shard_map/pallas_call | solution.py:388
  149.7 18.4 %shard_map.142 = (bf16[2,256,512]{2,1,0:T(8,128)(2,1)S(1)}, bf16[2,256,512]{2,1,0:T(8,128)(2,1)S(1)}) custom-call(s32[2]{0:T(128)S(1)} %bitcast.80, f32[2,256,512]{2,1,0:T(8,128)S(1)} %get-tuple-element.66.p32_ref, bf16[2,256,512]{2,1,0:T(8,128)(2,1)S(1)} %get-tuple-element.67.hg_ref), custom_call_target="tpu_custom_call" | custom-call | tf_op jit(solution)/shard_map/pallas_call | solution.py:291
  168.1 5.6 %shard_map.143 = (f32[2,256,512]{2,1,0:T(8,128)S(1)}, bf16[2,256,512]{2,1,0:T(8,128)(2,1)S(1)}) custom-call(s32[2]{0:T(128)S(1)} %bitcast.81, bf16[2,256,512]{2,1,0:T(8,128)(2,1)S(1)} %get-tuple-element.68.pin_ref, f32[2,256,512]{2,1,0:T(8,128)} %get-tuple-element.96.a_ref, f32[2,256,512]{2,1,0:T(8,128)} %get-tuple-element.95.u_ref, ...), custom_call_target="tpu_custom_call" | custom-call | tf_op jit(solution)/shard_map/pallas_call | solution.py:388
  173.7 19.9 %shard_map.144 = (bf16[2,256,512]{2,1,0:T(8,128)(2,1)S(1)}, bf16[2,256,512]{2,1,0:T(8,128)(2,1)S(1)}) custom-call(s32[2]{0:T(128)S(1)} %bitcast.82, f32[2,256,512]{2,1,0:T(8,128)S(1)} %get-tuple-element.69.p32_ref, bf16[2,256,512]{2,1,0:T(8,128)(2,1)S(1)} %get-tuple-element.70.hg_ref), custom_call_target="tpu_custom_call" | custom-call | tf_op jit(solution)/shard_map/pallas_call | solution.py:291
  193.6 6.0 %shard_map.145 = (f32[2,256,512]{2,1,0:T(8,128)S(1)}, bf16[2,256,512]{2,1,0:T(8,128)(2,1)S(1)}) custom-call(s32[2]{0:T(128)S(1)} %bitcast.83, bf16[2,256,512]{2,1,0:T(8,128)(2,1)S(1)} %get-tuple-element.71.pin_ref, f32[2,256,512]{2,1,0:T(8,128)} %get-tuple-element.96.a_ref, f32[2,256,512]{2,1,0:T(8,128)} %get-tuple-element.95.u_ref, ...), custom_call_target="tpu_custom_call" | custom-call | tf_op jit(solution)/shard_map/pallas_call | solution.py:388
  199.6 10.8 %shard_map.146 = bf16[2,256,512]{2,1,0:T(8,128)(2,1)S(1)} custom-call(s32[2]{0:T(128)S(1)} %bitcast.84, f32[2,256,512]{2,1,0:T(8,128)S(1)} %get-tuple-element.72.p32_ref, bf16[2,256,512]{2,1,0:T(8,128)(2,1)S(1)} %get-tuple-element.73.hg_ref), custom_call_target="tpu_custom_call" | custom-call | tf_op jit(solution)/shard_map/pallas_call | solution.py:291
  210.4 0.9 select_bitcast_fusion
  (43 shorter events, 3.2 us)
Async XLA Ops:
  0.6 0.7 copy-start.14
  5.8 19.3 %copy-start.19 = (s32[2,128]{1,0:T(2,128)S(1)}, s32[2,128]{1,0:T(2,128)}, u32[]{:S(2)}) copy-start(s32[2,128]{1,0:T(2,128)} %param.22) | copy-start | bytes 3076
  5.8 19.5 %copy-start.20 = (s32[2]{0:T(128)S(1)}, s32[2]{0:T(128)}, u32[]{:S(2)}) copy-start(s32[2]{0:T(128)} %param.24) | copy-start | bytes 28
  5.8 19.5 %copy-start.18 = (s32[2,128]{1,0:T(2,128)S(1)}, s32[2,128]{1,0:T(2,128)}, u32[]{:S(2)}) copy-start(s32[2,128]{1,0:T(2,128)} %param.23) | copy-start | bytes 3076
  5.8 19.7 %copy-start.2 = (bf16[1,512,512]{2,1,0:T(8,128)(2,1)S(1)}, bf16[1,512,512]{2,1,0:T(8,128)(2,1)}, u32[]{:S(2)}) copy-start(bf16[1,512,512]{2,1,0:T(8,128)(2,1)} %param.18) | copy-start | bytes 1572868
  5.8 19.7 %copy-start.3 = (bf16[1,512,512]{2,1,0:T(8,128)(2,1)S(1)}, bf16[1,512,512]{2,1,0:T(8,128)(2,1)}, u32[]{:S(2)}) copy-start(bf16[1,512,512]{2,1,0:T(8,128)(2,1)} %param.19) | copy-start | bytes 1572868
  7.8 17.7 %copy-start = (bf16[1,512,512]{2,1,0:T(8,128)(2,1)S(1)}, bf16[1,512,512]{2,1,0:T(8,128)(2,1)}, u32[]{:S(2)}) copy-start(bf16[1,512,512]{2,1,0:T(8,128)(2,1)} %param.16) | copy-start | bytes 1572868
  7.8 17.7 %copy-start.1 = (bf16[1,512,512]{2,1,0:T(8,128)(2,1)S(1)}, bf16[1,512,512]{2,1,0:T(8,128)(2,1)}, u32[]{:S(2)}) copy-start(bf16[1,512,512]{2,1,0:T(8,128)(2,1)} %param.17) | copy-start | bytes 1572868
  25.5 0.7 copy-start.15
  26.2 1.0 copy-start.4
  27.2 1.0 copy-start.7
  28.3 0.9 copy-start.12
  29.2 0.9 copy-start.13
  85.8 28.5 %copy-start.6 = (bf16[2,256,512]{2,1,0:T(8,128)(2,1)}, bf16[2,256,512]{2,1,0:T(8,128)(2,1)S(1)}, u32[]{:S(2)}) copy-start(bf16[2,256,512]{2,1,0:T(8,128)(2,1)S(1)} %get-tuple-element.50.out_ref) | copy-start | bytes 1572868
  114.3 0.8 copy-start.8
  115.1 2.1 copy-start.16
  115.1 2.1 copy-start.17
  117.1 4.4 %copy-start.5 = (bf16[1,512,512]{2,1,0:T(8,128)(2,1)S(1)}, bf16[1,512,512]{2,1,0:T(8,128)(2,1)}, u32[]{:S(2)}) copy-start(bf16[1,512,512]{2,1,0:T(8,128)(2,1)} %param.20) | copy-start | bytes 1572868
  117.2 4.4 %copy-start.11 = (bf16[2,256,512]{2,1,0:T(8,128)(2,1)S(1)}, bf16[2,256,512]{2,1,0:T(8,128)(2,1)}, u32[]{:S(2)}) copy-start(bf16[2,256,512]{2,1,0:T(8,128)(2,1)} %pin_ref.1) | copy-start | bytes 1572868
  193.6 6.0 %copy-start.9 = (bf16[2,256,512]{2,1,0:T(8,128)(2,1)}, bf16[2,256,512]{2,1,0:T(8,128)(2,1)S(1)}, u32[]{:S(2)}) copy-start(bf16[2,256,512]{2,1,0:T(8,128)(2,1)S(1)} %get-tuple-element.74) | copy-start | bytes 1572868
  199.5 10.8 %copy-start.10 = (bf16[2,256,512]{2,1,0:T(8,128)(2,1)S(1)}, bf16[2,256,512]{2,1,0:T(8,128)(2,1)}, u32[]{:S(2)}) copy-start(bf16[2,256,512]{2,1,0:T(8,128)(2,1)} %copy-done.9) | copy-start | bytes 1572868

commit v4 on v3

--- a/solution.py
+++ b/solution.py
@@ -30,78 +30,63 @@
     return mm(onehot, hi) + mm(onehot, lo)
 
 
-def fwd_kernel(hs_ref, h_ref, fp_ref, fn_ref, osnd_ref, orcv_ref, orcvt_ref,
-               ws_ref, wr_ref, wm_ref, wn_ref, wa_ref, g_ref,
-               out_ref, a_ref, u_ref, hn_ref, hp_ref):
+def fwd_micro(m, hs_ref, h_ref, fp_ref, fn_ref, osnd_ref, orcv_ref, orcvt_ref,
+              ws_ref, wr_ref, wm_ref, wn_ref, wa_ref, g_ref, out_ref, a_ref, u_ref):
     own = h_ref.shape[1]
     span = fp_ref.shape[1]
-    block = span
-    gain = g_ref[...]
     osnd = osnd_ref[...]
-    for m in range(h_ref.shape[0]):
-        h = h_ref[m]
-        gathered = (mm(osnd[:, :own], h) + mm(osnd[:, own:own + span], fp_ref[m])
-                    + mm(osnd[:, own + span:], fn_ref[m])).astype(BF16)
-        send_part = mm(gathered, ws_ref[...]).astype(BF16).astype(F32)
-        recv_rows = mm(orcv_ref[...], h).astype(BF16)
-        pre = send_part + mm(recv_rows, wr_ref[...])
-        a_ref[m] = pre
-        edge_hidden = (pre * sigmoid(pre)).astype(BF16)
-        messages = mm(edge_hidden, wm_ref[...])
-        agg = split_sum(orcvt_ref[...], messages).astype(BF16)
-        node_pre = mm(h, wn_ref[...]) + mm(agg, wa_ref[...])
-        u_ref[m] = node_pre
-        act = node_pre * sigmoid(node_pre)
-        mean = jnp.mean(act, axis=-1, keepdims=True)
-        cen = act - mean
-        var = jnp.mean(cen * cen, axis=-1, keepdims=True)
-        unit = cen * lax.rsqrt(var + EPSILON)
-        out = (h.astype(F32) + unit * gain).astype(BF16)
-        out_ref[m] = out
-        hs0 = hs_ref[0]
-        hs1 = hs_ref[1]
-        nblocks = own // block
-        sel_n = out[0:block]
-        sel_p = out[0:block]
-        for b in range(1, nblocks):
-            piece = out[b * block:(b + 1) * block]
-            sel_n = jnp.where(hs0 == b, piece, sel_n)
-            sel_p = jnp.where(hs1 == b, piece, sel_p)
-        hn_ref[m] = sel_n
-        hp_ref[m] = sel_p
-
-
-def bwd_kernel(hs_ref, pin_ref, a_ref, u_ref, osndt_ref, orcvl_ref, orcvt_ref,
-               ws_ref, wr_ref, wm_ref, wn_ref, wa_ref, g_ref,
-               p32_ref, hg_ref):
+    h = h_ref[m]
+    gathered = (mm(osnd[:, :own], h) + mm(osnd[:, own:own + span], fp_ref[m])
+                + mm(osnd[:, own + span:], fn_ref[m])).astype(BF16)
+    send_part = mm(gathered, ws_ref[...]).astype(BF16).astype(F32)
+    recv_rows = mm(orcv_ref[...], h).astype(BF16)
+    pre = send_part + mm(recv_rows, wr_ref[...])
+    a_ref[m] = pre
+    edge_hidden = (pre * sigmoid(pre)).astype(BF16)
+    messages = mm(edge_hidden, wm_ref[...])
+    agg = split_sum(orcvt_ref[...], messages).astype(BF16)
+    node_pre = mm(h, wn_ref[...]) + mm(agg, wa_ref[...])
+    u_ref[m] = node_pre
+    act = node_pre * sigmoid(node_pre)
+    mean = jnp.mean(act, axis=-1, keepdims=True)
+    cen = act - mean
+    var = jnp.mean(cen * cen, axis=-1, keepdims=True)
+    unit = cen * lax.rsqrt(var + EPSILON)
+    out_ref[m] = (h.astype(F32) + unit * g_ref[...]).astype(BF16)
+
+
+def fwd_kernel(*refs):
+    for m in range(refs[1].shape[0]):
+        fwd_micro(m, *refs)
+
+
+def bwd_micro(m, pin_ref, a_ref, u_ref, osndt_ref, orcvl_ref, orcvt_ref,
+              ws_ref, wr_ref, wm_ref, wn_ref, wa_ref, g_ref, p32_ref, hg_ref):
     own = pin_ref.shape[1]
     gain = g_ref[...]
-    osndt = osndt_ref[...]
-    for m in range(pin_ref.shape[0]):
-        c = pin_ref[m].astype(F32)
-        node_pre = u_ref[m]
-        sig_u = sigmoid(node_pre)
-        act = node_pre * sig_u
-        mean = jnp.mean(act, axis=-1, keepdims=True)
-        cen = act - mean
-        var = jnp.mean(cen * cen, axis=-1, keepdims=True)
-        rs = lax.rsqrt(var + EPSILON)
-        unit = cen * rs
-        gu = c * gain
-        gact = rs * (gu - jnp.mean(gu, axis=-1, keepdims=True)
-                     - unit * jnp.mean(gu * unit, axis=-1, keepdims=True))
-        du = (gact * (sig_u * (1.0 + node_pre * (1.0 - sig_u)))).astype(BF16)
-        dagg = mm_t(du, wa_ref[...]).astype(BF16)
-        rows = c + mm_t(du, wn_ref[...])
-        gmsg = mm(orcvl_ref[...], dagg).astype(BF16)
-        pre = a_ref[m]
-        sig_a = sigmoid(pre)
-        dedge = (mm_t(gmsg, wm_ref[...]) * (sig_a * (1.0 + pre * (1.0 - sig_a)))).astype(BF16)
-        rows = rows + split_sum(orcvt_ref[...], mm_t(dedge, wr_ref[...]))
-        send_rows = split_sum(osndt, mm_t(dedge, ws_ref[...]))
-        total = rows + send_rows[:own]
-        p32_ref[m] = total
-        hg_ref[m] = send_rows[own:].astype(BF16)
+    c = pin_ref[m].astype(F32)
+    node_pre = u_ref[m]
+    sig_u = sigmoid(node_pre)
+    act = node_pre * sig_u
+    mean = jnp.mean(act, axis=-1, keepdims=True)
+    cen = act - mean
+    var = jnp.mean(cen * cen, axis=-1, keepdims=True)
+    rs = lax.rsqrt(var + EPSILON)
+    unit = cen * rs
+    gu = c * gain
+    gact = rs * (gu - jnp.mean(gu, axis=-1, keepdims=True)
+                 - unit * jnp.mean(gu * unit, axis=-1, keepdims=True))
+    du = (gact * (sig_u * (1.0 + node_pre * (1.0 - sig_u)))).astype(BF16)
+    dagg = mm_t(du, wa_ref[...]).astype(BF16)
+    rows = c + mm_t(du, wn_ref[...])
+    gmsg = mm(orcvl_ref[...], dagg).astype(BF16)
+    pre = a_ref[m]
+    sig_a = sigmoid(pre)
+    dedge = (mm_t(gmsg, wm_ref[...]) * (sig_a * (1.0 + pre * (1.0 - sig_a)))).astype(BF16)
+    rows = rows + split_sum(orcvt_ref[...], mm_t(dedge, wr_ref[...]))
+    send_rows = split_sum(osndt_ref[...], mm_t(dedge, ws_ref[...]))
+    p32_ref[m] = rows + send_rows[:own]
+    hg_ref[m] = send_rows[own:].astype(BF16)
 
 
 MESH_ID = pl.DeviceIdType.MESH
@@ -149,9 +134,11 @@
     )(*payloads)
 
 
-def fwd_comm_kernel(parts, sections, hs_ref, out_ref, h_ref, fp_ref, fn_ref,
+def fwd_tick_kernel(parts, sections, hs_ref, h_ref, fp_ref, fn_ref, osnd_ref, orcv_ref, orcvt_ref,
+                    ws_ref, wr_ref, wm_ref, wn_ref, wa_ref, g_ref,
+                    out_ref, a_ref, u_ref, hn_ref, fpn_ref, fnn_ref,
                     hbuf, fpbuf, fnbuf, stage_n, stage_p, send_sem, recv_sem):
-    micro, own, _ = out_ref.shape
+    micro, own, _ = h_ref.shape
     block = fp_ref.shape[1]
     d = lax.axis_index("dom")
     p = lax.axis_index("pipe")
@@ -162,9 +149,13 @@
     barrier = pltpu.get_barrier_semaphore()
     for src in (pipe_prev, dom_prev, dom_next):
         pl.semaphore_signal(barrier, 1, device_id=src, device_id_type=MESH_ID)
-    pl.semaphore_wait(barrier, 3)
+    compute_refs = (hs_ref, h_ref, fp_ref, fn_ref, osnd_ref, orcv_ref, orcvt_ref,
+                    ws_ref, wr_ref, wm_ref, wn_ref, wa_ref, g_ref, out_ref, a_ref, u_ref)
     pipe_copies = []
     for m in range(micro):
+        fwd_micro(m, *compute_refs)
+        if m == 0:
+            pl.semaphore_wait(barrier, 3)
         copy = pltpu.make_async_remote_copy(
             src_ref=out_ref.at[m], dst_ref=hbuf.at[m], send_sem=send_sem.at[0, m],
             recv_sem=recv_sem.at[0, m], device_id=pipe_next, device_id_type=MESH_ID)
@@ -194,39 +185,41 @@
         copy.wait_send()
     for copy in halo_copies:
         copy.wait()
-    h_ref[...] = hbuf[...]
-    fp_ref[...] = fpbuf[...]
-    fn_ref[...] = fnbuf[...]
-
-
-def fwd_comm(hs, out, span, parts, sections):
-    micro, own, latent = out.shape
+    hn_ref[...] = hbuf[...]
+    fpn_ref[...] = fpbuf[...]
+    fnn_ref[...] = fnbuf[...]
+
+
+def fwd_tick(operands, span, parts, sections):
+    h = operands[1]
+    micro, own, latent = h.shape
     vm = pl.BlockSpec(memory_space=pltpu.VMEM)
+    bf = lambda rows: jax.ShapeDtypeStruct((micro, rows, latent), BF16)
+    f32 = jax.ShapeDtypeStruct((micro, own, latent), F32)
     return pl.pallas_call(
-        functools.partial(fwd_comm_kernel, parts, sections),
-        out_shape=(jax.ShapeDtypeStruct((micro, own, latent), out.dtype),
-                   jax.ShapeDtypeStruct((micro, span, latent), out.dtype),
-                   jax.ShapeDtypeStruct((micro, span, latent), out.dtype)),
-        in_specs=[pl.BlockSpec(memory_space=pltpu.SMEM), vm],
-        out_specs=(vm, vm, vm),
-        scratch_shapes=[pltpu.VMEM((micro, own, latent), out.dtype),
-                        pltpu.VMEM((micro, span, latent), out.dtype),
-                        pltpu.VMEM((micro, span, latent), out.dtype),
-                        pltpu.VMEM((micro, span, latent), out.dtype),
-                        pltpu.VMEM((micro, span, latent), out.dtype),
+        functools.partial(fwd_tick_kernel, parts, sections),
+        out_shape=(bf(own), f32, f32, bf(own), bf(span), bf(span)),
+        in_specs=[pl.BlockSpec(memory_space=pltpu.SMEM)] + [vm] * (len(operands) - 1),
+        out_specs=tuple(vm for _ in range(6)),
+        scratch_shapes=[pltpu.VMEM((micro, own, latent), BF16),
+                        pltpu.VMEM((micro, span, latent), BF16),
+                        pltpu.VMEM((micro, span, latent), BF16),
+                        pltpu.VMEM((micro, span, latent), BF16),
+                        pltpu.VMEM((micro, span, latent), BF16),
                         pltpu.SemaphoreType.DMA((3, micro)),
                         pltpu.SemaphoreType.DMA((3, micro))],
         compiler_params=pltpu.CompilerParams(collective_id=4, has_side_effects=True,
                                              vmem_limit_bytes=48 * 1024 * 1024),
-    )(hs, out)
-
-
-def bwd_comm_kernel(parts, sections, send_pipe, hs_ref, p32_ref, hg_ref, *refs):
+    )(*operands)
+
+
+def bwd_tick_kernel(parts, sections, send_pipe, hs_ref, pin_ref, a_ref, u_ref, osndt_ref, orcvl_ref,
+                    orcvt_ref, ws_ref, wr_ref, wm_ref, wn_ref, wa_ref, g_ref, *refs):
     if send_pipe:
-        grad_ref, pin_ref, snbuf, spbuf, gbuf, pinbuf, send_sem, recv_sem = refs
+        grad_ref, pinn_ref, p32, hg, snbuf, spbuf, gbuf, pinbuf, send_sem, recv_sem = refs
     else:
-        grad_ref, snbuf, spbuf, gbuf, send_sem, recv_sem = refs
-    micro, own, _ = p32_ref.shape
+        grad_ref, p32, hg, snbuf, spbuf, gbuf, send_sem, recv_sem = refs
+    micro, own, _ = pin_ref.shape
     block = snbuf.shape[1]
     d = lax.axis_index("dom")
     p = lax.axis_index("pipe")
@@ -238,13 +231,17 @@
     sources = [dom_next, dom_prev] + ([pipe_next] if send_pipe else [])
     for src in sources:
         pl.semaphore_signal(barrier, 1, device_id=src, device_id_type=MESH_ID)
-    pl.semaphore_wait(barrier, len(sources))
+    compute_refs = (pin_ref, a_ref, u_ref, osndt_ref, orcvl_ref, orcvt_ref,
+                    ws_ref, wr_ref, wm_ref, wn_ref, wa_ref, g_ref, p32, hg)
     halo_copies = []
     for m in range(micro):
+        bwd_micro(m, *compute_refs)
+        if m == 0:
+            pl.semaphore_wait(barrier, len(sources))
         pair = []
         for j, (lo, buf, dst) in enumerate(((0, snbuf, dom_prev), (block, spbuf, dom_next))):
             copy = pltpu.make_async_remote_copy(
-                src_ref=hg_ref.at[m, pl.ds(lo, block)], dst_ref=buf.at[m],
+                src_ref=hg.at[m, pl.ds(lo, block)], dst_ref=buf.at[m],
                 send_sem=send_sem.at[j, m], recv_sem=recv_sem.at[j, m],
                 device_id=dst, device_id_type=MESH_ID)
             copy.start()
@@ -259,7 +256,7 @@
         sn = snbuf[m].astype(F32)
         sp = spbuf[m].astype(F32)
         for b in range(own // block):
-            piece = p32_ref[m, b * block:(b + 1) * block]
+            piece = p32[m, b * block:(b + 1) * block]
             piece = piece + jnp.where(hs0 == b, sn, 0.0) + jnp.where(hs1 == b, sp, 0.0)
             gbuf[m, b * block:(b + 1) * block] = piece.astype(gbuf.dtype)
         if send_pipe:
@@ -275,28 +272,30 @@
         copy.wait()
     grad_ref[...] = gbuf[...]
     if send_pipe:
-        pin_ref[...] = pinbuf[...]
-
-
-def bwd_comm(hs, p32, hg, span, parts, sections, send_pipe):
-    micro, own, latent = p32.shape
+        pinn_ref[...] = pinbuf[...]
+
+
+def bwd_tick(operands, span, parts, sections, send_pipe):
+    pin = operands[1]
+    micro, own, latent = pin.shape
     vm = pl.BlockSpec(memory_space=pltpu.VMEM)
     grad = jax.ShapeDtypeStruct((micro, own, latent), BF16)
-    scratch = [pltpu.VMEM((micro, span, latent), BF16), pltpu.VMEM((micro, span, latent), BF16),
+    scratch = [pltpu.VMEM((micro, own, latent), F32), pltpu.VMEM((micro, 2 * span, latent), BF16),
+               pltpu.VMEM((micro, span, latent), BF16), pltpu.VMEM((micro, span, latent), BF16),
                pltpu.VMEM((micro, own, latent), BF16)]
     if send_pipe:
         scratch.append(pltpu.VMEM((micro, own, latent), BF16))
     scratch += [pltpu.SemaphoreType.DMA((3, micro)), pltpu.SemaphoreType.DMA((3, micro))]
     outs = (grad, grad) if send_pipe else (grad,)
     return pl.pallas_call(
-        functools.partial(bwd_comm_kernel, parts, sections, send_pipe),
+        functools.partial(bwd_tick_kernel, parts, sections, send_pipe),
         out_shape=outs,
-        in_specs=[pl.BlockSpec(memory_space=pltpu.SMEM), vm, vm],
+        in_specs=[pl.BlockSpec(memory_space=pltpu.SMEM)] + [vm] * (len(operands) - 1),
         out_specs=tuple(vm for _ in outs),
         scratch_shapes=scratch,
         compiler_params=pltpu.CompilerParams(collective_id=5 if send_pipe else 6, has_side_effects=True,
                                              vmem_limit_bytes=48 * 1024 * 1024),
-    )(hs, p32, hg)
+    )(*operands)
 
 
 def vmem_call(kernel, out_shapes, n_in, smem_first=True):
@@ -355,14 +354,7 @@
         fwd_kernel,
         (jax.ShapeDtypeStruct((micro, own, latent), BF16),
          jax.ShapeDtypeStruct((micro, own, latent), F32),
-         jax.ShapeDtypeStruct((micro, own, latent), F32),
-         jax.ShapeDtypeStruct((micro, span, latent), BF16),
-         jax.ShapeDtypeStruct((micro, span, latent), BF16)),
-        13)
-    bwd = vmem_call(
-        bwd_kernel,
-        (jax.ShapeDtypeStruct((micro, own, latent), F32),
-         jax.ShapeDtypeStruct((micro, 2 * span, latent), BF16)),
+         jax.ShapeDtypeStruct((micro, own, latent), F32)),
         13)
 
     nxt0, prv0 = blocks_of(inputs)
@@ -371,7 +363,11 @@
     h = inputs
     out_rec = a_rec = u_rec = None
     for t in range(S):
-        out, a, u, hn, hp = fwd(hs, h, from_prev, from_next, osnd, orcv, orcvt, *weights, gain)
+        operands = (hs, h, from_prev, from_next, osnd, orcv, orcvt, *weights, gain)
+        if t < S - 1:
+            out, a, u, h, from_prev, from_next = fwd_tick(operands, span, D, S)
+        else:
+            out, a, u = fwd(*operands)
         here = p_idx == t
         if t == 0:
             out_rec, a_rec, u_rec = out, a, u
@@ -379,17 +375,15 @@
             out_rec = jnp.where(here, out, out_rec)
             a_rec = jnp.where(here, a, a_rec)
             u_rec = jnp.where(here, u, u_rec)
-        if t < S - 1:
-            h, from_prev, from_next = fwd_comm(hs, out, span, D, S)
 
     pin = cotangent
     grad_rec = None
     for t in range(S - 1, -1, -1):
-        p32, hg = bwd(hs, pin, a_rec, u_rec, osndt, orcvl, orcvt, *weights, gain)
+        operands = (hs, pin, a_rec, u_rec, osndt, orcvl, orcvt, *weights, gain)
         if t > 0:
-            grad, pin = bwd_comm(hs, p32, hg, span, D, S, True)
+            grad, pin = bwd_tick(operands, span, D, S, True)
         else:
-            (grad,) = bwd_comm(hs, p32, hg, span, D, S, False)
+            (grad,) = bwd_tick(operands, span, D, S, False)
         here = p_idx == t
         grad_rec = grad if t == S - 1 else jnp.where(here, grad, grad_rec)
     return (out_rec[None], grad_rec[None])

time: 212 us -> 187 us (0.88)
  Pallas kernels: 190 us -> 161 us
  local copies, waits for them, and re-layouts: 6.71 us -> 9.95 us
    pallas_call x15 -> x8, Pallas kernels: 173 us -> 144 us  [the longest x4 71.8 us: bwd_tick(): pl.pallas_call(functools.partial(bwd_tick_kernel, parts, sections, send_p...]
    unnamed x42 -> x46, local copies, waits for them, and re-layouts: 6.13 us -> 9.37 us
where the time goes in v4:
time: 187 us; the launch traced here: 186 us
  Pallas kernels  161 us (86%)
  other arithmetic  10.4 us (6%)
  local copies, waits for them, and re-layouts  9.95 us (5%)
  between operations  4.8 us (3%)
    pallas_call x4, Pallas kernels, bwd_tick(): pl.pallas_call(functools.partial(bwd_tick_kernel, parts, sections, send_p...  71.8 us
    pallas_call x3, Pallas kernels, fwd_tick(): pl.pallas_call(functools.partial(fwd_tick_kernel, parts, sections), out_s...  67.2 us
    pallas_call x1, Pallas kernels, exchange(): pl.pallas_call(functools.partial(comm_kernel, tuple(sends), len(payloads)...  17.3 us
    unnamed x46, local copies, waits for them, and re-layouts  9.37 us
    pallas_call x1, Pallas kernels, shards(): out, a, u = fwd(*operands)  4.91 us
    broadcast_in_dim x2, other arithmetic, shards(): return (out_rec[None], grad_rec[None])  4.18 us
    select_n x1, other arithmetic, shards(): u_rec = jnp.where(here, u, u_rec)  3.82 us

profile of v4, /device:TPU:4, one launch (start us, length us, event | category | flops | bytes accessed | tf_op | source)
XLA Modules:
  0.0 186.4 jit_solution(12081686492639285734)
XLA Ops:
  0.6 0.6 copy-done.17
  5.8 2.0 %fusion.2 = (bf16[2,128,512]{2,1,0:T(8,128)(2,1)}, bf16[2,128,512]{2,1,0:T(8,128)(2,1)}) fusion(bf16[2,2,128,512]{3,2,1,0:T(8,128)(2,1)} %bitcast.69, s32[]{:T(128)S(6)} %select_n.91, pred[]{:T(512)S(6)} %and.25, s32[]{:T(128)S(6)} %select_n.89, pred[]{:T(512)S(6)} %and.24), kind=kLoop, calls=%fused_computation.9 | loop fusion | flops 262144 | bytes 1048586 | tf_op jit(solution)/shard_map/jit(_take)/select_n | solution.py:339
  7.8 17.3 %shard_map.131 = (bf16[2,128,512]{2,1,0:T(8,128)(2,1)}, bf16[2,128,512]{2,1,0:T(8,128)(2,1)}) custom-call(bf16[2,128,512]{2,1,0:T(8,128)(2,1)} %get-tuple-element.73.refs_0_, bf16[2,128,512]{2,1,0:T(8,128)(2,1)} %get-tuple-element.72.refs_1_), custom_call_target="tpu_custom_call" | custom-call | tf_op jit(solution)/shard_map/pallas_call | solution.py:127
  25.5 0.6 copy-done.16
  26.2 1.0 copy-done.4
  27.2 1.0 copy-done.6
  28.3 0.9 copy-done.14
  29.2 0.9 copy-done.15
  30.2 23.2 %shard_map.132 = (bf16[2,256,512]{2,1,0:T(8,128)(2,1)S(1)}, f32[2,256,512]{2,1,0:T(8,128)}, f32[2,256,512]{2,1,0:T(8,128)}, bf16[2,256,512]{2,1,0:T(8,128)(2,1)S...) custom-call(s32[2]{0:T(128)S(1)} %bitcast.70, bf16[2,256,512]{2,1,0:T(8,128)(2,1)S(1)} %copy-done.6, ...), custom_call_target="tpu_custom_call" | custom-call | tf_op jit(solution)/shard_map/pallas_call | solution.py:199
  53.4 0.8 copy-done.7
  54.2 18.9 %shard_map.133 = (bf16[2,256,512]{2,1,0:T(8,128)(2,1)S(1)}, f32[2,256,512]{2,1,0:T(8,128)}, f32[2,256,512]{2,1,0:T(8,128)}, bf16[2,256,512]{2,1,0:T(8,128)(2,1)S...) custom-call(s32[2]{0:T(128)S(1)} %bitcast.71, bf16[2,256,512]{2,1,0:T(8,128)(2,1)S(1)} %get-tuple-element.34.h_ref, ...), custom_call_target="tpu_custom_call" | custom-call | tf_op jit(solution)/shard_map/pallas_call | solution.py:199
  73.1 0.8 copy-done.8
  73.9 25.1 %shard_map.134 = (bf16[2,256,512]{2,1,0:T(8,128)(2,1)S(1)}, f32[2,256,512]{2,1,0:T(8,128)}, f32[2,256,512]{2,1,0:T(8,128)}, bf16[2,256,512]{2,1,0:T(8,128)(2,1)S...) custom-call(s32[2]{0:T(128)S(1)} %bitcast.72, bf16[2,256,512]{2,1,0:T(8,128)(2,1)S(1)} %get-tuple-element.37.h_ref, ...), custom_call_target="tpu_custom_call" | custom-call | tf_op jit(solution)/shard_map/pallas_call | solution.py:199
  99.1 0.8 copy-done.9
  99.9 4.9 %shard_map.135 = (bf16[2,256,512]{2,1,0:T(8,128)(2,1)S(1)}, f32[2,256,512]{2,1,0:T(8,128)S(1)}, f32[2,256,512]{2,1,0:T(8,128)}) custom-call(s32[2]{0:T(128)S(1)} %bitcast.73, bf16[2,256,512]{2,1,0:T(8,128)(2,1)S(1)} %get-tuple-element.40.refs_1_, bf16[2,128,512]{2,1,0:T(8,128)(2,1)S(1)} %get-tuple-element.41.refs_2_, ...), custom_call_target="tpu_custom_call" | custom-call | tf_op jit(solution)/shard_map/pallas_call | solution.py:370
  104.8 0.8 copy-done.10
  105.6 2.2 %select_bitcast_fusion.1 = bf16[1,2,256,512]{3,2,1,0:T(8,128)(2,1)} fusion(bf16[2,256,512]{2,1,0:T(8,128)(2,1)} %copy-done.10, bf16[2,256,512]{2,1,0:T(8,128)(2,1)} %copy-done.9, bf16[2,256,512]{2,1,0:T(8,128)(2,1)} %copy-done.8, bf16[2,256,512]{2,1,0:T(8,128)(2,1)} %copy-done.7, pred[]{:T(512)S(6)} %eq.71, pred[]{:T(512)S(6)} %eq.70, pred[]{:T(512)S(6)} %eq.58), kind=kLoop, calls=%fused_computation.4 | loop fusion | flops 786432 | bytes 2621443 | tf_op jit(solution)/shard_map/broadcast_in_dim | solution.py:389
  107.9 3.8 %select_select_fusion = (f32[2,256,512]{2,1,0:T(8,128)}, f32[2,256,512]{2,1,0:T(8,128)S(1)}) fusion(f32[2,256,512]{2,1,0:T(8,128)} %get-tuple-element.51, f32[2,256,512]{2,1,0:T(8,128)} %get-tuple-element.52, f32[2,256,512]{2,1,0:T(8,128)} %get-tuple-element.53, f32[2,256,512]{2,1,0:T(8,128)S(1)} %copy-done.19, pred[]{:T(512)S(6)} %eq.71, pred[]{:T(512)S(6)} %eq.70, ...), kind=kLoop, calls=%fused_computation | loop fusion | flops 1572864 | bytes 10485763 | tf_op jit(solution)/shard_map/jit(_where)/select_n | solution.py:377
  111.8 17.7 %shard_map.136 = (bf16[2,256,512]{2,1,0:T(8,128)(2,1)S(1)}, bf16[2,256,512]{2,1,0:T(8,128)(2,1)S(1)}) custom-call(s32[2]{0:T(128)S(1)} %bitcast.74, bf16[2,256,512]{2,1,0:T(8,128)(2,1)S(1)} %copy-done.13, f32[2,256,512]{2,1,0:T(8,128)S(1)} %get-tuple-element.80.a_ref, f32[2,256,512]{2,1,0:T(8,128)} %get-tuple-element.79.u_ref, ...), custom_call_target="tpu_custom_call" | custom-call | tf_op jit(solution)/shard_map/pallas_call | solution.py:290
  129.5 19.2 %shard_map.137 = (bf16[2,256,512]{2,1,0:T(8,128)(2,1)S(1)}, bf16[2,256,512]{2,1,0:T(8,128)(2,1)S(1)}) custom-call(s32[2]{0:T(128)S(1)} %bitcast.75, bf16[2,256,512]{2,1,0:T(8,128)(2,1)S(1)} %get-tuple-element.55.pin_ref, f32[2,256,512]{2,1,0:T(8,128)S(1)} %get-tuple-element.80.a_ref, f32[2,256,512]{2,1,0:T(8,128)} %get-tuple-element.79.u_ref, ...), custom_call_target="tpu_custom_call" | custom-call | tf_op jit(solution)/shard_map/pallas_call | solution.py:290
  148.7 0.8 copy-done.11
  149.5 21.0 %shard_map.138 = (bf16[2,256,512]{2,1,0:T(8,128)(2,1)S(1)}, bf16[2,256,512]{2,1,0:T(8,128)(2,1)S(1)}) custom-call(s32[2]{0:T(128)S(1)} %bitcast.76, bf16[2,256,512]{2,1,0:T(8,128)(2,1)S(1)} %get-tuple-element.56.pin_ref, f32[2,256,512]{2,1,0:T(8,128)S(1)} %get-tuple-element.80.a_ref, f32[2,256,512]{2,1,0:T(8,128)} %get-tuple-element.79.u_ref, ...), custom_call_target="tpu_custom_call" | custom-call | tf_op jit(solution)/shard_map/pallas_call | solution.py:290
  170.5 13.9 %shard_map.139 = bf16[2,256,512]{2,1,0:T(8,128)(2,1)S(1)} custom-call(s32[2]{0:T(128)S(1)} %bitcast.77, bf16[2,256,512]{2,1,0:T(8,128)(2,1)S(1)} %get-tuple-element.57.pin_ref, f32[2,256,512]{2,1,0:T(8,128)S(1)} %get-tuple-element.80.a_ref, f32[2,256,512]{2,1,0:T(8,128)} %get-tuple-element.79.u_ref, bf16[512,256]{1,0:T(8,128)(2,1)S(1)} %fusion.1.osndt_ref, ...), custom_call_target="tpu_custom_call" | custom-call | tf_op jit(solution)/shard_map/pallas_call | solution.py:290
  184.5 1.9 %select_bitcast_fusion = bf16[1,2,256,512]{3,2,1,0:T(8,128)(2,1)} fusion(bf16[2,256,512]{2,1,0:T(8,128)(2,1)S(1)} %shard_map.139, bf16[2,256,512]{2,1,0:T(8,128)(2,1)} %copy-done.12, bf16[2,256,512]{2,1,0:T(8,128)(2,1)} %copy-done.11, bf16[2,256,512]{2,1,0:T(8,128)(2,1)S(1)} %get-tuple-element.60, pred[]{:T(512)S(6)} %eq.72, pred[]{:T(512)S(6)} %eq.71, ...), kind=kLoop, calls=%fused_computation.2 | loop fusion | flops 786432 | bytes 2621443 | tf_op jit(solution)/shard_map/broadcast_in_dim | solution.py:389
  (40 shorter events, 1.1 us)
Async XLA Ops:
  0.6 0.7 copy-start.17
  5.8 19.3 %copy-start.21 = (s32[2,128]{1,0:T(2,128)S(1)}, s32[2,128]{1,0:T(2,128)}, u32[]{:S(2)}) copy-start(s32[2,128]{1,0:T(2,128)} %param.22) | copy-start | bytes 3076
  5.8 19.5 %copy-start.22 = (s32[2]{0:T(128)S(1)}, s32[2]{0:T(128)}, u32[]{:S(2)}) copy-start(s32[2]{0:T(128)} %param.24) | copy-start | bytes 28
  5.8 19.5 %copy-start.20 = (s32[2,128]{1,0:T(2,128)S(1)}, s32[2,128]{1,0:T(2,128)}, u32[]{:S(2)}) copy-start(s32[2,128]{1,0:T(2,128)} %param.23) | copy-start | bytes 3076
  5.8 19.7 %copy-start.2 = (bf16[1,512,512]{2,1,0:T(8,128)(2,1)S(1)}, bf16[1,512,512]{2,1,0:T(8,128)(2,1)}, u32[]{:S(2)}) copy-start(bf16[1,512,512]{2,1,0:T(8,128)(2,1)} %param.18) | copy-start | bytes 1572868
  5.8 19.7 %copy-start.3 = (bf16[1,512,512]{2,1,0:T(8,128)(2,1)S(1)}, bf16[1,512,512]{2,1,0:T(8,128)(2,1)}, u32[]{:S(2)}) copy-start(bf16[1,512,512]{2,1,0:T(8,128)(2,1)} %param.19) | copy-start | bytes 1572868
  7.8 17.7 %copy-start = (bf16[1,512,512]{2,1,0:T(8,128)(2,1)S(1)}, bf16[1,512,512]{2,1,0:T(8,128)(2,1)}, u32[]{:S(2)}) copy-start(bf16[1,512,512]{2,1,0:T(8,128)(2,1)} %param.16) | copy-start | bytes 1572868
  7.8 17.7 %copy-start.1 = (bf16[1,512,512]{2,1,0:T(8,128)(2,1)S(1)}, bf16[1,512,512]{2,1,0:T(8,128)(2,1)}, u32[]{:S(2)}) copy-start(bf16[1,512,512]{2,1,0:T(8,128)(2,1)} %param.17) | copy-start | bytes 1572868
  25.5 0.7 copy-start.16
  26.2 1.0 copy-start.4
  27.2 1.0 copy-start.6
  28.3 0.9 copy-start.14
  29.2 0.9 copy-start.15
  53.4 0.8 copy-start.7
  73.1 0.8 copy-start.8
  99.1 0.8 copy-start.9
  104.8 0.8 copy-start.10
  105.6 2.2 %copy-start.18 = (f32[2,256,512]{2,1,0:T(8,128)S(1)}, f32[2,256,512]{2,1,0:T(8,128)}, u32[]{:S(2)}) copy-start(f32[2,256,512]{2,1,0:T(8,128)} %get-tuple-element.50) | copy-start | bytes 3145732
  105.6 2.2 %copy-start.19 = (f32[2,256,512]{2,1,0:T(8,128)S(1)}, f32[2,256,512]{2,1,0:T(8,128)}, u32[]{:S(2)}) copy-start(f32[2,256,512]{2,1,0:T(8,128)} %get-tuple-element.54) | copy-start | bytes 3145732
  107.8 3.9 %copy-start.5 = (bf16[1,512,512]{2,1,0:T(8,128)(2,1)S(1)}, bf16[1,512,512]{2,1,0:T(8,128)(2,1)}, u32[]{:S(2)}) copy-start(bf16[1,512,512]{2,1,0:T(8,128)(2,1)} %param.20) | copy-start | bytes 1572868
  107.9 3.9 %copy-start.13 = (bf16[2,256,512]{2,1,0:T(8,128)(2,1)S(1)}, bf16[2,256,512]{2,1,0:T(8,128)(2,1)}, u32[]{:S(2)}) copy-start(bf16[2,256,512]{2,1,0:T(8,128)(2,1)} %pin_ref.1) | copy-start | bytes 1572868
  148.7 0.8 copy-start.11
  170.5 13.9 %copy-start.12 = (bf16[2,256,512]{2,1,0:T(8,128)(2,1)}, bf16[2,256,512]{2,1,0:T(8,128)(2,1)S(1)}, u32[]{:S(2)}) copy-start(bf16[2,256,512]{2,1,0:T(8,128)(2,1)S(1)} %get-tuple-element.58) | copy-start | bytes 1572868

commit v5 on v4

--- a/solution.py
+++ b/solution.py
@@ -134,10 +134,25 @@
     )(*payloads)
 
 
-def fwd_tick_kernel(parts, sections, hs_ref, h_ref, fp_ref, fn_ref, osnd_ref, orcv_ref, orcvt_ref,
-                    ws_ref, wr_ref, wm_ref, wn_ref, wa_ref, g_ref,
-                    out_ref, a_ref, u_ref, hn_ref, fpn_ref, fnn_ref,
-                    hbuf, fpbuf, fnbuf, stage_n, stage_p, send_sem, recv_sem):
+def record_copies(pairs, sem, active):
+    def run():
+        copies = [pltpu.make_async_copy(buf, rec, sem.at[i]) for i, (buf, rec) in enumerate(pairs)]
+        for copy in copies:
+            copy.start()
+        for copy in copies:
+            copy.wait()
+    if active is None:
+        run()
+    else:
+        pl.when(active)(run)
+
+
+def fwd_tick_kernel(parts, sections, tick, hs_ref, h_ref, fp_ref, fn_ref, osnd_ref, orcv_ref, orcvt_ref,
+                    ws_ref, wr_ref, wm_ref, wn_ref, wa_ref, g_ref, *refs):
+    if tick > 0:
+        refs = refs[3:]
+    (orec, arec, urec, hn_ref, fpn_ref, fnn_ref, obuf, abuf, ubuf,
+     hbuf, fpbuf, fnbuf, stage_n, stage_p, send_sem, recv_sem, rec_sem) = refs
     micro, own, _ = h_ref.shape
     block = fp_ref.shape[1]
     d = lax.axis_index("dom")
@@ -150,17 +165,19 @@
     for src in (pipe_prev, dom_prev, dom_next):
         pl.semaphore_signal(barrier, 1, device_id=src, device_id_type=MESH_ID)
     compute_refs = (hs_ref, h_ref, fp_ref, fn_ref, osnd_ref, orcv_ref, orcvt_ref,
-                    ws_ref, wr_ref, wm_ref, wn_ref, wa_ref, g_ref, out_ref, a_ref, u_ref)
+                    ws_ref, wr_ref, wm_ref, wn_ref, wa_ref, g_ref, obuf, abuf, ubuf)
     pipe_copies = []
     for m in range(micro):
         fwd_micro(m, *compute_refs)
         if m == 0:
             pl.semaphore_wait(barrier, 3)
         copy = pltpu.make_async_remote_copy(
-            src_ref=out_ref.at[m], dst_ref=hbuf.at[m], send_sem=send_sem.at[0, m],
+            src_ref=obuf.at[m], dst_ref=hbuf.at[m], send_sem=send_sem.at[0, m],
             recv_sem=recv_sem.at[0, m], device_id=pipe_next, device_id_type=MESH_ID)
         copy.start()
         pipe_copies.append(copy)
+    record_copies(((obuf, orec), (abuf, arec), (ubuf, urec)), rec_sem,
+                  None if tick == 0 else p == tick)
     hs0 = hs_ref[0]
     hs1 = hs_ref[1]
     halo_copies = []
@@ -190,35 +207,78 @@
     fnn_ref[...] = fnbuf[...]
 
 
-def fwd_tick(operands, span, parts, sections):
+def fwd_tick(operands, records, tick, span, parts, sections):
     h = operands[1]
     micro, own, latent = h.shape
     vm = pl.BlockSpec(memory_space=pltpu.VMEM)
+    anyspec = pl.BlockSpec(memory_space=pl.ANY)
     bf = lambda rows: jax.ShapeDtypeStruct((micro, rows, latent), BF16)
     f32 = jax.ShapeDtypeStruct((micro, own, latent), F32)
+    n = len(operands)
+    extra = () if tick == 0 else tuple(records)
     return pl.pallas_call(
-        functools.partial(fwd_tick_kernel, parts, sections),
+        functools.partial(fwd_tick_kernel, parts, sections, tick),
         out_shape=(bf(own), f32, f32, bf(own), bf(span), bf(span)),
-        in_specs=[pl.BlockSpec(memory_space=pltpu.SMEM)] + [vm] * (len(operands) - 1),
-        out_specs=tuple(vm for _ in range(6)),
+        in_specs=[pl.BlockSpec(memory_space=pltpu.SMEM)] + [vm] * (n - 1) + [anyspec] * len(extra),
+        out_specs=(anyspec, anyspec, anyspec, vm, vm, vm),
         scratch_shapes=[pltpu.VMEM((micro, own, latent), BF16),
+                        pltpu.VMEM((micro, own, latent), F32),
+                        pltpu.VMEM((micro, own, latent), F32),
+                        pltpu.VMEM((micro, own, latent), BF16),
                         pltpu.VMEM((micro, span, latent), BF16),
                         pltpu.VMEM((micro, span, latent), BF16),
                         pltpu.VMEM((micro, span, latent), BF16),
                         pltpu.VMEM((micro, span, latent), BF16),
                         pltpu.SemaphoreType.DMA((3, micro)),
-                        pltpu.SemaphoreType.DMA((3, micro))],
-        compiler_params=pltpu.CompilerParams(collective_id=4, has_side_effects=True,
+                        pltpu.SemaphoreType.DMA((3, micro)),
+                        pltpu.SemaphoreType.DMA((3,))],
+        input_output_aliases={} if tick == 0 else {n: 0, n + 1: 1, n + 2: 2},
+        compiler_params=pltpu.CompilerParams(collective_id=10 + tick,
+                                             has_side_effects=True,
                                              vmem_limit_bytes=48 * 1024 * 1024),
-    )(*operands)
-
-
-def bwd_tick_kernel(parts, sections, send_pipe, hs_ref, pin_ref, a_ref, u_ref, osndt_ref, orcvl_ref,
+    )(*operands, *extra)
+
+
+def fwd_last_kernel(tick, hs_ref, h_ref, fp_ref, fn_ref, osnd_ref, orcv_ref, orcvt_ref,
+                    ws_ref, wr_ref, wm_ref, wn_ref, wa_ref, g_ref, orec_in, arec_in, urec_in,
+                    orec, arec, urec, obuf, abuf, ubuf, rec_sem):
+    compute_refs = (hs_ref, h_ref, fp_ref, fn_ref, osnd_ref, orcv_ref, orcvt_ref,
+                    ws_ref, wr_ref, wm_ref, wn_ref, wa_ref, g_ref, obuf, abuf, ubuf)
+    for m in range(h_ref.shape[0]):
+        fwd_micro(m, *compute_refs)
+    record_copies(((obuf, orec), (abuf, arec), (ubuf, urec)), rec_sem,
+                  lax.axis_index("pipe") == tick)
+
+
+def fwd_last(operands, records, tick):
+    h = operands[1]
+    micro, own, latent = h.shape
+    vm = pl.BlockSpec(memory_space=pltpu.VMEM)
+    anyspec = pl.BlockSpec(memory_space=pl.ANY)
+    n = len(operands)
+    return pl.pallas_call(
+        functools.partial(fwd_last_kernel, tick),
+        out_shape=tuple(jax.ShapeDtypeStruct(r.shape, r.dtype) for r in records),
+        in_specs=[pl.BlockSpec(memory_space=pltpu.SMEM)] + [vm] * (n - 1) + [anyspec] * 3,
+        out_specs=(anyspec, anyspec, anyspec),
+        scratch_shapes=[pltpu.VMEM((micro, own, latent), BF16),
+                        pltpu.VMEM((micro, own, latent), F32),
+                        pltpu.VMEM((micro, own, latent), F32),
+                        pltpu.SemaphoreType.DMA((3,))],
+        input_output_aliases={n: 0, n + 1: 1, n + 2: 2},
+        compiler_params=pltpu.CompilerParams(vmem_limit_bytes=48 * 1024 * 1024),
+    )(*operands, *records)
+
+
+def bwd_tick_kernel(parts, sections, tick, first, hs_ref, pin_ref, a_ref, u_ref, osndt_ref, orcvl_ref,
                     orcvt_ref, ws_ref, wr_ref, wm_ref, wn_ref, wa_ref, g_ref, *refs):
+    send_pipe = tick > 0
+    if not first:
+        refs = refs[1:]
     if send_pipe:
-        grad_ref, pinn_ref, p32, hg, snbuf, spbuf, gbuf, pinbuf, send_sem, recv_sem = refs
+        grec, pinn_ref, p32, hg, snbuf, spbuf, gbuf, pinbuf, send_sem, recv_sem, rec_sem = refs
     else:
-        grad_ref, p32, hg, snbuf, spbuf, gbuf, send_sem, recv_sem = refs
+        grec, p32, hg, snbuf, spbuf, gbuf, send_sem, recv_sem, rec_sem = refs
     micro, own, _ = pin_ref.shape
     block = snbuf.shape[1]
     d = lax.axis_index("dom")
@@ -265,37 +325,44 @@
                 recv_sem=recv_sem.at[2, m], device_id=pipe_prev, device_id_type=MESH_ID)
             copy.start()
             pipe_copies.append(copy)
+    record_copies(((gbuf, grec),), rec_sem, None if first else p == tick)
     for pair in halo_copies:
         for copy in pair:
             copy.wait_send()
     for copy in pipe_copies:
         copy.wait()
-    grad_ref[...] = gbuf[...]
     if send_pipe:
         pinn_ref[...] = pinbuf[...]
 
 
-def bwd_tick(operands, span, parts, sections, send_pipe):
+def bwd_tick(operands, grad_rec, tick, span, parts, sections):
     pin = operands[1]
     micro, own, latent = pin.shape
+    send_pipe = tick > 0
+    first = grad_rec is None
     vm = pl.BlockSpec(memory_space=pltpu.VMEM)
+    anyspec = pl.BlockSpec(memory_space=pl.ANY)
     grad = jax.ShapeDtypeStruct((micro, own, latent), BF16)
     scratch = [pltpu.VMEM((micro, own, latent), F32), pltpu.VMEM((micro, 2 * span, latent), BF16),
                pltpu.VMEM((micro, span, latent), BF16), pltpu.VMEM((micro, span, latent), BF16),
                pltpu.VMEM((micro, own, latent), BF16)]
     if send_pipe:
         scratch.append(pltpu.VMEM((micro, own, latent), BF16))
-    scratch += [pltpu.SemaphoreType.DMA((3, micro)), pltpu.SemaphoreType.DMA((3, micro))]
+    scratch += [pltpu.SemaphoreType.DMA((3, micro)), pltpu.SemaphoreType.DMA((3, micro)),
+                pltpu.SemaphoreType.DMA((1,))]
     outs = (grad, grad) if send_pipe else (grad,)
+    n = len(operands)
+    extra = () if first else (grad_rec,)
     return pl.pallas_call(
-        functools.partial(bwd_tick_kernel, parts, sections, send_pipe),
+        functools.partial(bwd_tick_kernel, parts, sections, tick, first),
         out_shape=outs,
-        in_specs=[pl.BlockSpec(memory_space=pltpu.SMEM)] + [vm] * (len(operands) - 1),
-        out_specs=tuple(vm for _ in outs),
+        in_specs=[pl.BlockSpec(memory_space=pltpu.SMEM)] + [vm] * (n - 1) + [anyspec] * len(extra),
+        out_specs=(anyspec,) + ((vm,) if send_pipe else ()),
         scratch_shapes=scratch,
-        compiler_params=pltpu.CompilerParams(collective_id=5 if send_pipe else 6, has_side_effects=True,
+        input_output_aliases={} if first else {n: 0},
+        compiler_params=pltpu.CompilerParams(collective_id=20 + tick, has_side_effects=True,
                                              vmem_limit_bytes=48 * 1024 * 1024),
-    )(*operands)
+    )(*operands, *extra)
 
 
 def vmem_call(kernel, out_shapes, n_in, smem_first=True):
@@ -361,31 +428,23 @@
     halo_fwd = [(0, None, span, 1, 0), (1, None, span, -1, 0)]
     from_prev, from_next = exchange(halo_fwd, (nxt0, prv0), D, S, 0)
     h = inputs
-    out_rec = a_rec = u_rec = None
+    records = None
     for t in range(S):
         operands = (hs, h, from_prev, from_next, osnd, orcv, orcvt, *weights, gain)
         if t < S - 1:
-            out, a, u, h, from_prev, from_next = fwd_tick(operands, span, D, S)
+            out_rec, a_rec, u_rec, h, from_prev, from_next = fwd_tick(operands, records, t, span, D, S)
         else:
-            out, a, u = fwd(*operands)
-        here = p_idx == t
-        if t == 0:
-            out_rec, a_rec, u_rec = out, a, u
-        else:
-            out_rec = jnp.where(here, out, out_rec)
-            a_rec = jnp.where(here, a, a_rec)
-            u_rec = jnp.where(here, u, u_rec)
+            out_rec, a_rec, u_rec = fwd_last(operands, records, t)
+        records = (out_rec, a_rec, u_rec)
 
     pin = cotangent
     grad_rec = None
     for t in range(S - 1, -1, -1):
         operands = (hs, pin, a_rec, u_rec, osndt, orcvl, orcvt, *weights, gain)
         if t > 0:
-            grad, pin = bwd_tick(operands, span, D, S, True)
+            grad_rec, pin = bwd_tick(operands, grad_rec, t, span, D, S)
         else:
-            (grad,) = bwd_tick(operands, span, D, S, False)
-        here = p_idx == t
-        grad_rec = grad if t == S - 1 else jnp.where(here, grad, grad_rec)
+            (grad_rec,) = bwd_tick(operands, grad_rec, t, span, D, S)
     return (out_rec[None], grad_rec[None])
 
 

time: 187 us -> 176 us (0.941)
  other arithmetic: 10.4 us -> 2.37 us
  Pallas kernels: 161 us -> 157 us
    pallas_call x8, Pallas kernels: 144 us -> 140 us  [the longest x4 71.7 us: bwd_tick(): pl.pallas_call(functools.partial(bwd_tick_kernel, parts, sections, tick,...]
    broadcast_in_dim x2 -> x0, other arithmetic: 4.18 us -> none  [shards(): return (out_rec[None], grad_rec[None])]
    select_n x1 -> x0, other arithmetic: 3.82 us -> none  [shards(): u_rec = jnp.where(here, u, u_rec)]
    unnamed x46 -> x36, local copies, waits for them, and re-layouts: 9.37 us -> 9.57 us
where the time goes in v5:
time: 176 us; the launch traced here: 175 us
  Pallas kernels  157 us (89%)
  local copies, waits for them, and re-layouts  10.9 us (6%)
  between operations  4.76 us (3%)
  other arithmetic  2.37 us (1%)
    pallas_call x4, Pallas kernels, bwd_tick(): pl.pallas_call(functools.partial(bwd_tick_kernel, parts, sections, tick,...  71.7 us
    pallas_call x3, Pallas kernels, fwd_tick(): pl.pallas_call(functools.partial(fwd_tick_kernel, parts, sections, tick),...  63.5 us
    pallas_call x1, Pallas kernels, exchange(): pl.pallas_call(functools.partial(comm_kernel, tuple(sends), len(payloads)...  17.3 us
    unnamed x36, local copies, waits for them, and re-layouts  9.57 us
    pallas_call x1, Pallas kernels, fwd_last(): pl.pallas_call(functools.partial(fwd_last_kernel, tick), out_shape=tuple(...  4.46 us

profile of v5, /device:TPU:4, one launch (start us, length us, event | category | flops | bytes accessed | tf_op | source)
XLA Modules:
  0.0 175.0 jit_solution(6928166891626018857)
XLA Ops:
  0.6 1.3 fusion.9
  5.9 2.0 %fusion.2 = (bf16[2,128,512]{2,1,0:T(8,128)(2,1)}, bf16[2,128,512]{2,1,0:T(8,128)(2,1)}) fusion(bf16[2,2,128,512]{3,2,1,0:T(8,128)(2,1)} %bitcast.69, s32[]{:T(128)S(6)} %select_n.15, pred[]{:T(512)S(6)} %and.24, s32[]{:T(128)S(6)} %select_n.13, pred[]{:T(512)S(6)} %and.23), kind=kLoop, calls=%fused_computation.5 | loop fusion | flops 262144 | bytes 1048586 | tf_op jit(solution)/shard_map/jit(_take)/select_n | solution.py:406
  7.9 17.3 %shard_map.131 = (bf16[2,128,512]{2,1,0:T(8,128)(2,1)}, bf16[2,128,512]{2,1,0:T(8,128)(2,1)}) custom-call(bf16[2,128,512]{2,1,0:T(8,128)(2,1)} %get-tuple-element.73.refs_0_, bf16[2,128,512]{2,1,0:T(8,128)(2,1)} %get-tuple-element.72.refs_1_), custom_call_target="tpu_custom_call" | custom-call | tf_op jit(solution)/shard_map/pallas_call | solution.py:127
  25.2 0.1 compare_bitcast_fusion
  25.3 0.2 fusion.6
  25.5 0.1 fusion.osnd_ref
  25.6 0.5 copy-done.12
  26.1 1.0 copy-done.7
  27.2 1.0 copy-done.8
  28.2 0.9 copy-done.10
  29.2 0.9 copy-done.11
  30.1 21.9 %shard_map.132 = (bf16[2,256,512]{2,1,0:T(8,128)(2,1)S(1)}, f32[2,256,512]{2,1,0:T(8,128)}, f32[2,256,512]{2,1,0:T(8,128)}, bf16[2,256,512]{2,1,0:T(8,128)(2,1)S...) custom-call(s32[2]{0:T(128)S(1)} %bitcast.70, bf16[2,256,512]{2,1,0:T(8,128)(2,1)S(1)} %copy-done.8, ...), custom_call_target="tpu_custom_call" | custom-call | tf_op jit(solution)/shard_map/pallas_call | solution.py:219
  52.1 17.7 %shard_map.133 = (bf16[2,256,512]{2,1,0:T(8,128)(2,1)S(1)}, f32[2,256,512]{2,1,0:T(8,128)}, f32[2,256,512]{2,1,0:T(8,128)}, bf16[2,256,512]{2,1,0:T(8,128)(2,1)S...) custom-call(s32[2]{0:T(128)S(1)} %bitcast.71, ...), custom_call_target="tpu_custom_call", output_to_operand_aliasing={{0}: (13, {}), {1}: (14, {}), {2}: (15, {})} | custom-call | tf_op jit(solution)/shard_map/pallas_call | solution.py:219
  69.7 23.9 %shard_map.134 = (bf16[2,256,512]{2,1,0:T(8,128)(2,1)S(1)}, f32[2,256,512]{2,1,0:T(8,128)}, f32[2,256,512]{2,1,0:T(8,128)}, bf16[2,256,512]{2,1,0:T(8,128)(2,1)S...) custom-call(s32[2]{0:T(128)S(1)} %bitcast.72, ...), custom_call_target="tpu_custom_call", output_to_operand_aliasing={{0}: (13, {}), {1}: (14, {}), {2}: (15, {})} | custom-call | tf_op jit(solution)/shard_map/pallas_call | solution.py:219
  93.6 1.2 copy-done
  94.9 4.5 %shard_map.135 = (bf16[2,256,512]{2,1,0:T(8,128)(2,1)S(1)}, f32[2,256,512]{2,1,0:T(8,128)S(1)}, f32[2,256,512]{2,1,0:T(8,128)}) custom-call(s32[2]{0:T(128)S(1)} %bitcast.73, bf16[2,256,512]{2,1,0:T(8,128)(2,1)S(1)} %get-tuple-element.46.h_ref, ...), custom_call_target="tpu_custom_call", output_to_operand_aliasing={{0}: (13, {}), {1}: (14, {}), {2}: (15, {})} | custom-call | tf_op jit(solution)/shard_map/pallas_call | solution.py:259
  99.3 1.0 copy-done.1
  100.4 1.2 copy-done.2
  101.6 18.4 %shard_map.136 = (bf16[2,256,512]{2,1,0:T(8,128)(2,1)S(1)}, bf16[2,256,512]{2,1,0:T(8,128)(2,1)S(1)}) custom-call(s32[2]{0:T(128)S(1)} %bitcast.74, bf16[2,256,512]{2,1,0:T(8,128)(2,1)S(1)} %copy-done.9, f32[2,256,512]{2,1,0:T(8,128)S(1)} %copy-done.2, f32[2,256,512]{2,1,0:T(8,128)} %get-tuple-element.54.u_ref, bf16[512,256]{1,0:T(8,128)(2,1)S(1)} %fusion.1.osndt_ref, ...), custom_call_target="tpu_custom_call" | custom-call | tf_op jit(solution)/shard_map/pallas_call | solution.py:356
  120.0 20.2 %shard_map.137 = (bf16[2,256,512]{2,1,0:T(8,128)(2,1)S(1)}, bf16[2,256,512]{2,1,0:T(8,128)(2,1)S(1)}) custom-call(s32[2]{0:T(128)S(1)} %bitcast.75, bf16[2,256,512]{2,1,0:T(8,128)(2,1)S(1)} %get-tuple-element.55.pin_ref, f32[2,256,512]{2,1,0:T(8,128)S(1)} %copy-done.2, f32[2,256,512]{2,1,0:T(8,128)} %get-tuple-element.54.u_ref, ...), custom_call_target="tpu_custom_call", output_to_operand_aliasing={{0}: (13, {})} | custom-call | tf_op jit(solution)/shard_map/pallas_call | solution.py:356
  140.3 19.4 %shard_map.138 = (bf16[2,256,512]{2,1,0:T(8,128)(2,1)S(1)}, bf16[2,256,512]{2,1,0:T(8,128)(2,1)S(1)}) custom-call(s32[2]{0:T(128)S(1)} %bitcast.76, bf16[2,256,512]{2,1,0:T(8,128)(2,1)S(1)} %get-tuple-element.57.pin_ref, f32[2,256,512]{2,1,0:T(8,128)S(1)} %copy-done.2, f32[2,256,512]{2,1,0:T(8,128)} %get-tuple-element.54.u_ref, ...), custom_call_target="tpu_custom_call", output_to_operand_aliasing={{0}: (13, {})} | custom-call | tf_op jit(solution)/shard_map/pallas_call | solution.py:356
  159.7 13.7 %shard_map.139 = bf16[2,256,512]{2,1,0:T(8,128)(2,1)S(1)} custom-call(s32[2]{0:T(128)S(1)} %bitcast.77, bf16[2,256,512]{2,1,0:T(8,128)(2,1)S(1)} %get-tuple-element.59.pin_ref, f32[2,256,512]{2,1,0:T(8,128)S(1)} %copy-done.2, f32[2,256,512]{2,1,0:T(8,128)} %get-tuple-element.54.u_ref, ...), custom_call_target="tpu_custom_call", output_to_operand_aliasing={{}: (13, {})} | custom-call | tf_op jit(solution)/shard_map/pallas_call | solution.py:356
  173.4 0.8 copy.44
  174.2 0.8 copy.45
  (27 shorter events, 0.1 us)
Async XLA Ops:
  5.8 19.3 %copy-start.16 = (s32[2]{0:T(128)S(1)}, s32[2]{0:T(128)}, u32[]{:S(2)}) copy-start(s32[2]{0:T(128)} %param.24) | copy-start | bytes 28
  5.8 19.4 %copy-start.14 = (s32[2,128]{1,0:T(2,128)S(1)}, s32[2,128]{1,0:T(2,128)}, u32[]{:S(2)}) copy-start(s32[2,128]{1,0:T(2,128)} %param.23) | copy-start | bytes 3076
  5.9 19.6 %copy-start.15 = (s32[2,128]{1,0:T(2,128)S(1)}, s32[2,128]{1,0:T(2,128)}, u32[]{:S(2)}) copy-start(s32[2,128]{1,0:T(2,128)} %param.22) | copy-start | bytes 3076
  5.9 19.7 %copy-start.5 = (bf16[1,512,512]{2,1,0:T(8,128)(2,1)S(1)}, bf16[1,512,512]{2,1,0:T(8,128)(2,1)}, u32[]{:S(2)}) copy-start(bf16[1,512,512]{2,1,0:T(8,128)(2,1)} %param.18) | copy-start | bytes 1572868
  5.9 19.7 %copy-start.6 = (bf16[1,512,512]{2,1,0:T(8,128)(2,1)S(1)}, bf16[1,512,512]{2,1,0:T(8,128)(2,1)}, u32[]{:S(2)}) copy-start(bf16[1,512,512]{2,1,0:T(8,128)(2,1)} %param.19) | copy-start | bytes 1572868
  7.9 17.7 %copy-start.3 = (bf16[1,512,512]{2,1,0:T(8,128)(2,1)S(1)}, bf16[1,512,512]{2,1,0:T(8,128)(2,1)}, u32[]{:S(2)}) copy-start(bf16[1,512,512]{2,1,0:T(8,128)(2,1)} %param.16) | copy-start | bytes 1572868
  7.9 17.8 %copy-start.4 = (bf16[1,512,512]{2,1,0:T(8,128)(2,1)S(1)}, bf16[1,512,512]{2,1,0:T(8,128)(2,1)}, u32[]{:S(2)}) copy-start(bf16[1,512,512]{2,1,0:T(8,128)(2,1)} %param.17) | copy-start | bytes 1572868
  25.4 0.7 copy-start.12
  25.5 0.7 copy-start.13
  26.1 1.0 copy-start.7
  27.2 1.0 copy-start.8
  28.2 0.9 copy-start.10
  29.2 0.9 copy-start.11
  93.6 1.2 copy-start
  94.9 5.6 %copy-start.9 = (bf16[2,256,512]{2,1,0:T(8,128)(2,1)S(1)}, bf16[2,256,512]{2,1,0:T(8,128)(2,1)}, u32[]{:S(2)}) copy-start(bf16[2,256,512]{2,1,0:T(8,128)(2,1)} %pin_ref.1) | copy-start | bytes 1572868
  99.3 1.0 copy-start.1
  100.4 1.2 copy-start.2

commit v6 on v5

--- a/solution.py
+++ b/solution.py
@@ -376,6 +376,126 @@
     )
 
 
+def whole_kernel(parts, sections, hs_ref, x_ref, cot_ref, osnd_ref, orcv_ref, orcvt_ref, osndt_ref,
+                 orcvl_ref, ws_ref, wr_ref, wm_ref, wn_ref, wa_ref, g_ref,
+                 out_ref, grad_ref,
+                 hbuf, fpbuf, fnbuf, stage_n, stage_p, abuf, ubuf, cbuf, p32, hg, snbuf, spbuf,
+                 fsend, frecv, bsend, brecv):
+    micro, own, _ = x_ref.shape
+    block = fpbuf.shape[1]
+    d = lax.axis_index("dom")
+    p = lax.axis_index("pipe")
+    pipe_next = (d, lax.rem(p + 1, sections))
+    pipe_prev = (d, lax.rem(p - 1 + sections, sections))
+    dom_next = (lax.rem(d + 1, parts), p)
+    dom_prev = (lax.rem(d - 1 + parts, parts), p)
+    barrier = pltpu.get_barrier_semaphore()
+    for nb in (pipe_prev, pipe_next, dom_prev, dom_next):
+        pl.semaphore_signal(barrier, 1, device_id=nb, device_id_type=MESH_ID)
+    pl.semaphore_wait(barrier, 4)
+    hs0 = hs_ref[0]
+    hs1 = hs_ref[1]
+    has_prev = p > 0
+    has_next = p < sections - 1
+
+    def remote(src, dst, sems, idx, target):
+        send_sem, recv_sem = sems
+        return pltpu.make_async_remote_copy(
+            src_ref=src, dst_ref=dst, send_sem=send_sem.at[idx], recv_sem=recv_sem.at[idx],
+            device_id=target, device_id_type=MESH_ID)
+
+    fwd_refs = (hs_ref, hbuf, fpbuf, fnbuf, osnd_ref, orcv_ref, orcvt_ref,
+                ws_ref, wr_ref, wm_ref, wn_ref, wa_ref, g_ref, out_ref, abuf, ubuf)
+    fwd_pipe = []
+    fwd_halo = []
+    for m in range(micro):
+        pipe_in = remote(out_ref.at[m], hbuf.at[m], (fsend, frecv), m, pipe_next)
+        pl.when(has_prev)(pipe_in.wait_recv)
+
+        @pl.when(p == 0)
+        def _():
+            hbuf[m] = x_ref[m]
+
+        h = hbuf[m]
+        sel_n = h[0:block]
+        sel_p = h[0:block]
+        for b in range(1, own // block):
+            piece = h[b * block:(b + 1) * block]
+            sel_n = jnp.where(hs0 == b, piece, sel_n)
+            sel_p = jnp.where(hs1 == b, piece, sel_p)
+        stage_n[m] = sel_n
+        stage_p[m] = sel_p
+        pair = [remote(stage_n.at[m], fpbuf.at[m], (fsend, frecv), micro + 2 * m, dom_next),
+                remote(stage_p.at[m], fnbuf.at[m], (fsend, frecv), micro + 2 * m + 1, dom_prev)]
+        for copy in pair:
+            copy.start()
+        for copy in pair:
+            copy.wait_recv()
+        fwd_halo.extend(pair)
+        fwd_micro(m, *fwd_refs)
+        pl.when(has_next)(pipe_in.start)
+        fwd_pipe.append(pipe_in)
+
+    bwd_refs = (cbuf, abuf, ubuf, osndt_ref, orcvl_ref, orcvt_ref,
+                ws_ref, wr_ref, wm_ref, wn_ref, wa_ref, g_ref, p32, hg)
+    bwd_pipe = []
+    bwd_halo = []
+    for m in range(micro):
+        pipe_in = remote(grad_ref.at[m], cbuf.at[m], (bsend, brecv), m, pipe_prev)
+        pl.when(has_next)(pipe_in.wait_recv)
+
+        @pl.when(p == sections - 1)
+        def _():
+            cbuf[m] = cot_ref[m]
+
+        bwd_micro(m, *bwd_refs)
+        pair = [remote(hg.at[m, pl.ds(0, block)], snbuf.at[m], (bsend, brecv), micro + 2 * m, dom_prev),
+                remote(hg.at[m, pl.ds(block, block)], spbuf.at[m], (bsend, brecv), micro + 2 * m + 1,
+                       dom_next)]
+        for copy in pair:
+            copy.start()
+        for copy in pair:
+            copy.wait_recv()
+        bwd_halo.extend(pair)
+        sn = snbuf[m].astype(F32)
+        sp = spbuf[m].astype(F32)
+        for b in range(own // block):
+            piece = p32[m, b * block:(b + 1) * block]
+            piece = piece + jnp.where(hs0 == b, sn, 0.0) + jnp.where(hs1 == b, sp, 0.0)
+            grad_ref[m, b * block:(b + 1) * block] = piece.astype(grad_ref.dtype)
+        pl.when(has_prev)(pipe_in.start)
+        bwd_pipe.append(pipe_in)
+
+    for copy in fwd_pipe:
+        pl.when(has_next)(copy.wait_send)
+    for copy in bwd_pipe:
+        pl.when(has_prev)(copy.wait_send)
+    for copy in fwd_halo + bwd_halo:
+        copy.wait_send()
+
+
+def whole(operands, span, parts, sections):
+    x = operands[1]
+    micro, own, latent = x.shape
+    vm = pl.BlockSpec(memory_space=pltpu.VMEM)
+    bf = lambda rows: pltpu.VMEM((micro, rows, latent), BF16)
+    f32 = pltpu.VMEM((micro, own, latent), F32)
+    n = 2 * micro + micro * 2
+    return pl.pallas_call(
+        functools.partial(whole_kernel, parts, sections),
+        out_shape=(jax.ShapeDtypeStruct((micro, own, latent), BF16),
+                   jax.ShapeDtypeStruct((micro, own, latent), BF16)),
+        in_specs=[pl.BlockSpec(memory_space=pltpu.SMEM)] + [vm] * (len(operands) - 1),
+        out_specs=(vm, vm),
+        scratch_shapes=[bf(own), bf(span), bf(span), bf(span), bf(span), f32, f32, bf(own), f32,
+                        bf(2 * span), bf(span), bf(span),
+                        pltpu.SemaphoreType.DMA((3 * micro,)), pltpu.SemaphoreType.DMA((3 * micro,)),
+                        pltpu.SemaphoreType.DMA((3 * micro,)), pltpu.SemaphoreType.DMA((3 * micro,))],
+        compiler_params=pltpu.CompilerParams(collective_id=0, has_side_effects=True,
+                                             vmem_limit_bytes=48 * 1024 * 1024),
+    )(*operands)
+
+
 def shards(inputs, cotangent, w_send, w_recv, w_message, w_node, w_aggregate, gains,
            edge_send, edge_recv, edge_count, halo_send):
     sections = lax.axis_size("pipe")
@@ -424,27 +544,8 @@
          jax.ShapeDtypeStruct((micro, own, latent), F32)),
         13)
 
-    nxt0, prv0 = blocks_of(inputs)
-    halo_fwd = [(0, None, span, 1, 0), (1, None, span, -1, 0)]
-    from_prev, from_next = exchange(halo_fwd, (nxt0, prv0), D, S, 0)
-    h = inputs
-    records = None
-    for t in range(S):
-        operands = (hs, h, from_prev, from_next, osnd, orcv, orcvt, *weights, gain)
-        if t < S - 1:
-            out_rec, a_rec, u_rec, h, from_prev, from_next = fwd_tick(operands, records, t, span, D, S)
-        else:
-            out_rec, a_rec, u_rec = fwd_last(operands, records, t)
-        records = (out_rec, a_rec, u_rec)
-
-    pin = cotangent
-    grad_rec = None
-    for t in range(S - 1, -1, -1):
-        operands = (hs, pin, a_rec, u_rec, osndt, orcvl, orcvt, *weights, gain)
-        if t > 0:
-            grad_rec, pin = bwd_tick(operands, grad_rec, t, span, D, S)
-        else:
-            (grad_rec,) = bwd_tick(operands, grad_rec, t, span, D, S)
+    out_rec, grad_rec = whole(
+        (hs, inputs, cotangent, osnd, orcv, orcvt, osndt, orcvl, *weights, gain), span, D, S)
     return (out_rec[None], grad_rec[None])
 
 

time: 176 us -> 129 us (0.73)
  the two profiles are of different devices: /device:TPU:4 before, /device:TPU:1 now
where the time goes in v6:
time: 129 us; the launch traced here: 128 us
  Pallas kernels  116 us (90%)
  local copies, waits for them, and re-layouts  8.51 us (7%)
  other arithmetic  2.49 us (2%)
    pallas_call x1, Pallas kernels, whole(): pl.pallas_call(functools.partial(whole_kernel, parts, sections), out_shap...  116 us
    unnamed x22, local copies, waits for them, and re-layouts  8.51 us

profile of v6, /device:TPU:1, one launch (start us, length us, event | category | flops | bytes accessed | tf_op | source)
XLA Modules:
  0.0 128.1 jit_solution(10897165990002693547)
XLA Ops:
  0.6 0.0 copy-start
  0.6 0.8 compare_bitcast_fusion
  1.4 0.7 fusion.1.osndt_ref
  2.2 0.0 copy-start.9
  2.2 0.8 fusion.osnd_ref
  3.0 0.0 copy-done.9
  3.0 0.2 fusion.4
  3.2 0.0 copy-start.7
  3.2 0.0 copy-start.8
  3.2 0.0 copy-done
  3.2 0.7 copy-done.7
  3.9 0.0 copy-done.8
  3.9 0.0 copy-start.1
  3.9 1.0 copy-done.1
  4.9 0.0 copy-start.2
  4.9 1.0 copy-done.2
  5.9 0.0 copy-start.3
  5.9 1.0 copy-done.3
  7.0 1.0 copy-done.4
  8.0 1.0 copy-done.5
  9.1 1.0 copy-done.6
  10.1 116.4 %shard_map.131 = (bf16[2,256,512]{2,1,0:T(8,128)(2,1)S(1)}, bf16[2,256,512]{2,1,0:T(8,128)(2,1)S(1)}) custom-call(s32[2]{0:T(128)S(1)} %bitcast.19, bf16[2,256,512]{2,1,0:T(8,128)(2,1)S(1)} %copy-done, bf16[2,256,512]{2,1,0:T(8,128)(2,1)S(1)} %copy-done.1, bf16[256,512]{1,0:T(8,128)(2,1)S(1)} %fusion.osnd_ref, ...), custom_call_target="tpu_custom_call" | custom-call | tf_op jit(solution)/shard_map/pallas_call | solution.py:484
  126.5 0.8 copy.16
  127.3 0.8 copy.17
  (3 shorter events, 0.0 us)
Async XLA Ops:
  0.6 2.6 %copy-start = (bf16[2,256,512]{2,1,0:T(8,128)(2,1)S(1)}, bf16[2,256,512]{2,1,0:T(8,128)(2,1)}, u32[]{:S(2)}) copy-start(bf16[2,256,512]{2,1,0:T(8,128)(2,1)} %x_ref.1) | copy-start | bytes 1572868
  2.2 0.8 copy-start.9
  3.2 0.7 copy-start.7
  3.2 0.7 copy-start.8
  3.9 1.0 copy-start.1
  4.9 1.0 copy-start.2
  5.9 1.0 copy-start.3
  7.0 1.0 copy-start.4
  8.0 1.0 copy-start.5
  9.1 1.0 copy-start.6

commit v7 on v6

--- a/solution.py
+++ b/solution.py
@@ -376,13 +376,21 @@
     )
 
 
-def whole_kernel(parts, sections, hs_ref, x_ref, cot_ref, osnd_ref, orcv_ref, orcvt_ref, osndt_ref,
-                 orcvl_ref, ws_ref, wr_ref, wm_ref, wn_ref, wa_ref, g_ref,
+def whole_kernel(parts, sections, hs_ref, x_hbm, cot_hbm, osnd_ref, orcv_ref, orcvt_ref, osndt_ref,
+                 orcvl_ref, ws_hbm, wr_hbm, wm_hbm, wn_hbm, wa_hbm, g_ref,
                  out_ref, grad_ref,
+                 xbuf, cotbuf, wbuf,
                  hbuf, fpbuf, fnbuf, stage_n, stage_p, abuf, ubuf, cbuf, p32, hg, snbuf, spbuf,
-                 fsend, frecv, bsend, brecv):
-    micro, own, _ = x_ref.shape
+                 fsend, frecv, bsend, brecv, lsem):
+    micro, own, latent = xbuf.shape
     block = fpbuf.shape[1]
+    span = block
+    loads = [pltpu.make_async_copy(x_hbm, xbuf, lsem.at[0])]
+    for i, w in enumerate((ws_hbm, wr_hbm, wm_hbm, wn_hbm, wa_hbm)):
+        loads.append(pltpu.make_async_copy(w, wbuf.at[i], lsem.at[1 + i]))
+    loads.append(pltpu.make_async_copy(cot_hbm, cotbuf, lsem.at[6]))
+    for copy in loads:
+        copy.start()
     d = lax.axis_index("dom")
     p = lax.axis_index("pipe")
     pipe_next = (d, lax.rem(p + 1, sections))
@@ -397,6 +405,8 @@
     hs1 = hs_ref[1]
     has_prev = p > 0
     has_next = p < sections - 1
+    gain = g_ref[...]
+    ws, wr, wm, wn, wa = (wbuf.at[i] for i in range(5))
 
     def remote(src, dst, sems, idx, target):
         send_sem, recv_sem = sems
@@ -404,8 +414,7 @@
             src_ref=src, dst_ref=dst, send_sem=send_sem.at[idx], recv_sem=recv_sem.at[idx],
             device_id=target, device_id_type=MESH_ID)
 
-    fwd_refs = (hs_ref, hbuf, fpbuf, fnbuf, osnd_ref, orcv_ref, orcvt_ref,
-                ws_ref, wr_ref, wm_ref, wn_ref, wa_ref, g_ref, out_ref, abuf, ubuf)
+    loads[0].wait()
     fwd_pipe = []
     fwd_halo = []
     for m in range(micro):
@@ -414,7 +423,7 @@
 
         @pl.when(p == 0)
         def _():
-            hbuf[m] = x_ref[m]
+            hbuf[m] = xbuf[m]
 
         h = hbuf[m]
         sel_n = h[0:block]
@@ -429,15 +438,37 @@
                 remote(stage_p.at[m], fnbuf.at[m], (fsend, frecv), micro + 2 * m + 1, dom_prev)]
         for copy in pair:
             copy.start()
+        if m == 0:
+            for copy in loads[1:6]:
+                copy.wait()
+        osnd = osnd_ref[...]
+        own_gather = mm(osnd[:, :own], h)
+        recv_rows = mm(orcv_ref[...], h).astype(BF16)
+        recv_part = mm(recv_rows, wr[...])
+        node_part = mm(h, wn[...])
         for copy in pair:
             copy.wait_recv()
         fwd_halo.extend(pair)
-        fwd_micro(m, *fwd_refs)
+        gathered = (own_gather + mm(osnd[:, own:own + span], fpbuf[m])
+                    + mm(osnd[:, own + span:], fnbuf[m])).astype(BF16)
+        send_part = mm(gathered, ws[...]).astype(BF16).astype(F32)
+        pre = send_part + recv_part
+        abuf[m] = pre
+        edge_hidden = (pre * sigmoid(pre)).astype(BF16)
+        messages = mm(edge_hidden, wm[...])
+        agg = split_sum(orcvt_ref[...], messages).astype(BF16)
+        node_pre = node_part + mm(agg, wa[...])
+        ubuf[m] = node_pre
+        act = node_pre * sigmoid(node_pre)
+        mean = jnp.mean(act, axis=-1, keepdims=True)
+        cen = act - mean
+        var = jnp.mean(cen * cen, axis=-1, keepdims=True)
+        unit = cen * lax.rsqrt(var + EPSILON)
+        out_ref[m] = (h.astype(F32) + unit * gain).astype(BF16)
         pl.when(has_next)(pipe_in.start)
         fwd_pipe.append(pipe_in)
 
-    bwd_refs = (cbuf, abuf, ubuf, osndt_ref, orcvl_ref, orcvt_ref,
-                ws_ref, wr_ref, wm_ref, wn_ref, wa_ref, g_ref, p32, hg)
+    loads[6].wait()
     bwd_pipe = []
     bwd_halo = []
     for m in range(micro):
@@ -446,14 +477,37 @@
 
         @pl.when(p == sections - 1)
         def _():
-            cbuf[m] = cot_ref[m]
-
-        bwd_micro(m, *bwd_refs)
+            cbuf[m] = cotbuf[m]
+
+        c = cbuf[m].astype(F32)
+        node_pre = ubuf[m]
+        sig_u = sigmoid(node_pre)
+        act = node_pre * sig_u
+        mean = jnp.mean(act, axis=-1, keepdims=True)
+        cen = act - mean
+        var = jnp.mean(cen * cen, axis=-1, keepdims=True)
+        rs = lax.rsqrt(var + EPSILON)
+        unit = cen * rs
+        gu = c * gain
+        gact = rs * (gu - jnp.mean(gu, axis=-1, keepdims=True)
+                     - unit * jnp.mean(gu * unit, axis=-1, keepdims=True))
+        du = (gact * (sig_u * (1.0 + node_pre * (1.0 - sig_u)))).astype(BF16)
+        dagg = mm_t(du, wa[...]).astype(BF16)
+        gmsg = mm(orcvl_ref[...], dagg).astype(BF16)
+        pre = abuf[m]
+        sig_a = sigmoid(pre)
+        dedge = (mm_t(gmsg, wm[...]) * (sig_a * (1.0 + pre * (1.0 - sig_a)))).astype(BF16)
+        send_x = mm_t(dedge, ws[...])
+        osndt = osndt_ref[...]
+        hg[m] = split_sum(osndt[own:], send_x).astype(BF16)
         pair = [remote(hg.at[m, pl.ds(0, block)], snbuf.at[m], (bsend, brecv), micro + 2 * m, dom_prev),
                 remote(hg.at[m, pl.ds(block, block)], spbuf.at[m], (bsend, brecv), micro + 2 * m + 1,
                        dom_next)]
         for copy in pair:
             copy.start()
+        rows = c + mm_t(du, wn[...])
+        rows = rows + split_sum(orcvt_ref[...], mm_t(dedge, wr[...]))
+        p32[m] = rows + split_sum(osndt[:own], send_x)
         for copy in pair:
             copy.wait_recv()
         bwd_halo.extend(pair)
@@ -478,19 +532,22 @@
     x = operands[1]
     micro, own, latent = x.shape
     vm = pl.BlockSpec(memory_space=pltpu.VMEM)
+    anyspec = pl.BlockSpec(memory_space=pl.ANY)
     bf = lambda rows: pltpu.VMEM((micro, rows, latent), BF16)
     f32 = pltpu.VMEM((micro, own, latent), F32)
-    n = 2 * micro + micro * 2
+    in_specs = [pl.BlockSpec(memory_space=pltpu.SMEM), anyspec, anyspec] + [vm] * 5 + [anyspec] * 5 + [vm]
     return pl.pallas_call(
         functools.partial(whole_kernel, parts, sections),
         out_shape=(jax.ShapeDtypeStruct((micro, own, latent), BF16),
                    jax.ShapeDtypeStruct((micro, own, latent), BF16)),
-        in_specs=[pl.BlockSpec(memory_space=pltpu.SMEM)] + [vm] * (len(operands) - 1),
+        in_specs=in_specs,
         out_specs=(vm, vm),
-        scratch_shapes=[bf(own), bf(span), bf(span), bf(span), bf(span), f32, f32, bf(own), f32,
+        scratch_shapes=[bf(own), bf(own), pltpu.VMEM((5, latent, latent), BF16),
+                        bf(own), bf(span), bf(span), bf(span), bf(span), f32, f32, bf(own), f32,
                         bf(2 * span), bf(span), bf(span),
                         pltpu.SemaphoreType.DMA((3 * micro,)), pltpu.SemaphoreType.DMA((3 * micro,)),
-                        pltpu.SemaphoreType.DMA((3 * micro,)), pltpu.SemaphoreType.DMA((3 * micro,))],
+                        pltpu.SemaphoreType.DMA((3 * micro,)), pltpu.SemaphoreType.DMA((3 * micro,)),
+                        pltpu.SemaphoreType.DMA((7,))],
         compiler_params=pltpu.CompilerParams(collective_id=0, has_side_effects=True,
                                              vmem_limit_bytes=48 * 1024 * 1024),
     )(*operands)

time: 129 us -> 125 us (0.969)
  Pallas kernels: 116 us -> 113 us
    pallas_call x1, Pallas kernels: 116 us -> 113 us  [whole(): pl.pallas_call(functools.partial(whole_kernel, parts, sections), out_shap...]
where the time goes in v7:
time: 125 us
  Pallas kernels  113 us (90%)
  local copies, waits for them, and re-layouts  8.51 us (7%)
  other arithmetic  2.49 us (2%)
    pallas_call x1, Pallas kernels, whole(): pl.pallas_call(functools.partial(whole_kernel, parts, sections), out_shap...  113 us
    unnamed x22, local copies, waits for them, and re-layouts  8.51 us

profile of v7, /device:TPU:1, one launch (start us, length us, event | category | flops | bytes accessed | tf_op | source)
XLA Modules:
  0.0 124.5 jit_solution(8497686716355351874)
XLA Ops:
  0.6 0.0 copy-start
  0.6 0.8 compare_bitcast_fusion
  1.4 0.7 fusion.1.osndt_ref
  2.2 0.0 copy-start.9
  2.2 0.8 fusion.osnd_ref
  3.0 0.0 copy-done.9
  3.0 0.2 fusion.4
  3.2 0.0 copy-start.7
  3.2 0.0 copy-start.8
  3.2 0.0 copy-done
  3.2 0.7 copy-done.7
  3.9 0.0 copy-done.8
  3.9 0.0 copy-start.1
  3.9 1.0 copy-done.1
  4.9 0.0 copy-start.2
  4.9 1.0 copy-done.2
  5.9 0.0 copy-start.3
  5.9 1.0 copy-done.3
  7.0 1.0 copy-done.4
  8.0 1.0 copy-done.5
  9.1 1.0 copy-done.6
  10.1 112.8 %shard_map.131 = (bf16[2,256,512]{2,1,0:T(8,128)(2,1)S(1)}, bf16[2,256,512]{2,1,0:T(8,128)(2,1)S(1)}) custom-call(s32[2]{0:T(128)S(1)} %bitcast.19, bf16[2,256,512]{2,1,0:T(8,128)(2,1)S(1)} %copy-done, bf16[2,256,512]{2,1,0:T(8,128)(2,1)S(1)} %copy-done.1, bf16[256,512]{1,0:T(8,128)(2,1)S(1)} %fusion.osnd_ref, ...), custom_call_target="tpu_custom_call" | custom-call | tf_op jit(solution)/shard_map/pallas_call | solution.py:539
  122.9 0.8 copy.16
  123.7 0.8 copy.17
  (3 shorter events, 0.0 us)
Async XLA Ops:
  0.6 2.6 %copy-start = (bf16[2,256,512]{2,1,0:T(8,128)(2,1)S(1)}, bf16[2,256,512]{2,1,0:T(8,128)(2,1)}, u32[]{:S(2)}) copy-start(bf16[2,256,512]{2,1,0:T(8,128)(2,1)} %x_hbm.1) | copy-start | bytes 1572868
  2.2 0.8 copy-start.9
  3.2 0.7 copy-start.7
  3.2 0.7 copy-start.8
  3.9 1.0 copy-start.1
  4.9 1.0 copy-start.2
  5.9 1.0 copy-start.3
  7.0 1.0 copy-start.4
  8.0 1.0 copy-start.5
  9.1 1.0 copy-start.6

commit v8 on v7

--- a/solution.py
+++ b/solution.py
@@ -532,7 +532,7 @@
     x = operands[1]
     micro, own, latent = x.shape
     vm = pl.BlockSpec(memory_space=pltpu.VMEM)
-    anyspec = pl.BlockSpec(memory_space=pl.ANY)
+    anyspec = pl.BlockSpec(memory_space=pltpu.HBM)
     bf = lambda rows: pltpu.VMEM((micro, rows, latent), BF16)
     f32 = pltpu.VMEM((micro, own, latent), F32)
     in_specs = [pl.BlockSpec(memory_space=pltpu.SMEM), anyspec, anyspec] + [vm] * 5 + [anyspec] * 5 + [vm]
@@ -549,7 +549,7 @@
                         pltpu.SemaphoreType.DMA((3 * micro,)), pltpu.SemaphoreType.DMA((3 * micro,)),
                         pltpu.SemaphoreType.DMA((7,))],
         compiler_params=pltpu.CompilerParams(collective_id=0, has_side_effects=True,
-                                             vmem_limit_bytes=48 * 1024 * 1024),
+                                             vmem_limit_bytes=67043328),
     )(*operands)
 
 

time: 125 us -> 121 us (0.968)
  local copies, waits for them, and re-layouts: 8.51 us -> 3.98 us
    unnamed x22 -> x10, local copies, waits for them, and re-layouts: 8.51 us -> 3.98 us
where the time goes in v8:
time: 121 us
  Pallas kernels  114 us (94%)
  local copies, waits for them, and re-layouts  3.98 us (3%)
  other arithmetic  2.56 us (2%)
    pallas_call x1, Pallas kernels, whole(): pl.pallas_call(functools.partial(whole_kernel, parts, sections), out_shap...  114 us
    unnamed x10, local copies, waits for them, and re-layouts  3.98 us

profile of v8, /device:TPU:1, one launch (start us, length us, event | category | flops | bytes accessed | tf_op | source)
XLA Modules:
  0.0 121.2 jit_solution(9697608235048139625)
XLA Ops:
  0.6 0.0 copy-start.3
  0.6 0.6 copy-done.3
  1.3 0.0 copy-start.1
  1.3 0.1 compare_bitcast_fusion
  1.4 0.6 copy-done.1
  2.0 0.8 fusion.1.osndt_ref
  2.7 0.0 copy-start.2
  2.7 0.8 fusion.osnd_ref
  3.6 0.0 copy-done.2
  3.6 0.9 fusion.4
  4.5 114.0 %shard_map.131 = (bf16[2,256,512]{2,1,0:T(8,128)(2,1)}, bf16[2,256,512]{2,1,0:T(8,128)(2,1)}) custom-call(s32[2]{0:T(128)} %bitcast.22, bf16[2,256,512]{2,1,0:T(8,128)(2,1)} %x_hbm.1, bf16[2,256,512]{2,1,0:T(8,128)(2,1)} %cot_hbm.1, bf16[256,512]{1,0:T(8,128)(2,1)} %fusion.osnd_ref, bf16[256,256]{1,0:T(8,128)(2,1)} %get-tuple-element.8.orcv_ref, ...), custom_call_target="tpu_custom_call" | custom-call | tf_op jit(solution)/shard_map/pallas_call | solution.py:539
  118.5 0.0 copy-start
  118.5 1.9 %copy.16 = bf16[1,2,256,512]{3,2,1,0:T(8,128)(2,1)} copy(bf16[1,2,256,512]{3,2,1,0:T(8,128)(2,1)} %bitcast.18) | data formatting | bytes 1048576
  120.4 0.0 copy-done
  120.5 0.8 copy.17
Async XLA Ops:
  0.6 0.7 copy-start.3
  1.3 0.7 copy-start.1
  2.7 0.8 copy-start.2
  118.5 1.9 %copy-start = (bf16[2,256,512]{2,1,0:T(8,128)(2,1)S(1)}, bf16[2,256,512]{2,1,0:T(8,128)(2,1)}, u32[]{:S(2)}) copy-start(bf16[2,256,512]{2,1,0:T(8,128)(2,1)} %get-tuple-element.5) | copy-start | bytes 1572868

commit v9 on v8

--- a/solution.py
+++ b/solution.py
@@ -376,10 +376,10 @@
     )
 
 
-def whole_kernel(parts, sections, hs_ref, x_hbm, cot_hbm, osnd_ref, orcv_ref, orcvt_ref, osndt_ref,
-                 orcvl_ref, ws_hbm, wr_hbm, wm_hbm, wn_hbm, wa_hbm, g_ref,
+def whole_kernel(parts, sections, hs_ref, cnt_ref, x_hbm, cot_hbm, esnd_ref, ercv_ref,
+                 ws_hbm, wr_hbm, wm_hbm, wn_hbm, wa_hbm, g_ref,
                  out_ref, grad_ref,
-                 xbuf, cotbuf, wbuf,
+                 xbuf, cotbuf, wbuf, osnd_ref, orcv_ref, orcvt_ref, osndt_ref, orcvl_ref,
                  hbuf, fpbuf, fnbuf, stage_n, stage_p, abuf, ubuf, cbuf, p32, hg, snbuf, spbuf,
                  fsend, frecv, bsend, brecv, lsem):
     micro, own, latent = xbuf.shape
@@ -391,6 +391,28 @@
     loads.append(pltpu.make_async_copy(cot_hbm, cotbuf, lsem.at[6]))
     for copy in loads:
         copy.start()
+    edges = osnd_ref.shape[0]
+    ext_rows = osnd_ref.shape[1]
+    own_rows = orcv_ref.shape[1]
+    es = esnd_ref[...]
+    er = ercv_ref[...]
+    snd = jnp.concatenate([es[i:i + 1] for i in range(es.shape[0])], axis=1)
+    rcv = jnp.concatenate([er[i:i + 1] for i in range(er.shape[0])], axis=1)
+    lane = lax.broadcasted_iota(jnp.int32, (1, edges), 1)
+    per_block = es.shape[1]
+    live = lane < 0
+    for i in range(es.shape[0]):
+        live = live | ((lane >= i * per_block) & (lane < i * per_block + cnt_ref[i]))
+    sndt = lax.broadcasted_iota(jnp.int32, (ext_rows, edges), 0) == snd
+    rcvt = lax.broadcasted_iota(jnp.int32, (own_rows, edges), 0) == rcv
+    osndt_f = sndt.astype(F32)
+    rcvt_f = rcvt.astype(F32)
+    rcvlt_f = (rcvt & live).astype(F32)
+    osndt_ref[...] = osndt_f.astype(BF16)
+    orcvt_ref[...] = rcvlt_f.astype(BF16)
+    osnd_ref[...] = osndt_f.T.astype(BF16)
+    orcv_ref[...] = rcvt_f.T.astype(BF16)
+    orcvl_ref[...] = rcvlt_f.T.astype(BF16)
     d = lax.axis_index("dom")
     p = lax.axis_index("pipe")
     pipe_next = (d, lax.rem(p + 1, sections))
@@ -529,13 +551,16 @@
 
 
 def whole(operands, span, parts, sections):
-    x = operands[1]
+    x = operands[2]
     micro, own, latent = x.shape
     vm = pl.BlockSpec(memory_space=pltpu.VMEM)
     anyspec = pl.BlockSpec(memory_space=pltpu.HBM)
     bf = lambda rows: pltpu.VMEM((micro, rows, latent), BF16)
     f32 = pltpu.VMEM((micro, own, latent), F32)
-    in_specs = [pl.BlockSpec(memory_space=pltpu.SMEM), anyspec, anyspec] + [vm] * 5 + [anyspec] * 5 + [vm]
+    smem = pl.BlockSpec(memory_space=pltpu.SMEM)
+    in_specs = [smem, smem, anyspec, anyspec, vm, vm] + [anyspec] * 5 + [vm]
+    edges = operands[4].size
+    ext_rows = own + 2 * span
     return pl.pallas_call(
         functools.partial(whole_kernel, parts, sections),
         out_shape=(jax.ShapeDtypeStruct((micro, own, latent), BF16),
@@ -543,6 +568,9 @@
         in_specs=in_specs,
         out_specs=(vm, vm),
         scratch_shapes=[bf(own), bf(own), pltpu.VMEM((5, latent, latent), BF16),
+                        pltpu.VMEM((edges, ext_rows), BF16), pltpu.VMEM((edges, own), BF16),
+                        pltpu.VMEM((own, edges), BF16), pltpu.VMEM((ext_rows, edges), BF16),
+                        pltpu.VMEM((edges, own), BF16),
                         bf(own), bf(span), bf(span), bf(span), bf(span), f32, f32, bf(own), f32,
                         bf(2 * span), bf(span), bf(span),
                         pltpu.SemaphoreType.DMA((3 * micro,)), pltpu.SemaphoreType.DMA((3 * micro,)),
@@ -566,17 +594,6 @@
     gain = gains[0].reshape(1, latent)
     hs = halo_send[0].reshape(-1).astype(jnp.int32)
 
-    snd = edge_send.reshape(-1)
-    rcv = edge_recv.reshape(-1)
-    live = (jnp.arange(block)[None, :] < edge_count[:, None]).reshape(-1)
-    osnd = (snd[:, None] == jnp.arange(ext_rows)[None, :]).astype(BF16)
-    orcv_b = rcv[:, None] == jnp.arange(own)[None, :]
-    orcv = orcv_b.astype(BF16)
-    orcvl_b = orcv_b & live[:, None]
-    orcvl = orcvl_b.astype(BF16)
-    orcvt = orcvl_b.T.astype(BF16)
-    osndt = osnd.T
-
     def blocks_of(x):
         shaped = x.reshape(micro, own // block, block, latent)
         nxt = jnp.take(shaped, hs[0], axis=1)
@@ -602,7 +619,8 @@
         13)
 
     out_rec, grad_rec = whole(
-        (hs, inputs, cotangent, osnd, orcv, orcvt, osndt, orcvl, *weights, gain), span, D, S)
+        (hs, edge_count.astype(jnp.int32), inputs, cotangent, edge_send.astype(jnp.int32),
+         edge_recv.astype(jnp.int32), *weights, gain), span, D, S)
     return (out_rec[None], grad_rec[None])
 
 

time: 121 us -> 117 us (0.967)
  other arithmetic: 2.56 us -> 0 us
  local copies, waits for them, and re-layouts: 3.98 us -> 2.72 us
    convert_element_type x3 -> x0, other arithmetic: 2.49 us -> none  [the longest x2 1.58 us: shards(): osnd = (snd[:, None] == jnp.arange(ext_rows)[None, :]).astype(BF16)]
    unnamed x10 -> x4, local copies, waits for them, and re-layouts: 3.98 us -> 2.72 us
where the time goes in v9:
time: 117 us
  Pallas kernels  114 us (97%)
  local copies, waits for them, and re-layouts  2.72 us (2%)
    pallas_call x1, Pallas kernels, whole(): pl.pallas_call(functools.partial(whole_kernel, parts, sections), out_shap...  114 us
    unnamed x4, local copies, waits for them, and re-layouts  2.72 us

profile of v9, /device:TPU:1, one launch (start us, length us, event | category | flops | bytes accessed | tf_op | source)
XLA Modules:
  0.0 117.2 jit_solution(17872910203523905902)
XLA Ops:
  0.6 113.8 %shard_map.131 = (bf16[2,256,512]{2,1,0:T(8,128)(2,1)}, bf16[2,256,512]{2,1,0:T(8,128)(2,1)}) custom-call(s32[2]{0:T(128)} %bitcast.15, s32[2]{0:T(128)} %cnt_ref.1, bf16[2,256,512]{2,1,0:T(8,128)(2,1)} %x_hbm.1, bf16[2,256,512]{2,1,0:T(8,128)(2,1)} %cot_hbm.1, s32[2,128]{1,0:T(2,128)} %esnd_ref.1, s32[2,128]{1,0:T(2,128)} %ercv_ref.1, ...), custom_call_target="tpu_custom_call" | custom-call | tf_op jit(solution)/shard_map/pallas_call | solution.py:564
  114.5 0.0 copy-start
  114.5 1.9 %copy.16 = bf16[1,2,256,512]{3,2,1,0:T(8,128)(2,1)} copy(bf16[1,2,256,512]{3,2,1,0:T(8,128)(2,1)} %bitcast.14) | data formatting | bytes 1048576
  116.4 0.0 copy-done
  116.4 0.8 copy.17
Async XLA Ops:
  114.5 1.9 %copy-start = (bf16[2,256,512]{2,1,0:T(8,128)(2,1)S(1)}, bf16[2,256,512]{2,1,0:T(8,128)(2,1)}, u32[]{:S(2)}) copy-start(bf16[2,256,512]{2,1,0:T(8,128)(2,1)} %get-tuple-element.5) | copy-start | bytes 1572868

commit v10 on v9

--- a/solution.py
+++ b/solution.py
@@ -439,7 +439,8 @@
     loads[0].wait()
     fwd_pipe = []
     fwd_halo = []
-    for m in range(micro):
+
+    def fwd_step(m):
         pipe_in = remote(out_ref.at[m], hbuf.at[m], (fsend, frecv), m, pipe_next)
         pl.when(has_prev)(pipe_in.wait_recv)
 
@@ -490,10 +491,19 @@
         pl.when(has_next)(pipe_in.start)
         fwd_pipe.append(pipe_in)
 
-    loads[6].wait()
-    bwd_pipe = []
-    bwd_halo = []
-    for m in range(micro):
+
+    def bwd_step(m):
+        d = lax.axis_index("dom")
+        p = lax.axis_index("pipe")
+        pipe_prev = (d, lax.rem(p - 1 + sections, sections))
+        pipe_next = (d, lax.rem(p + 1, sections))
+        dom_next = (lax.rem(d + 1, parts), p)
+        dom_prev = (lax.rem(d - 1 + parts, parts), p)
+        has_prev = p > 0
+        has_next = p < sections - 1
+        hs0 = hs_ref[0]
+        hs1 = hs_ref[1]
+        gain = g_ref[...]
         pipe_in = remote(grad_ref.at[m], cbuf.at[m], (bsend, brecv), m, pipe_prev)
         pl.when(has_next)(pipe_in.wait_recv)
 
@@ -532,7 +542,6 @@
         p32[m] = rows + split_sum(osndt[:own], send_x)
         for copy in pair:
             copy.wait_recv()
-        bwd_halo.extend(pair)
         sn = snbuf[m].astype(F32)
         sp = spbuf[m].astype(F32)
         for b in range(own // block):
@@ -540,13 +549,28 @@
             piece = piece + jnp.where(hs0 == b, sn, 0.0) + jnp.where(hs1 == b, sp, 0.0)
             grad_ref[m, b * block:(b + 1) * block] = piece.astype(grad_ref.dtype)
         pl.when(has_prev)(pipe_in.start)
-        bwd_pipe.append(pipe_in)
+
+
+    last = p == sections - 1
+    fwd_step(0)
+    loads[6].wait()
+    pl.when(last)(functools.partial(bwd_step, 0))
+    for m in range(1, micro):
+        fwd_step(m)
+    pl.when(jnp.logical_not(last))(functools.partial(bwd_step, 0))
+    for m in range(1, micro):
+        bwd_step(m)
 
     for copy in fwd_pipe:
         pl.when(has_next)(copy.wait_send)
-    for copy in bwd_pipe:
-        pl.when(has_prev)(copy.wait_send)
-    for copy in fwd_halo + bwd_halo:
+    for m in range(micro):
+        done = remote(grad_ref.at[m], cbuf.at[m], (bsend, brecv), m, pipe_prev)
+        pl.when(has_prev)(done.wait_send)
+        fwd_halo.append(remote(hg.at[m, pl.ds(0, block)], snbuf.at[m], (bsend, brecv), micro + 2 * m,
+                               dom_prev))
+        fwd_halo.append(remote(hg.at[m, pl.ds(block, block)], spbuf.at[m], (bsend, brecv),
+                               micro + 2 * m + 1, dom_next))
+    for copy in fwd_halo:
         copy.wait_send()
 
 

time: 117 us -> 117 us (level)
  no operation moved by 1% of the time
where the time goes in v10:
time: 117 us
  Pallas kernels  114 us (97%)
  local copies, waits for them, and re-layouts  2.72 us (2%)
    pallas_call x1, Pallas kernels, whole(): pl.pallas_call(functools.partial(whole_kernel, parts, sections), out_shap...  114 us
    unnamed x4, local copies, waits for them, and re-layouts  2.72 us

profile of v10, /device:TPU:1, one launch (start us, length us, event | category | flops | bytes accessed | tf_op | source)
XLA Modules:
  0.0 117.3 jit_solution(5071255088718500661)
XLA Ops:
  0.6 113.9 %shard_map.131 = (bf16[2,256,512]{2,1,0:T(8,128)(2,1)}, bf16[2,256,512]{2,1,0:T(8,128)(2,1)}) custom-call(s32[2]{0:T(128)} %bitcast.15, s32[2]{0:T(128)} %cnt_ref.1, bf16[2,256,512]{2,1,0:T(8,128)(2,1)} %x_hbm.1, bf16[2,256,512]{2,1,0:T(8,128)(2,1)} %cot_hbm.1, s32[2,128]{1,0:T(2,128)} %esnd_ref.1, s32[2,128]{1,0:T(2,128)} %ercv_ref.1, ...), custom_call_target="tpu_custom_call" | custom-call | tf_op jit(solution)/shard_map/pallas_call | solution.py:588
  114.5 0.0 copy-start
  114.5 1.9 %copy.16 = bf16[1,2,256,512]{3,2,1,0:T(8,128)(2,1)} copy(bf16[1,2,256,512]{3,2,1,0:T(8,128)(2,1)} %bitcast.14) | data formatting | bytes 1048576
  116.5 0.0 copy-done
  116.5 0.8 copy.17
Async XLA Ops:
  114.5 1.9 %copy-start = (bf16[2,256,512]{2,1,0:T(8,128)(2,1)S(1)}, bf16[2,256,512]{2,1,0:T(8,128)(2,1)}, u32[]{:S(2)}) copy-start(bf16[2,256,512]{2,1,0:T(8,128)(2,1)} %get-tuple-element.5) | copy-start | bytes 1572868

commit v11 on v9

--- a/solution.py
+++ b/solution.py
@@ -440,8 +440,11 @@
     fwd_pipe = []
     fwd_halo = []
     for m in range(micro):
-        pipe_in = remote(out_ref.at[m], hbuf.at[m], (fsend, frecv), m, pipe_next)
-        pl.when(has_prev)(pipe_in.wait_recv)
+        half = own // 2
+        pipe_in = [remote(out_ref.at[m, pl.ds(k * half, half)], hbuf.at[m, pl.ds(k * half, half)],
+                          (fsend, frecv), 6 * micro + 2 * m + k, pipe_next) for k in range(2)]
+        for piece_copy in pipe_in:
+            pl.when(has_prev)(piece_copy.wait_recv)
 
         @pl.when(p == 0)
         def _():
@@ -487,15 +490,19 @@
         var = jnp.mean(cen * cen, axis=-1, keepdims=True)
         unit = cen * lax.rsqrt(var + EPSILON)
         out_ref[m] = (h.astype(F32) + unit * gain).astype(BF16)
-        pl.when(has_next)(pipe_in.start)
-        fwd_pipe.append(pipe_in)
+        for piece_copy in pipe_in:
+            pl.when(has_next)(piece_copy.start)
+        fwd_pipe.extend(pipe_in)
 
     loads[6].wait()
     bwd_pipe = []
     bwd_halo = []
     for m in range(micro):
-        pipe_in = remote(grad_ref.at[m], cbuf.at[m], (bsend, brecv), m, pipe_prev)
-        pl.when(has_next)(pipe_in.wait_recv)
+        half = own // 2
+        pipe_in = [remote(grad_ref.at[m, pl.ds(k * half, half)], cbuf.at[m, pl.ds(k * half, half)],
+                          (bsend, brecv), 6 * micro + 2 * m + k, pipe_prev) for k in range(2)]
+        for piece_copy in pipe_in:
+            pl.when(has_next)(piece_copy.wait_recv)
 
         @pl.when(p == sections - 1)
         def _():
@@ -539,8 +546,9 @@
             piece = p32[m, b * block:(b + 1) * block]
             piece = piece + jnp.where(hs0 == b, sn, 0.0) + jnp.where(hs1 == b, sp, 0.0)
             grad_ref[m, b * block:(b + 1) * block] = piece.astype(grad_ref.dtype)
-        pl.when(has_prev)(pipe_in.start)
-        bwd_pipe.append(pipe_in)
+        for piece_copy in pipe_in:
+            pl.when(has_prev)(piece_copy.start)
+        bwd_pipe.extend(pipe_in)
 
     for copy in fwd_pipe:
         pl.when(has_next)(copy.wait_send)
@@ -573,8 +581,8 @@
                         pltpu.VMEM((edges, own), BF16),
                         bf(own), bf(span), bf(span), bf(span), bf(span), f32, f32, bf(own), f32,
                         bf(2 * span), bf(span), bf(span),
-                        pltpu.SemaphoreType.DMA((3 * micro,)), pltpu.SemaphoreType.DMA((3 * micro,)),
-                        pltpu.SemaphoreType.DMA((3 * micro,)), pltpu.SemaphoreType.DMA((3 * micro,)),
+                        pltpu.SemaphoreType.DMA((8 * micro,)), pltpu.SemaphoreType.DMA((8 * micro,)),
+                        pltpu.SemaphoreType.DMA((8 * micro,)), pltpu.SemaphoreType.DMA((8 * micro,)),
                         pltpu.SemaphoreType.DMA((7,))],
         compiler_params=pltpu.CompilerParams(collective_id=0, has_side_effects=True,
                                              vmem_limit_bytes=67043328),

time: 117 us -> 118 us (level)
  no operation moved by 1% of the time
where the time goes in v11:
time: 118 us
  Pallas kernels  114 us (97%)
  local copies, waits for them, and re-layouts  2.72 us (2%)
    pallas_call x1, Pallas kernels, whole(): pl.pallas_call(functools.partial(whole_kernel, parts, sections), out_shap...  114 us
    unnamed x4, local copies, waits for them, and re-layouts  2.72 us

profile of v11, /device:TPU:1, one launch (start us, length us, event | category | flops | bytes accessed | tf_op | source)
XLA Modules:
  0.0 117.6 jit_solution(12102851706411950165)
XLA Ops:
  0.6 114.3 %shard_map.131 = (bf16[2,256,512]{2,1,0:T(8,128)(2,1)}, bf16[2,256,512]{2,1,0:T(8,128)(2,1)}) custom-call(s32[2]{0:T(128)} %bitcast.15, s32[2]{0:T(128)} %cnt_ref.1, bf16[2,256,512]{2,1,0:T(8,128)(2,1)} %x_hbm.1, bf16[2,256,512]{2,1,0:T(8,128)(2,1)} %cot_hbm.1, s32[2,128]{1,0:T(2,128)} %esnd_ref.1, s32[2,128]{1,0:T(2,128)} %ercv_ref.1, ...), custom_call_target="tpu_custom_call" | custom-call | tf_op jit(solution)/shard_map/pallas_call | solution.py:572
  114.9 0.0 copy-start
  114.9 1.9 %copy.16 = bf16[1,2,256,512]{3,2,1,0:T(8,128)(2,1)} copy(bf16[1,2,256,512]{3,2,1,0:T(8,128)(2,1)} %bitcast.14) | data formatting | bytes 1048576
  116.8 0.0 copy-done
  116.8 0.8 copy.17
Async XLA Ops:
  114.9 1.9 %copy-start = (bf16[2,256,512]{2,1,0:T(8,128)(2,1)S(1)}, bf16[2,256,512]{2,1,0:T(8,128)(2,1)}, u32[]{:S(2)}) copy-start(bf16[2,256,512]{2,1,0:T(8,128)(2,1)} %get-tuple-element.5) | copy-start | bytes 1572868

commit v12 on v9

--- a/solution.py
+++ b/solution.py
@@ -487,6 +487,8 @@
         var = jnp.mean(cen * cen, axis=-1, keepdims=True)
         unit = cen * lax.rsqrt(var + EPSILON)
         out_ref[m] = (h.astype(F32) + unit * gain).astype(BF16)
+        if fwd_pipe:
+            pl.when(has_next)(fwd_pipe[-1].wait_send)
         pl.when(has_next)(pipe_in.start)
         fwd_pipe.append(pipe_in)
 
@@ -539,13 +541,13 @@
             piece = p32[m, b * block:(b + 1) * block]
             piece = piece + jnp.where(hs0 == b, sn, 0.0) + jnp.where(hs1 == b, sp, 0.0)
             grad_ref[m, b * block:(b + 1) * block] = piece.astype(grad_ref.dtype)
+        if bwd_pipe:
+            pl.when(has_prev)(bwd_pipe[-1].wait_send)
         pl.when(has_prev)(pipe_in.start)
         bwd_pipe.append(pipe_in)
 
-    for copy in fwd_pipe:
-        pl.when(has_next)(copy.wait_send)
-    for copy in bwd_pipe:
-        pl.when(has_prev)(copy.wait_send)
+    pl.when(has_next)(fwd_pipe[-1].wait_send)
+    pl.when(has_prev)(bwd_pipe[-1].wait_send)
     for copy in fwd_halo + bwd_halo:
         copy.wait_send()
 

time: 117 us -> 117 us (level)
  no operation moved by 1% of the time
where the time goes in v12:
time: 117 us
  Pallas kernels  113 us (97%)
  local copies, waits for them, and re-layouts  2.72 us (2%)
    pallas_call x1, Pallas kernels, whole(): pl.pallas_call(functools.partial(whole_kernel, parts, sections), out_shap...  113 us
    unnamed x4, local copies, waits for them, and re-layouts  2.72 us

profile of v12, /device:TPU:1, one launch (start us, length us, event | category | flops | bytes accessed | tf_op | source)
XLA Modules:
  0.0 116.7 jit_solution(6588452213414761951)
XLA Ops:
  0.6 113.3 %shard_map.131 = (bf16[2,256,512]{2,1,0:T(8,128)(2,1)}, bf16[2,256,512]{2,1,0:T(8,128)(2,1)}) custom-call(s32[2]{0:T(128)} %bitcast.15, s32[2]{0:T(128)} %cnt_ref.1, bf16[2,256,512]{2,1,0:T(8,128)(2,1)} %x_hbm.1, bf16[2,256,512]{2,1,0:T(8,128)(2,1)} %cot_hbm.1, s32[2,128]{1,0:T(2,128)} %esnd_ref.1, s32[2,128]{1,0:T(2,128)} %ercv_ref.1, ...), custom_call_target="tpu_custom_call" | custom-call | tf_op jit(solution)/shard_map/pallas_call | solution.py:566
  113.9 0.0 copy-start
  113.9 1.9 %copy.16 = bf16[1,2,256,512]{3,2,1,0:T(8,128)(2,1)} copy(bf16[1,2,256,512]{3,2,1,0:T(8,128)(2,1)} %bitcast.14) | data formatting | bytes 1048576
  115.9 0.0 copy-done
  115.9 0.8 copy.17
Async XLA Ops:
  113.9 1.9 %copy-start = (bf16[2,256,512]{2,1,0:T(8,128)(2,1)S(1)}, bf16[2,256,512]{2,1,0:T(8,128)(2,1)}, u32[]{:S(2)}) copy-start(bf16[2,256,512]{2,1,0:T(8,128)(2,1)} %get-tuple-element.5) | copy-start | bytes 1572868

commit v13 on v9

--- a/solution.py
+++ b/solution.py
@@ -381,6 +381,7 @@
                  out_ref, grad_ref,
                  xbuf, cotbuf, wbuf, osnd_ref, orcv_ref, orcvt_ref, osndt_ref, orcvl_ref,
                  hbuf, fpbuf, fnbuf, stage_n, stage_p, abuf, ubuf, cbuf, p32, hg, snbuf, spbuf,
+                 unitbuf, rsbuf,
                  fsend, frecv, bsend, brecv, lsem):
     micro, own, latent = xbuf.shape
     block = fpbuf.shape[1]
@@ -475,34 +476,11 @@
                     + mm(osnd[:, own + span:], fnbuf[m])).astype(BF16)
         send_part = mm(gathered, ws[...]).astype(BF16).astype(F32)
         pre = send_part + recv_part
-        abuf[m] = pre
-        edge_hidden = (pre * sigmoid(pre)).astype(BF16)
+        sig_a = sigmoid(pre)
+        edge_hidden = (pre * sig_a).astype(BF16)
         messages = mm(edge_hidden, wm[...])
         agg = split_sum(orcvt_ref[...], messages).astype(BF16)
         node_pre = node_part + mm(agg, wa[...])
-        ubuf[m] = node_pre
-        act = node_pre * sigmoid(node_pre)
-        mean = jnp.mean(act, axis=-1, keepdims=True)
-        cen = act - mean
-        var = jnp.mean(cen * cen, axis=-1, keepdims=True)
-        unit = cen * lax.rsqrt(var + EPSILON)
-        out_ref[m] = (h.astype(F32) + unit * gain).astype(BF16)
-        pl.when(has_next)(pipe_in.start)
-        fwd_pipe.append(pipe_in)
-
-    loads[6].wait()
-    bwd_pipe = []
-    bwd_halo = []
-    for m in range(micro):
-        pipe_in = remote(grad_ref.at[m], cbuf.at[m], (bsend, brecv), m, pipe_prev)
-        pl.when(has_next)(pipe_in.wait_recv)
-
-        @pl.when(p == sections - 1)
-        def _():
-            cbuf[m] = cotbuf[m]
-
-        c = cbuf[m].astype(F32)
-        node_pre = ubuf[m]
         sig_u = sigmoid(node_pre)
         act = node_pre * sig_u
         mean = jnp.mean(act, axis=-1, keepdims=True)
@@ -510,15 +488,35 @@
         var = jnp.mean(cen * cen, axis=-1, keepdims=True)
         rs = lax.rsqrt(var + EPSILON)
         unit = cen * rs
+        out_ref[m] = (h.astype(F32) + unit * gain).astype(BF16)
+        pl.when(has_next)(pipe_in.start)
+        fwd_pipe.append(pipe_in)
+        unitbuf[m] = unit
+        rsbuf[m] = jnp.broadcast_to(rs, rsbuf.shape[1:])
+        ubuf[m] = sig_u * (1.0 + node_pre * (1.0 - sig_u))
+        abuf[m] = sig_a * (1.0 + pre * (1.0 - sig_a))
+
+    loads[6].wait()
+    bwd_pipe = []
+    bwd_halo = []
+    for m in range(micro):
+        pipe_in = remote(grad_ref.at[m], cbuf.at[m], (bsend, brecv), m, pipe_prev)
+        pl.when(has_next)(pipe_in.wait_recv)
+
+        @pl.when(p == sections - 1)
+        def _():
+            cbuf[m] = cotbuf[m]
+
+        c = cbuf[m].astype(F32)
+        unit = unitbuf[m]
+        rs = rsbuf[m][:, 0:1]
         gu = c * gain
         gact = rs * (gu - jnp.mean(gu, axis=-1, keepdims=True)
                      - unit * jnp.mean(gu * unit, axis=-1, keepdims=True))
-        du = (gact * (sig_u * (1.0 + node_pre * (1.0 - sig_u)))).astype(BF16)
+        du = (gact * ubuf[m]).astype(BF16)
         dagg = mm_t(du, wa[...]).astype(BF16)
         gmsg = mm(orcvl_ref[...], dagg).astype(BF16)
-        pre = abuf[m]
-        sig_a = sigmoid(pre)
-        dedge = (mm_t(gmsg, wm[...]) * (sig_a * (1.0 + pre * (1.0 - sig_a)))).astype(BF16)
+        dedge = (mm_t(gmsg, wm[...]) * abuf[m]).astype(BF16)
         send_x = mm_t(dedge, ws[...])
         osndt = osndt_ref[...]
         hg[m] = split_sum(osndt[own:], send_x).astype(BF16)
@@ -572,7 +570,7 @@
                         pltpu.VMEM((own, edges), BF16), pltpu.VMEM((ext_rows, edges), BF16),
                         pltpu.VMEM((edges, own), BF16),
                         bf(own), bf(span), bf(span), bf(span), bf(span), f32, f32, bf(own), f32,
-                        bf(2 * span), bf(span), bf(span),
+                        bf(2 * span), bf(span), bf(span), f32, pltpu.VMEM((micro, own, 128), F32),
                         pltpu.SemaphoreType.DMA((3 * micro,)), pltpu.SemaphoreType.DMA((3 * micro,)),
                         pltpu.SemaphoreType.DMA((3 * micro,)), pltpu.SemaphoreType.DMA((3 * micro,)),
                         pltpu.SemaphoreType.DMA((7,))],

time: 117 us -> 117 us (level)
  no operation moved by 1% of the time
where the time goes in v13:
time: 117 us; the launch traced here: 116 us
  Pallas kernels  113 us (97%)
  local copies, waits for them, and re-layouts  2.72 us (2%)
    pallas_call x1, Pallas kernels, whole(): pl.pallas_call(functools.partial(whole_kernel, parts, sections), out_shap...  113 us
    unnamed x4, local copies, waits for them, and re-layouts  2.72 us

profile of v13, /device:TPU:1, one launch (start us, length us, event | category | flops | bytes accessed | tf_op | source)
XLA Modules:
  0.0 116.4 jit_solution(3941443980143816574)
XLA Ops:
  0.6 113.1 %shard_map.131 = (bf16[2,256,512]{2,1,0:T(8,128)(2,1)}, bf16[2,256,512]{2,1,0:T(8,128)(2,1)}) custom-call(s32[2]{0:T(128)} %bitcast.15, s32[2]{0:T(128)} %cnt_ref.1, bf16[2,256,512]{2,1,0:T(8,128)(2,1)} %x_hbm.1, bf16[2,256,512]{2,1,0:T(8,128)(2,1)} %cot_hbm.1, s32[2,128]{1,0:T(2,128)} %esnd_ref.1, s32[2,128]{1,0:T(2,128)} %ercv_ref.1, ...), custom_call_target="tpu_custom_call" | custom-call | tf_op jit(solution)/shard_map/pallas_call | solution.py:562
  113.7 0.0 copy-start
  113.7 1.9 %copy.16 = bf16[1,2,256,512]{3,2,1,0:T(8,128)(2,1)} copy(bf16[1,2,256,512]{3,2,1,0:T(8,128)(2,1)} %bitcast.14) | data formatting | bytes 1048576
  115.6 0.0 copy-done
  115.6 0.8 copy.17
Async XLA Ops:
  113.7 1.9 %copy-start = (bf16[2,256,512]{2,1,0:T(8,128)(2,1)S(1)}, bf16[2,256,512]{2,1,0:T(8,128)(2,1)}, u32[]{:S(2)}) copy-start(bf16[2,256,512]{2,1,0:T(8,128)(2,1)} %get-tuple-element.5) | copy-start | bytes 1572868

commit v14 on v13

--- a/solution.py
+++ b/solution.py
@@ -21,7 +21,7 @@
 
 
 def sigmoid(v):
-    return 1.0 / (1.0 + jnp.exp(-v))
+    return 0.5 * (1.0 + jnp.tanh(0.5 * v))
 
 
 def split_sum(onehot, values):

time: 117 us -> 116 us (level)
  no operation moved by 1% of the time
where the time goes in v14:
time: 116 us
  Pallas kernels  113 us (97%)
  local copies, waits for them, and re-layouts  2.72 us (2%)
    pallas_call x1, Pallas kernels, whole(): pl.pallas_call(functools.partial(whole_kernel, parts, sections), out_shap...  113 us
    unnamed x4, local copies, waits for them, and re-layouts  2.72 us

profile of v14, /device:TPU:1, one launch (start us, length us, event | category | flops | bytes accessed | tf_op | source)
XLA Modules:
  0.0 116.0 jit_solution(4556526328088456828)
XLA Ops:
  0.6 112.7 %shard_map.131 = (bf16[2,256,512]{2,1,0:T(8,128)(2,1)}, bf16[2,256,512]{2,1,0:T(8,128)(2,1)}) custom-call(s32[2]{0:T(128)} %bitcast.15, s32[2]{0:T(128)} %cnt_ref.1, bf16[2,256,512]{2,1,0:T(8,128)(2,1)} %x_hbm.1, bf16[2,256,512]{2,1,0:T(8,128)(2,1)} %cot_hbm.1, s32[2,128]{1,0:T(2,128)} %esnd_ref.1, s32[2,128]{1,0:T(2,128)} %ercv_ref.1, ...), custom_call_target="tpu_custom_call" | custom-call | tf_op jit(solution)/shard_map/pallas_call | solution.py:562
  113.3 0.0 copy-start
  113.3 1.9 %copy.16 = bf16[1,2,256,512]{3,2,1,0:T(8,128)(2,1)} copy(bf16[1,2,256,512]{3,2,1,0:T(8,128)(2,1)} %bitcast.14) | data formatting | bytes 1048576
  115.2 0.0 copy-done
  115.2 0.8 copy.17
Async XLA Ops:
  113.3 1.9 %copy-start = (bf16[2,256,512]{2,1,0:T(8,128)(2,1)S(1)}, bf16[2,256,512]{2,1,0:T(8,128)(2,1)}, u32[]{:S(2)}) copy-start(bf16[2,256,512]{2,1,0:T(8,128)(2,1)} %get-tuple-element.5) | copy-start | bytes 1572868

commit v15 on v13

--- a/solution.py
+++ b/solution.py
@@ -392,28 +392,6 @@
     loads.append(pltpu.make_async_copy(cot_hbm, cotbuf, lsem.at[6]))
     for copy in loads:
         copy.start()
-    edges = osnd_ref.shape[0]
-    ext_rows = osnd_ref.shape[1]
-    own_rows = orcv_ref.shape[1]
-    es = esnd_ref[...]
-    er = ercv_ref[...]
-    snd = jnp.concatenate([es[i:i + 1] for i in range(es.shape[0])], axis=1)
-    rcv = jnp.concatenate([er[i:i + 1] for i in range(er.shape[0])], axis=1)
-    lane = lax.broadcasted_iota(jnp.int32, (1, edges), 1)
-    per_block = es.shape[1]
-    live = lane < 0
-    for i in range(es.shape[0]):
-        live = live | ((lane >= i * per_block) & (lane < i * per_block + cnt_ref[i]))
-    sndt = lax.broadcasted_iota(jnp.int32, (ext_rows, edges), 0) == snd
-    rcvt = lax.broadcasted_iota(jnp.int32, (own_rows, edges), 0) == rcv
-    osndt_f = sndt.astype(F32)
-    rcvt_f = rcvt.astype(F32)
-    rcvlt_f = (rcvt & live).astype(F32)
-    osndt_ref[...] = osndt_f.astype(BF16)
-    orcvt_ref[...] = rcvlt_f.astype(BF16)
-    osnd_ref[...] = osndt_f.T.astype(BF16)
-    orcv_ref[...] = rcvt_f.T.astype(BF16)
-    orcvl_ref[...] = rcvlt_f.T.astype(BF16)
     d = lax.axis_index("dom")
     p = lax.axis_index("pipe")
     pipe_next = (d, lax.rem(p + 1, sections))
@@ -437,6 +415,30 @@
             src_ref=src, dst_ref=dst, send_sem=send_sem.at[idx], recv_sem=recv_sem.at[idx],
             device_id=target, device_id_type=MESH_ID)
 
+    def build_onehots():
+        edges = osnd_ref.shape[0]
+        ext_rows = osnd_ref.shape[1]
+        own_rows = orcv_ref.shape[1]
+        es = esnd_ref[...]
+        er = ercv_ref[...]
+        snd = jnp.concatenate([es[i:i + 1] for i in range(es.shape[0])], axis=1)
+        rcv = jnp.concatenate([er[i:i + 1] for i in range(er.shape[0])], axis=1)
+        lane = lax.broadcasted_iota(jnp.int32, (1, edges), 1)
+        per_block = es.shape[1]
+        live = lane < 0
+        for i in range(es.shape[0]):
+            live = live | ((lane >= i * per_block) & (lane < i * per_block + cnt_ref[i]))
+        sndt = lax.broadcasted_iota(jnp.int32, (ext_rows, edges), 0) == snd
+        rcvt = lax.broadcasted_iota(jnp.int32, (own_rows, edges), 0) == rcv
+        osndt_f = sndt.astype(F32)
+        rcvt_f = rcvt.astype(F32)
+        rcvlt_f = (rcvt & live).astype(F32)
+        osndt_ref[...] = osndt_f.astype(BF16)
+        orcvt_ref[...] = rcvlt_f.astype(BF16)
+        osnd_ref[...] = osndt_f.T.astype(BF16)
+        orcv_ref[...] = rcvt_f.T.astype(BF16)
+        orcvl_ref[...] = rcvlt_f.T.astype(BF16)
+
     loads[0].wait()
     fwd_pipe = []
     fwd_halo = []
@@ -462,6 +464,7 @@
         for copy in pair:
             copy.start()
         if m == 0:
+            build_onehots()
             for copy in loads[1:6]:
                 copy.wait()
         osnd = osnd_ref[...]

time: 117 us -> 116 us (level)
  no operation moved by 1% of the time
where the time goes in v15:
time: 116 us
  Pallas kernels  113 us (97%)
  local copies, waits for them, and re-layouts  2.72 us (2%)
    pallas_call x1, Pallas kernels, whole(): pl.pallas_call(functools.partial(whole_kernel, parts, sections), out_shap...  113 us
    unnamed x4, local copies, waits for them, and re-layouts  2.72 us

profile of v15, /device:TPU:1, one launch (start us, length us, event | category | flops | bytes accessed | tf_op | source)
XLA Modules:
  0.0 116.3 jit_solution(2948093642503849697)
XLA Ops:
  0.6 112.9 %shard_map.131 = (bf16[2,256,512]{2,1,0:T(8,128)(2,1)}, bf16[2,256,512]{2,1,0:T(8,128)(2,1)}) custom-call(s32[2]{0:T(128)} %bitcast.15, s32[2]{0:T(128)} %cnt_ref.1, bf16[2,256,512]{2,1,0:T(8,128)(2,1)} %x_hbm.1, bf16[2,256,512]{2,1,0:T(8,128)(2,1)} %cot_hbm.1, s32[2,128]{1,0:T(2,128)} %esnd_ref.1, s32[2,128]{1,0:T(2,128)} %ercv_ref.1, ...), custom_call_target="tpu_custom_call" | custom-call | tf_op jit(solution)/shard_map/pallas_call | solution.py:565
  113.5 0.0 copy-start
  113.5 1.9 %copy.16 = bf16[1,2,256,512]{3,2,1,0:T(8,128)(2,1)} copy(bf16[1,2,256,512]{3,2,1,0:T(8,128)(2,1)} %bitcast.14) | data formatting | bytes 1048576
  115.5 0.0 copy-done
  115.5 0.8 copy.17
Async XLA Ops:
  113.5 1.9 %copy-start = (bf16[2,256,512]{2,1,0:T(8,128)(2,1)S(1)}, bf16[2,256,512]{2,1,0:T(8,128)(2,1)}, u32[]{:S(2)}) copy-start(bf16[2,256,512]{2,1,0:T(8,128)(2,1)} %get-tuple-element.5) | copy-start | bytes 1572868

commit v16 on v13

--- a/solution.py
+++ b/solution.py
@@ -479,7 +479,7 @@
         sig_a = sigmoid(pre)
         edge_hidden = (pre * sig_a).astype(BF16)
         messages = mm(edge_hidden, wm[...])
-        agg = split_sum(orcvt_ref[...], messages).astype(BF16)
+        agg = mm(orcvt_ref[...], messages.astype(BF16)).astype(BF16)
         node_pre = node_part + mm(agg, wa[...])
         sig_u = sigmoid(node_pre)
         act = node_pre * sig_u
@@ -519,7 +519,7 @@
         dedge = (mm_t(gmsg, wm[...]) * abuf[m]).astype(BF16)
         send_x = mm_t(dedge, ws[...])
         osndt = osndt_ref[...]
-        hg[m] = split_sum(osndt[own:], send_x).astype(BF16)
+        hg[m] = mm(osndt[own:], send_x.astype(BF16)).astype(BF16)
         pair = [remote(hg.at[m, pl.ds(0, block)], snbuf.at[m], (bsend, brecv), micro + 2 * m, dom_prev),
                 remote(hg.at[m, pl.ds(block, block)], spbuf.at[m], (bsend, brecv), micro + 2 * m + 1,
                        dom_next)]

time: 117 us -> 116 us (level)
  no operation moved by 1% of the time
where the time goes in v16:
time: 116 us
  Pallas kernels  112 us (97%)
  local copies, waits for them, and re-layouts  2.72 us (2%)
    pallas_call x1, Pallas kernels, whole(): pl.pallas_call(functools.partial(whole_kernel, parts, sections), out_shap...  112 us
    unnamed x4, local copies, waits for them, and re-layouts  2.72 us

profile of v16, /device:TPU:1, one launch (start us, length us, event | category | flops | bytes accessed | tf_op | source)
XLA Modules:
  0.0 115.5 jit_solution(502286774824031367)
XLA Ops:
  0.6 112.1 %shard_map.131 = (bf16[2,256,512]{2,1,0:T(8,128)(2,1)}, bf16[2,256,512]{2,1,0:T(8,128)(2,1)}) custom-call(s32[2]{0:T(128)} %bitcast.15, s32[2]{0:T(128)} %cnt_ref.1, bf16[2,256,512]{2,1,0:T(8,128)(2,1)} %x_hbm.1, bf16[2,256,512]{2,1,0:T(8,128)(2,1)} %cot_hbm.1, s32[2,128]{1,0:T(2,128)} %esnd_ref.1, s32[2,128]{1,0:T(2,128)} %ercv_ref.1, ...), custom_call_target="tpu_custom_call" | custom-call | tf_op jit(solution)/shard_map/pallas_call | solution.py:562
  112.8 0.0 copy-start
  112.8 1.9 %copy.16 = bf16[1,2,256,512]{3,2,1,0:T(8,128)(2,1)} copy(bf16[1,2,256,512]{3,2,1,0:T(8,128)(2,1)} %bitcast.14) | data formatting | bytes 1048576
  114.7 0.0 copy-done
  114.7 0.8 copy.17
Async XLA Ops:
  112.8 1.9 %copy-start = (bf16[2,256,512]{2,1,0:T(8,128)(2,1)S(1)}, bf16[2,256,512]{2,1,0:T(8,128)(2,1)}, u32[]{:S(2)}) copy-start(bf16[2,256,512]{2,1,0:T(8,128)(2,1)} %get-tuple-element.5) | copy-start | bytes 1572868

commit v17 on v16

--- a/solution.py
+++ b/solution.py
@@ -21,7 +21,7 @@
 
 
 def sigmoid(v):
-    return 1.0 / (1.0 + jnp.exp(-v))
+    return 0.5 * (1.0 + jnp.tanh(0.5 * v))
 
 
 def split_sum(onehot, values):

time: 116 us -> 116 us (level)
  no operation moved by 1% of the time
where the time goes in v17:
time: 116 us; the launch traced here: 115 us
  Pallas kernels  112 us (97%)
  local copies, waits for them, and re-layouts  2.72 us (2%)
    pallas_call x1, Pallas kernels, whole(): pl.pallas_call(functools.partial(whole_kernel, parts, sections), out_shap...  112 us
    unnamed x4, local copies, waits for them, and re-layouts  2.72 us

profile of v17, /device:TPU:1, one launch (start us, length us, event | category | flops | bytes accessed | tf_op | source)
XLA Modules:
  0.0 115.5 jit_solution(18142615522650686831)
XLA Ops:
  0.6 112.1 %shard_map.131 = (bf16[2,256,512]{2,1,0:T(8,128)(2,1)}, bf16[2,256,512]{2,1,0:T(8,128)(2,1)}) custom-call(s32[2]{0:T(128)} %bitcast.15, s32[2]{0:T(128)} %cnt_ref.1, bf16[2,256,512]{2,1,0:T(8,128)(2,1)} %x_hbm.1, bf16[2,256,512]{2,1,0:T(8,128)(2,1)} %cot_hbm.1, s32[2,128]{1,0:T(2,128)} %esnd_ref.1, s32[2,128]{1,0:T(2,128)} %ercv_ref.1, ...), custom_call_target="tpu_custom_call" | custom-call | tf_op jit(solution)/shard_map/pallas_call | solution.py:562
  112.7 0.0 copy-start
  112.7 1.9 %copy.16 = bf16[1,2,256,512]{3,2,1,0:T(8,128)(2,1)} copy(bf16[1,2,256,512]{3,2,1,0:T(8,128)(2,1)} %bitcast.14) | data formatting | bytes 1048576
  114.7 0.0 copy-done
  114.7 0.8 copy.17
Async XLA Ops:
  112.7 1.9 %copy-start = (bf16[2,256,512]{2,1,0:T(8,128)(2,1)S(1)}, bf16[2,256,512]{2,1,0:T(8,128)(2,1)}, u32[]{:S(2)}) copy-start(bf16[2,256,512]{2,1,0:T(8,128)(2,1)} %get-tuple-element.5) | copy-start | bytes 1572868
